TPU v7x, 32 devices: a whole 2x2x4 slice. The times are simulated.
32 devices in a mesh: sect: 4 (over y, x), dom: 8 (over z, core).
Axes of the slice: x: 2, y: 2, z: 4, core: 2. Of those that a mesh axis runs over, the one named last changes fastest.
Arguments:
- cells: int32 [3, 4, 8, 256], P(None, 'sect', 'dom'), may hold values from 0 to 255, as said below
- fracs: float32 [3, 4, 8, 256], P(None, 'sect', 'dom'), may hold values from 0 to 1
- charges: float32 [4, 8, 256], P('sect', 'dom'), may hold values from -1 to 1
- pair_blocks: int32 [4, 8, 2, 8], P('sect', 'dom'), may hold values from 0 to 17
- influence: float32 [256, 256, 256], P('dom', 'sect'), may hold values from 1 to 100
Outputs:
- forces: float32 [3, 4, 8, 256], P(None, 'sect', 'dom')
Inputs may be any that keep to these rules, and one draw needn't show every extreme that they name: On device (s, d), cells[0] lies in [s * 64, (s + 1) * 64) and cells[2] in [d * 32, (d + 1) * 32). With owner = cells[1] // 32, each device's atoms come in order of ascending owner, no owner has more than 64 atoms of one device, and for each index of sect one owner has exactly 64 atoms of every device of that index.
All inputs are finite; a program needn't handle non-finite values.
Results may differ from a plain program's by a relative error of at most 0.0003.
Values sent between devices are 32-bit elements; how exact they have to be, the bound alone decides.
No kernel may reach another device: no remote copies, remote signals or barrier semaphores. Data moves between devices by JAX's collectives and lax.ppermute only.
A program may use at most 128 MiB of HBM per device.

v0:
```python
import math

import jax
import jax.numpy as jnp
from jax import lax
from jax.sharding import PartitionSpec as P

BLOCK = 128


ewald_beta = 0.1
soft_square = 9.0
highest = lax.Precision.HIGHEST


def with_halo(block, sides, width):
    for axis, dim in sides:
        count = lax.axis_size(axis)
        forward = [(i, i + 1) for i in range(count - 1)]
        forward.append((count - 1, 0))
        backward = [(target, source) for source, target in forward]
        low = lax.ppermute(
            lax.slice_in_dim(block, block.shape[dim] - width, None, axis=dim), axis, forward
        )
        high = lax.ppermute(lax.slice_in_dim(block, 0, width, axis=dim), axis, backward)
        block = jnp.concatenate([low, block, high], axis=dim)
    return block


def spline_weights(frac):
    inner = 1.0 - frac
    square = frac * frac
    cube = square * frac
    weights = jnp.stack(
        [
            inner * inner * inner / 6.0,
            (3.0 * cube - 6.0 * square + 4.0) / 6.0,
            (-3.0 * cube + 3.0 * square + 3.0 * frac + 1.0) / 6.0,
            cube / 6.0,
        ]
    )
    slopes = jnp.stack(
        [
            -inner * inner / 2.0,
            (3.0 * square - 4.0 * frac) / 2.0,
            (-3.0 * square + 2.0 * frac + 1.0) / 2.0,
            square / 2.0,
        ]
    )
    return (weights, slopes)


def pair_kernel(centre, others, mesh_size):
    half_mesh = float(mesh_size // 2)
    displace = []
    for component in range(3):
        offset = centre[component][None, :, None] - others[component][:, None, :]
        wrapped = jnp.mod(offset + half_mesh, float(mesh_size)) - half_mesh
        displace.append(
            wrapped + (centre[component + 3][None, :, None] - others[component + 3][:, None, :])
        )
    square = (
        displace[0] * displace[0]
        + displace[1] * displace[1]
        + displace[2] * displace[2]
        + soft_square
    )
    distance = jnp.sqrt(square)
    kernel = (
        lax.erfc(ewald_beta * distance) / (square * distance)
        + 2.0
        * ewald_beta
        / math.sqrt(math.pi)
        * jnp.exp(-ewald_beta * ewald_beta * square)
        / square
    )
    coupling = centre[6][None, :, None] * others[6][:, None, :] * kernel
    return jnp.stack([jnp.sum(coupling * shift_vector, axis=(0, 2)) for shift_vector in displace])


def axis_matrix(start, coefs, extent, wrap):
    offsets = jnp.arange(4, dtype=jnp.int32)
    places = start[None, :] + offsets[:, None]
    if wrap:
        places = places % extent
    columns = jnp.arange(extent, dtype=jnp.int32)
    hits = places[:, None, :] == columns[None, :, None]
    return jnp.sum(jnp.where(hits, coefs[:, None, :], 0.0), axis=0)


def spread_dense(first, second, third, charge, weights, x_extent, y_extent, mesh_size):
    first_mat = axis_matrix(first, weights[0], x_extent, False)
    second_mat = axis_matrix(second, weights[1], y_extent, False)
    third_mat = axis_matrix(third, weights[2], mesh_size, True) * charge[None, :]
    joined = (first_mat[:, None, :] * second_mat[None, :, :]).reshape(x_extent * y_extent, -1)
    brick = contract(joined, third_mat, (1,), (1,))
    return brick.reshape(x_extent, y_extent, mesh_size)


def gradients_dense(field, first, second, third, charge, weights, slopes):
    x_extent, y_extent, mesh_size = field.shape
    flat = field.reshape(x_extent * y_extent, mesh_size)
    third_w = axis_matrix(third, weights[2], mesh_size, True)
    third_v = axis_matrix(third, slopes[2], mesh_size, True)
    along_w = contract(flat, third_w, (1,), (0,)).reshape(x_extent, y_extent, -1)
    along_v = contract(flat, third_v, (1,), (0,)).reshape(x_extent, y_extent, -1)
    first_w = axis_matrix(first, weights[0], x_extent, False)
    first_v = axis_matrix(first, slopes[0], x_extent, False)
    second_w = axis_matrix(second, weights[1], y_extent, False)
    second_v = axis_matrix(second, slopes[1], y_extent, False)
    part_one = jnp.sum(first_v[:, None, :] * second_w[None, :, :] * along_w, axis=(0, 1))
    part_two = jnp.sum(first_w[:, None, :] * second_v[None, :, :] * along_w, axis=(0, 1))
    part_three = jnp.sum(first_w[:, None, :] * second_w[None, :, :] * along_v, axis=(0, 1))
    return -charge * jnp.stack([part_one, part_two, part_three])


def phase_table(positions, mesh_size):
    freqs = jnp.arange(mesh_size, dtype=jnp.int32)
    product = positions[..., None] * freqs % mesh_size
    angle = product.astype(jnp.float32) * (2.0 * math.pi / mesh_size)
    return (jnp.cos(angle), jnp.sin(angle))


def contract(left, right, left_dims, right_dims):
    return lax.dot_general(
        left,
        right,
        ((left_dims, right_dims), ((), ())),
        precision=highest,
        preferred_element_type=jnp.float32,
    )


def complex_forward(real_in, imag_in, table, left_dims, right_dims):
    real_out = contract(real_in, table[0], left_dims, right_dims) + contract(
        imag_in, table[1], left_dims, right_dims
    )
    imag_out = contract(imag_in, table[0], left_dims, right_dims) - contract(
        real_in, table[1], left_dims, right_dims
    )
    return (real_out, imag_out)


def complex_inverse(real_in, imag_in, table, left_dims, right_dims):
    real_out = contract(real_in, table[0], left_dims, right_dims) - contract(
        imag_in, table[1], left_dims, right_dims
    )
    imag_out = contract(imag_in, table[0], left_dims, right_dims) + contract(
        real_in, table[1], left_dims, right_dims
    )
    return (real_out, imag_out)


def dom_transpose(real_part, imag_part):
    return (
        lax.all_to_all(real_part, "dom", split_axis=2, concat_axis=2, tiled=True),
        lax.all_to_all(imag_part, "dom", split_axis=2, concat_axis=2, tiled=True),
    )


def sect_transpose(real_part, imag_part):
    return (
        lax.all_to_all(real_part, "sect", split_axis=2, concat_axis=2, tiled=True),
        lax.all_to_all(imag_part, "sect", split_axis=2, concat_axis=2, tiled=True),
    )


def solve_field(grid, influence, sect_count, dom_count, y_extent):
    mesh_size = influence.shape[2]
    x_width = mesh_size // sect_count
    y_width = mesh_size // dom_count
    x_extent = x_width + 3
    rows_x = (
        jnp.arange(sect_count, dtype=jnp.int32)[:, None] * x_width
        + jnp.arange(x_extent, dtype=jnp.int32)[None, :]
    )
    rows_y = (
        jnp.arange(dom_count, dtype=jnp.int32)[:, None] * y_width
        + jnp.arange(y_extent, dtype=jnp.int32)[None, :]
    )
    plain = phase_table(jnp.arange(mesh_size, dtype=jnp.int32), mesh_size)
    table_y = phase_table(rows_y, mesh_size)
    table_x = phase_table(rows_x, mesh_size)
    flat = grid.reshape(x_extent * y_extent, mesh_size)
    real_part = contract(flat, plain[0], (1,), (0,)).reshape(x_extent, y_extent, mesh_size)
    imag_part = -contract(flat, plain[1], (1,), (0,)).reshape(x_extent, y_extent, mesh_size)
    real_part, imag_part = dom_transpose(real_part, imag_part)
    real_part = real_part.reshape(x_extent, y_extent, dom_count, y_width)
    imag_part = imag_part.reshape(x_extent, y_extent, dom_count, y_width)
    real_part, imag_part = complex_forward(real_part, imag_part, table_y, (1, 2), (1, 0))
    real_part, imag_part = sect_transpose(real_part, imag_part)
    real_part = real_part.reshape(x_extent, y_width, sect_count, x_width)
    imag_part = imag_part.reshape(x_extent, y_width, sect_count, x_width)
    real_part, imag_part = complex_forward(real_part, imag_part, table_x, (0, 2), (1, 0))
    real_part = real_part * influence
    imag_part = imag_part * influence
    back_x = tuple((entry.reshape(sect_count * x_extent, mesh_size).T for entry in table_x))
    real_part, imag_part = complex_inverse(real_part, imag_part, back_x, (2,), (0,))
    real_part, imag_part = sect_transpose(real_part, imag_part)
    real_part = real_part.reshape(y_width, x_width, sect_count, x_extent)
    imag_part = imag_part.reshape(y_width, x_width, sect_count, x_extent)
    back_y = tuple(
        (
            entry.reshape(dom_count * y_extent, mesh_size).T.reshape(
                sect_count, x_width, dom_count * y_extent
            )
            for entry in table_y
        )
    )
    real_part, imag_part = complex_inverse(real_part, imag_part, back_y, (1, 2), (1, 0))
    real_part, imag_part = dom_transpose(real_part, imag_part)
    real_part = real_part.reshape(y_width, x_extent, dom_count, y_extent)
    imag_part = imag_part.reshape(y_width, x_extent, dom_count, y_extent)
    back_z = tuple((entry.reshape(dom_count, y_width, mesh_size) for entry in plain))
    field = contract(real_part, back_z[0], (0, 2), (1, 0)) - contract(
        imag_part, back_z[1], (0, 2), (1, 0)
    )
    return field * (1.0 / float(mesh_size * mesh_size * mesh_size))


def shards(cells, fracs, charges, pair_blocks, influence):
    sect_count = lax.axis_size("sect")
    dom_count = lax.axis_size("dom")
    sect_index = lax.axis_index("sect")
    mesh_size = influence.shape[2]
    x_width = mesh_size // sect_count
    y_width = mesh_size // dom_count
    x_extent = x_width + 3
    y_extent = y_width + 3
    atom_count = charges.shape[2]
    block_count = atom_count // BLOCK
    listed_count = pair_blocks.shape[3]
    cell_x = cells[0, 0, 0]
    cell_y = cells[1, 0, 0]
    cell_z = cells[2, 0, 0]
    charge = charges[0, 0]
    packed = jnp.concatenate([cells.astype(jnp.float32), fracs, charges[None]], axis=0)
    beside_all = with_halo(packed, (("sect", 1), ("dom", 2)), 1)
    candidates = beside_all.reshape(7, 9 * block_count, BLOCK)
    listed = candidates[:, pair_blocks[0, 0].reshape(-1)].reshape(
        7, block_count, listed_count, BLOCK
    )
    own_blocks = packed.reshape(7, block_count, BLOCK)

    def per_block(pieces):
        return pair_kernel(pieces[0], pieces[1], mesh_size)

    block_forces = lax.map(per_block, (jnp.moveaxis(own_blocks, 1, 0), jnp.moveaxis(listed, 1, 0)))
    short_force = jnp.transpose(block_forces, (1, 0, 2)).reshape(3, atom_count)
    cap = 2 * atom_count // dom_count
    slot_total = dom_count * cap
    owner = cell_y // y_width
    matches = owner[None, :] == jnp.arange(dom_count, dtype=jnp.int32)[:, None]
    counts = jnp.sum(matches.astype(jnp.int32), axis=1)
    starts = jnp.cumsum(counts) - counts
    first_row = jnp.sum(jnp.where(matches, starts[:, None], 0), axis=0)
    slot_rows = owner * cap + jnp.arange(atom_count, dtype=jnp.int32) - first_row
    packed_index = (
        (cell_x - sect_index * x_width) * y_width + (cell_y - owner * y_width)
    ) * mesh_size + cell_z
    send_index = jnp.zeros((1, slot_total), jnp.int32).at[0, slot_rows].set(packed_index)
    send_data = (
        jnp.zeros((4, slot_total), jnp.float32)
        .at[:, slot_rows]
        .set(jnp.stack([fracs[0, 0, 0], fracs[1, 0, 0], fracs[2, 0, 0], charge]))
    )
    recv_index, recv_data = (
        lax.all_to_all(send_index, "dom", split_axis=1, concat_axis=1, tiled=True),
        lax.all_to_all(send_data, "dom", split_axis=1, concat_axis=1, tiled=True),
    )
    slot_third = recv_index[0] % mesh_size
    remainder = recv_index[0] // mesh_size
    slot_second = remainder % y_width
    slot_first = remainder // y_width
    slot_splines = [spline_weights(recv_data[axis_pos]) for axis_pos in range(3)]
    grid = spread_dense(
        slot_first,
        slot_second,
        slot_third,
        recv_data[3],
        (slot_splines[0][0], slot_splines[1][0], slot_splines[2][0]),
        x_extent,
        y_extent,
        mesh_size,
    )
    field = solve_field(grid, influence, sect_count, dom_count, y_extent)
    slot_force = gradients_dense(
        field,
        slot_first,
        slot_second,
        slot_third,
        recv_data[3],
        (slot_splines[0][0], slot_splines[1][0], slot_splines[2][0]),
        (slot_splines[0][1], slot_splines[1][1], slot_splines[2][1]),
    )
    returned = lax.all_to_all(slot_force, "dom", split_axis=1, concat_axis=1, tiled=True)
    mesh_force = returned[:, slot_rows]
    forces = short_force + mesh_force
    return forces.reshape(3, 1, 1, atom_count)


def solution(mesh):
    in_specs = (
        P(None, "sect", "dom", None),
        P(None, "sect", "dom", None),
        P("sect", "dom", None),
        P("sect", "dom", None, None),
        P("dom", "sect", None),
    )
    out_specs = P(None, "sect", "dom", None)
    return jax.shard_map(shards, mesh=mesh, in_specs=in_specs, out_specs=out_specs, check_vma=False)
```

profile of v0, /device:TPU:0, one launch (start us, length us, event | category | flops | bytes accessed | tf_op | source)
XLA Modules:
  0.0 751.6 jit_solution(2250921359151148806)
XLA Ops:
  3.9 6.3 all-to-all-start.1
  20.4 4.2 all-to-all-done
  29.7 5.2 copy.148
  34.9 5.7 mul.1063
  41.9 6.1 fusion.54
  48.1 4.4 fusion.113
  55.7 5.5 copy.149
  61.2 9.3 %reshape.1151 = f32[8,1,75040]{2,1,0:T(1,128)} reshape(f32[256,35,67]{2,1,0:T(8,128)} %bitcast.265) | data formatting | bytes 4802560
  70.5 4.4 all-to-all-start.2
  74.9 4.5 convolution_negate_fusion
  81.7 3.9 copy.151
  85.6 8.9 %reshape.1149 = f32[8,1,75040]{2,1,0:T(1,128)} reshape(f32[256,35,67]{2,1,0:T(8,128)} %bitcast.266) | data formatting | bytes 4802560
  94.6 35.9 %all-to-all-done.2 = f32[8,1,75040]{2,1,0:T(1,128)} async-done(((f32[8,1,75040]{2,1,0:T(1,128)}), f32[8,1,75040]{2,1,0:T(1,128)}, u32[]{:S(2)}, u32[]{:S(2)}) %all-to-all-start.2) | async-done | bytes 2401312 | tf_op jit(solution)/shard_map/all_to_all | solution.py:156
  134.2 9.5 %reduce.18 = f32[8,75040]{1,0:T(8,128)} reduce(f32[8,1,75040]{2,1,0:T(1,128)} %all-to-all-done.2, f32[]{:T(128)} %broadcast.1727), dimensions={1}, to_apply=%all_to_all.49.reduce_sub_computation | reduce | bytes 4802564 | tf_op jit(solution)/shard_map/all_to_all | solution.py:156
  143.7 7.6 %reshape.1152 = f32[256,35,67]{2,1,0:T(8,128)} reshape(f32[8,75040]{1,0:T(8,128)} %reduce.18) | data formatting | bytes 4802560
  151.3 38.4 %all-to-all-done.3 = f32[8,1,75040]{2,1,0:T(1,128)S(1)} async-done(((f32[8,1,75040]{2,1,0:T(1,128)}), f32[8,1,75040]{2,1,0:T(1,128)S(1)}, u32[]{:S(2)}, u32[]{:S(2)}) %all-to-all-start.3) | async-done | bytes 2401312 | tf_op jit(solution)/shard_map/all_to_all | solution.py:157
  189.7 8.6 %reduce.17 = f32[8,75040]{1,0:T(8,128)} reduce(f32[8,1,75040]{2,1,0:T(1,128)S(1)} %all-to-all-done.3, f32[]{:T(128)} %broadcast.1727), dimensions={1}, to_apply=%all_to_all.50.reduce_sub_computation | reduce | bytes 4802564 | tf_op jit(solution)/shard_map/all_to_all | solution.py:157
  198.3 7.7 %reshape.1150 = f32[256,35,67]{2,1,0:T(8,128)} reshape(f32[8,75040]{1,0:T(8,128)} %reduce.17) | data formatting | bytes 4802560
  206.0 8.2 %copy.152 = f32[67,35,256]{1,2,0:T(8,128)} copy(f32[67,35,256]{0,1,2:T(8,128)} %bitcast.267) | data formatting | bytes 4802560 | tf_op jit(solution)/shard_map/all_to_all | solution.py:157
  214.2 8.2 %copy.150 = f32[67,35,256]{1,2,0:T(8,128)} copy(f32[67,35,256]{0,1,2:T(8,128)} %bitcast.264) | data formatting | bytes 4802560 | tf_op jit(solution)/shard_map/all_to_all | solution.py:156
  222.4 10.2 %fusion.70 = f32[67,32,256,1]{2,1,3,0:T(8,128)S(1)} fusion(f32[67,35,8,32]{1,3,2,0:T(8,128)} %bitcast.260, s32[8,35]{1,0:T(8,128)S(1)} %iota_add_fusion.2), kind=kOutput, calls=%fused_computation.144 | convolution fusion | flops 1845186560 | bytes 4597856 | tf_op jit(solution)/shard_map/dot_general | solution.py:125
  232.6 7.9 %bitcast_subtract_fusion.2 = f32[67,32,256]{2,1,0:T(8,128)S(1)} fusion(f32[67,32,256,1]{2,1,3,0:T(8,128)S(1)} %fusion.70, f32[67,35,8,32]{1,3,2,0:T(8,128)S(1)} %bitcast.263, s32[8,35]{1,0:T(8,128)S(1)} %iota_add_fusion.2), kind=kOutput, calls=%fused_computation.91 | convolution fusion | flops 1845735424 | bytes 6793312 | tf_op jit(solution)/shard_map/dot_general | solution.py:125
  244.3 4.9 all-to-all-start.5
  249.2 9.8 %fusion.72 = f32[67,32,256,1]{2,1,3,0:T(8,128)S(1)} fusion(f32[67,35,8,32]{1,3,2,0:T(8,128)} %bitcast.262, s32[8,35]{1,0:T(8,128)S(1)} %iota_add_fusion.2), kind=kOutput, calls=%fused_computation.146 | convolution fusion | flops 1845186560 | bytes 4597856 | tf_op jit(solution)/shard_map/dot_general | solution.py:125
  259.0 9.8 %bitcast_add_fusion.1 = f32[67,32,256]{2,1,0:T(8,128)S(1)} fusion(f32[67,32,256,1]{2,1,3,0:T(8,128)S(1)} %fusion.72, f32[67,35,8,32]{1,3,2,0:T(8,128)} %bitcast.261, s32[8,35]{1,0:T(8,128)S(1)} %iota_add_fusion.2), kind=kOutput, calls=%fused_computation.92 | convolution fusion | flops 1845735424 | bytes 6793312 | tf_op jit(solution)/shard_map/dot_general | solution.py:125
  272.5 24.1 %all-to-all-done.5 = f32[67,32,256]{0,1,2:T(8,128)} async-done(((f32[67,32,256]{0,1,2:T(8,128)}), f32[67,32,256]{0,1,2:T(8,128)}, u32[]{:S(2)}, u32[]{:S(2)}) %all-to-all-start.5) | async-done | bytes 2195488 | tf_op jit(solution)/shard_map/all_to_all | solution.py:164
  296.6 5.3 all-to-all-start.4
  302.1 10.7 %fusion.36 = f32[32,64,256,1]{2,1,3,0:T(8,128)} fusion(f32[67,32,4,64]{0,1,3,2:T(8,128)} %bitcast.61, s32[4,67]{1,0:T(4,128)S(1)} %iota_add_fusion.3), kind=kOutput, calls=%fused_computation.78 | convolution fusion | flops 1687070720 | bytes 4293680 | tf_op jit(solution)/shard_map/dot_general | solution.py:125
  312.9 9.6 %fusion.38 = f32[32,64,256,1]{2,1,3,0:T(8,128)S(1)} fusion(f32[67,32,4,64]{0,1,3,2:T(8,128)} %bitcast.61, s32[4,67]{1,0:T(4,128)S(1)} %iota_add_fusion.3), kind=kOutput, calls=%fused_computation.80 | convolution fusion | flops 1687070720 | bytes 4293680 | tf_op jit(solution)/shard_map/dot_general | solution.py:125
  322.5 25.9 %all-to-all-done.4 = f32[67,32,256]{0,1,2:T(8,128)} async-done(((f32[67,32,256]{0,1,2:T(8,128)}), f32[67,32,256]{0,1,2:T(8,128)}, u32[]{:S(2)}, u32[]{:S(2)}) %all-to-all-start.4) | async-done | bytes 2195488 | tf_op jit(solution)/shard_map/all_to_all | solution.py:163
  348.4 10.4 %fusion.46 = f32[32,64,256]{2,1,0:T(8,128)S(1)} fusion(f32[32,64,256]{2,1,0:T(8,128)} %param.11, f32[32,64,256,1]{2,1,3,0:T(8,128)S(1)} %fusion.38, f32[67,32,4,64]{0,1,3,2:T(8,128)} %bitcast.53, s32[4,67]{1,0:T(4,128)S(1)} %iota_add_fusion.3), kind=kOutput, calls=%fused_computation.96 | convolution fusion | flops 1688119296 | bytes 8487984 | tf_op jit(solution)/shard_map/dot_general | solution.py:125
  358.8 10.7 %fusion.45 = f32[32,64,256]{2,1,0:T(8,128)S(1)} fusion(f32[32,64,256]{2,1,0:T(8,128)S(1)} %copy-done.5, f32[32,64,256,1]{2,1,3,0:T(8,128)S(1)} %copy-done.4, f32[67,32,4,64]{0,1,3,2:T(8,128)} %bitcast.53, s32[4,67]{1,0:T(4,128)S(1)} %iota_add_fusion.3), kind=kOutput, calls=%fused_computation.94 | convolution fusion | flops 1688119296 | bytes 8487984 | tf_op jit(solution)/shard_map/dot_general | solution.py:125
  369.5 4.8 fusion.92
  374.3 6.5 convolution_add_fusion
  380.9 6.9 copy.164
  387.7 5.6 reshape.1155
  393.4 4.5 all-to-all-start.7
  397.8 6.4 fusion.94
  404.2 6.3 convolution_subtract_fusion
  410.6 6.9 copy.161
  417.4 5.7 reshape.1153
  423.3 4.9 all-to-all-start.6
  428.3 7.5 reduce.20
  435.7 4.1 reshape.1156
  439.8 5.5 copy.166
  445.3 8.3 %all-to-all-done.6 = f32[4,1,137216]{2,1,0:T(1,128)} async-done(((f32[4,1,137216]{2,1,0:T(1,128)}), f32[4,1,137216]{2,1,0:T(1,128)}, u32[]{:S(2)}, u32[]{:S(2)}) %all-to-all-start.6) | async-done | bytes 2195488 | tf_op jit(solution)/shard_map/all_to_all | solution.py:163
  453.6 7.5 reduce.19
  461.0 4.1 reshape.1154
  465.1 5.6 copy.163
  470.8 10.6 %fusion.63 = f32[32,67,280,1]{2,1,3,0:T(8,128)S(1)} fusion(f32[32,64,4,67]{3,1,2,0:T(8,128)} %copy.163, s32[4,64]{1,0:T(4,128)S(1)} %multiply_add_fusion.1, s32[280]{0:T(512)S(1)} %add.764), kind=kOutput, calls=%fused_computation.131 | convolution fusion | flops 1845186560 | bytes 4598880 | tf_op jit(solution)/shard_map/dot_general | solution.py:125
  481.4 8.7 %bitcast_subtract_fusion = f32[32,67,280]{2,1,0:T(8,128)S(1)} fusion(f32[32,67,280,1]{2,1,3,0:T(8,128)S(1)} %fusion.63, f32[32,64,4,67]{3,1,2,0:T(8,128)S(1)} %copy-done.1, s32[4,64]{1,0:T(4,128)S(1)} %multiply_add_fusion.1, s32[280]{0:T(512)S(1)} %add.764), kind=kOutput, calls=%fused_computation.87 | convolution fusion | flops 1845786880 | bytes 7000160 | tf_op jit(solution)/shard_map/dot_general | solution.py:125
  493.9 4.6 all-to-all-start.8
  498.5 10.6 %fusion.61 = f32[32,67,280,1]{2,1,3,0:T(8,128)S(1)} fusion(f32[32,64,4,67]{3,1,2,0:T(8,128)} %copy.166, s32[4,64]{1,0:T(4,128)S(1)} %multiply_add_fusion.1, s32[280]{0:T(512)S(1)} %add.764), kind=kOutput, calls=%fused_computation.129 | convolution fusion | flops 1845186560 | bytes 4598880 | tf_op jit(solution)/shard_map/dot_general | solution.py:125
  509.0 8.5 %bitcast_add_fusion = f32[32,67,280]{2,1,0:T(8,128)S(1)} fusion(f32[32,67,280,1]{2,1,3,0:T(8,128)S(1)} %fusion.61, f32[32,64,4,67]{3,1,2,0:T(8,128)S(1)} %copy-done.2, s32[4,64]{1,0:T(4,128)S(1)} %multiply_add_fusion.1, s32[280]{0:T(512)S(1)} %add.764), kind=kOutput, calls=%fused_computation.86 | convolution fusion | flops 1845786880 | bytes 7000160 | tf_op jit(solution)/shard_map/dot_general | solution.py:125
  521.1 79.7 %all-to-all-done.8 = f32[32,67,280]{1,0,2:T(8,128)} async-done(((f32[32,67,280]{1,0,2:T(8,128)}), f32[32,67,280]{1,0,2:T(8,128)}, u32[]{:S(2)}, u32[]{:S(2)}) %all-to-all-start.8) | async-done | bytes 2401312 | tf_op jit(solution)/shard_map/all_to_all | solution.py:156
  600.9 4.6 all-to-all-start.9
  614.1 66.7 %collective-permute-done.3 = f32[7,3,1,256]{3,2,1,0:T(1,128)S(1)} collective-permute-done((f32[7,3,1,256]{3,2,1,0:T(1,128)S(1)}, f32[7,3,1,256]{3,2,1,0:T(1,128)S(1)}, u32[]{:S(2)}, u32[]{:S(2)}) %collective-permute-start.3) | collective-permute-done | bytes 21536 | tf_op jit(solution)/shard_map/ppermute | solution.py:25
  685.0 10.5 %fusion.106 = f32[67,35,256,1]{2,0,1,3:T(8,128)S(1)} fusion(f32[32,67,8,35]{1,0,3,2:T(8,128)} %bitcast.79, s32[8,32]{1,0:T(8,128)S(1)} %multiply_add_fusion), kind=kOutput, calls=%fused_computation.183 | convolution fusion | flops 1845100544 | bytes 4803584 | tf_op jit(solution)/shard_map/dot_general | solution.py:125
  695.4 12.7 %all-to-all-done.9 = f32[32,67,280]{1,0,2:T(8,128)} async-done(((f32[32,67,280]{1,0,2:T(8,128)}), f32[32,67,280]{1,0,2:T(8,128)}, u32[]{:S(2)}, u32[]{:S(2)}) %all-to-all-start.9) | async-done | bytes 2401312 | tf_op jit(solution)/shard_map/all_to_all | solution.py:157
  708.1 10.9 %fusion.44 = f32[67,35,256]{2,0,1:T(8,128)S(1)} fusion(f32[67,35,256,1]{2,0,1,3:T(8,128)S(1)} %fusion.106, f32[32,67,8,35]{1,0,3,2:T(8,128)} %bitcast.87, s32[8,32]{1,0:T(8,128)S(1)} %multiply_add_fusion), kind=kOutput, calls=%fused_computation.89 | convolution fusion | flops 1846301184 | bytes 7204864 | tf_op jit(solution)/shard_map/dot_general | solution.py:125
  719.1 4.5 multiply_reduce_fusion.3
  723.6 5.1 multiply_reduce_fusion.5
  729.6 13.0 %all-to-all-start.10 = ((f32[8,1,192]{2,1,0:T(1,128)}), f32[8,1,192]{2,1,0:T(1,128)S(1)}, u32[]{:S(2)}, u32[]{:S(2)}) async-start(f32[8,1,192]{2,1,0:T(1,128)} %reshape.1157), calls=%async_computation.10 | async-start | bytes 16384 | tf_op jit(solution)/shard_map/all_to_all | solution.py:296
  742.6 6.1 while.13
  (140 shorter events, 67.1 us)
Async XLA Ops:
  3.9 11.9 %all-to-all-start.1 = ((s32[1,8,64]{2,0,1:T(1,128)}), s32[1,8,64]{2,0,1:T(1,128)S(1)}, u32[]{:S(2)}, u32[]{:S(2)}) async-start(s32[1,8,64]{2,0,1:T(1,128)} %all_to_all.46), calls=%async_computation.1 | async-start | bytes 8192 | tf_op jit(solution)/shard_map/all_to_all | solution.py:268
  15.8 8.9 %all-to-all-start = ((f32[8,1,256]{2,1,0:T(1,128)}), f32[8,1,256]{2,1,0:T(1,128)S(1)}, u32[]{:S(2)}, u32[]{:S(2)}) async-start(f32[8,1,256]{2,1,0:T(1,128)} %reshape.1147), calls=%async_computation | async-start | bytes 16384 | tf_op jit(solution)/shard_map/all_to_all | solution.py:269
  27.2 1.1 copy-start.11
  28.4 0.7 copy-start.8
  41.9 6.1 copy-start.6
  70.5 60.0 %all-to-all-start.2 = ((f32[8,1,75040]{2,1,0:T(1,128)}), f32[8,1,75040]{2,1,0:T(1,128)}, u32[]{:S(2)}, u32[]{:S(2)}) async-start(f32[8,1,75040]{2,1,0:T(1,128)} %reshape.1151), calls=%async_computation.2 | async-start | bytes 4808704 | tf_op jit(solution)/shard_map/all_to_all | solution.py:156
  130.5 59.2 %all-to-all-start.3 = ((f32[8,1,75040]{2,1,0:T(1,128)}), f32[8,1,75040]{2,1,0:T(1,128)S(1)}, u32[]{:S(2)}, u32[]{:S(2)}) async-start(f32[8,1,75040]{2,1,0:T(1,128)} %reshape.1149), calls=%async_computation.3 | async-start | bytes 4808704 | tf_op jit(solution)/shard_map/all_to_all | solution.py:157
  222.4 10.2 %copy-start = (f32[67,35,256]{1,2,0:T(8,128)S(1)}, f32[67,35,256]{1,2,0:T(8,128)}, u32[]{:S(2)}) copy-start(f32[67,35,256]{1,2,0:T(8,128)} %copy.150) | copy-start | bytes 7203844
  244.3 52.4 %all-to-all-start.5 = ((f32[67,32,256]{0,1,2:T(8,128)}), f32[67,32,256]{0,1,2:T(8,128)}, u32[]{:S(2)}, u32[]{:S(2)}) async-start(f32[67,32,256]{0,1,2:T(8,128)} %copy.156), calls=%async_computation.5 | async-start | bytes 8388608 | tf_op jit(solution)/shard_map/all_to_all | solution.py:164
  296.6 51.7 %all-to-all-start.4 = ((f32[67,32,256]{0,1,2:T(8,128)}), f32[67,32,256]{0,1,2:T(8,128)}, u32[]{:S(2)}, u32[]{:S(2)}) async-start(f32[67,32,256]{0,1,2:T(8,128)} %copy.153), calls=%async_computation.4 | async-start | bytes 8388608 | tf_op jit(solution)/shard_map/all_to_all | solution.py:163
  348.4 10.4 %copy-start.4 = (f32[32,64,256,1]{2,1,3,0:T(8,128)S(1)}, f32[32,64,256,1]{2,1,3,0:T(8,128)}, u32[]{:S(2)}) copy-start(f32[32,64,256,1]{2,1,3,0:T(8,128)} %fusion.36) | copy-start | bytes 6291460
  348.4 10.5 %copy-start.5 = (f32[32,64,256]{2,1,0:T(8,128)S(1)}, f32[32,64,256]{2,1,0:T(8,128)}, u32[]{:S(2)}) copy-start(f32[32,64,256]{2,1,0:T(8,128)} %param.11) | copy-start | bytes 6291460
  358.8 15.5 %copy-start.3 = (f32[32,64,256]{2,1,0:T(8,128)}, f32[32,64,256]{2,1,0:T(8,128)S(1)}, u32[]{:S(2)}) copy-start(f32[32,64,256]{2,1,0:T(8,128)S(1)} %fusion.46) | copy-start | bytes 6291460
  393.4 29.9 %all-to-all-start.7 = ((f32[4,1,137216]{2,1,0:T(1,128)}), f32[4,1,137216]{2,1,0:T(1,128)}, u32[]{:S(2)}, u32[]{:S(2)}) async-start(f32[4,1,137216]{2,1,0:T(1,128)} %reshape.1155), calls=%async_computation.7 | async-start | bytes 4390912 | tf_op jit(solution)/shard_map/all_to_all | solution.py:164
  423.3 30.3 %all-to-all-start.6 = ((f32[4,1,137216]{2,1,0:T(1,128)}), f32[4,1,137216]{2,1,0:T(1,128)}, u32[]{:S(2)}, u32[]{:S(2)}) async-start(f32[4,1,137216]{2,1,0:T(1,128)} %reshape.1153), calls=%async_computation.6 | async-start | bytes 4390912 | tf_op jit(solution)/shard_map/all_to_all | solution.py:163
  470.8 10.6 %copy-start.1 = (f32[32,64,4,67]{3,1,2,0:T(8,128)S(1)}, f32[32,64,4,67]{3,1,2,0:T(8,128)}, u32[]{:S(2)}) copy-start(f32[32,64,4,67]{3,1,2,0:T(8,128)} %copy.166) | copy-start | bytes 6586372
  493.9 107.0 %all-to-all-start.8 = ((f32[32,67,280]{1,0,2:T(8,128)}), f32[32,67,280]{1,0,2:T(8,128)}, u32[]{:S(2)}, u32[]{:S(2)}) async-start(f32[32,67,280]{1,0,2:T(8,128)} %copy.167), calls=%async_computation.8 | async-start | bytes 9175040 | tf_op jit(solution)/shard_map/all_to_all | solution.py:156
  498.4 10.6 %copy-start.2 = (f32[32,64,4,67]{3,1,2,0:T(8,128)S(1)}, f32[32,64,4,67]{3,1,2,0:T(8,128)}, u32[]{:S(2)}) copy-start(f32[32,64,4,67]{3,1,2,0:T(8,128)} %copy.163) | copy-start | bytes 6586372
  521.1 84.3 %copy-start.17 = (s32[3,1,1,256]{3,2,1,0:T(1,128)S(1)}, s32[3,1,1,256]{3,2,1,0:T(1,128)}, u32[]{:S(2)}) copy-start(s32[3,1,1,256]{3,2,1,0:T(1,128)} %param.7) | copy-start | bytes 9220
  521.1 84.4 %copy-start.15 = (f32[3,1,1,256]{3,2,1,0:T(1,128)S(1)}, f32[3,1,1,256]{3,2,1,0:T(1,128)}, u32[]{:S(2)}) copy-start(f32[3,1,1,256]{3,2,1,0:T(1,128)} %param.8) | copy-start | bytes 9220
  521.1 84.4 %copy-start.16 = (f32[1,1,256]{2,1,0:T(1,128)S(1)}, f32[1,1,256]{2,1,0:T(1,128)}, u32[]{:S(2)}) copy-start(f32[1,1,256]{2,1,0:T(1,128)} %param.9) | copy-start | bytes 3076
  521.1 86.5 %copy-start.18 = (s32[1,1,2,8]{3,2,1,0:T(2,128)S(1)}, s32[1,1,2,8]{3,2,1,0:T(2,128)}, u32[]{:S(2)}) copy-start(s32[1,1,2,8]{3,2,1,0:T(2,128)} %param.10) | copy-start | bytes 196
  600.9 107.3 %all-to-all-start.9 = ((f32[32,67,280]{1,0,2:T(8,128)}), f32[32,67,280]{1,0,2:T(8,128)}, u32[]{:S(2)}, u32[]{:S(2)}) async-start(f32[32,67,280]{1,0,2:T(8,128)} %copy.170), calls=%async_computation.9 | async-start | bytes 9175040 | tf_op jit(solution)/shard_map/all_to_all | solution.py:157
  605.5 3.7 collective-permute-start.1
  607.0 4.5 collective-permute-start
  611.6 69.1 %collective-permute-start.3 = (f32[7,3,1,256]{3,2,1,0:T(1,128)S(1)}, f32[7,3,1,256]{3,2,1,0:T(1,128)S(1)}, u32[]{:S(2)}, u32[]{:S(2)}) collective-permute-start(f32[7,3,1,256]{3,2,1,0:T(1,128)S(1)} %pad_maximum_fusion.1), channel_id=1, source_target_pairs={{1,0},{2,1},{3,2},{4,3},{5,4},{6,5},{7,6},{0,7},{9,8},{10,9},{11,1... | collective-permute-start | bytes 64520 | tf_op jit(solution)/shard_map/ppermute | solution.py:25
  614.1 70.2 %collective-permute-start.2 = (f32[7,3,1,256]{3,2,1,0:T(1,128)S(1)}, f32[7,3,1,256]{3,2,1,0:T(1,128)S(1)}, u32[]{:S(2)}, u32[]{:S(2)}) collective-permute-start(f32[7,3,1,256]{3,2,1,0:T(1,128)S(1)} %pad_maximum_fusion.1), channel_id=1, source_target_pairs={{0,1},{1,2},{2,3},{3,4},{4,5},{5,6},{6,7},{7,0},{8,9},{9,10},{10,1... | collective-permute-start | bytes 64520 | tf_op jit(solution)/shard_map/ppermute | solution.py:22
  708.1 11.0 %copy-start.9 = (f32[67,512]{1,0:T(8,128)S(1)}, f32[67,512]{1,0:T(8,128)}, u32[]{:S(2)}) copy-start(f32[67,512]{1,0:T(8,128)} %copy-done.8) | copy-start | bytes 411652
  708.1 11.0 %copy-start.10 = (f32[256,512]{1,0:T(8,128)S(1)}, f32[256,512]{1,0:T(8,128)}, u32[]{:S(2)}) copy-start(f32[256,512]{1,0:T(8,128)} %get-tuple-element.106) | copy-start | bytes 1572868
  708.1 11.0 %copy-start.12 = (f32[35,512]{1,0:T(8,128)S(1)}, f32[35,512]{1,0:T(8,128)}, u32[]{:S(2)}) copy-start(f32[35,512]{1,0:T(8,128)} %copy-done.11) | copy-start | bytes 215044
  719.1 4.5 copy-start.7
  719.1 4.5 copy-start.13
  719.1 4.5 copy-start.14
  729.6 19.2 %all-to-all-start.10 = ((f32[8,1,192]{2,1,0:T(1,128)}), f32[8,1,192]{2,1,0:T(1,128)S(1)}, u32[]{:S(2)}, u32[]{:S(2)}) async-start(f32[8,1,192]{2,1,0:T(1,128)} %reshape.1157), calls=%async_computation.10 | async-start | bytes 16384 | tf_op jit(solution)/shard_map/all_to_all | solution.py:296
where the time goes:
time: 764 us; the launch traced here: 752 us
  waiting for transfers between devices  305 us (40%)
  matrix products  187 us (24%)
  local copies, waits for them, and re-layouts  146 us (19%)
  starting transfers between devices  63.9 us (8%)
  other arithmetic  47.8 us (6%)
    dot_general x23, matrix products, contract(): lax.dot_general(left, right, ((left_dims, right_dims), ((), ())), precisi...  187 us
    all_to_all x2, waiting for transfers between devices, dom_transpose(): lax.all_to_all(real_part, 'dom', split_axis=2, concat_axis=2, tiled=True)  116 us
    ppermute x2, waiting for transfers between devices, with_halo(): lax.ppermute(lax.slice_in_dim(block, 0, width, axis=dim), axis, backward)  68.1 us
    unnamed x50, local copies, waits for them, and re-layouts  55.2 us
    all_to_all x2, waiting for transfers between devices, dom_transpose(): lax.all_to_all(imag_part, 'dom', split_axis=2, concat_axis=2, tiled=True)  51.1 us
    all_to_all x2, waiting for transfers between devices, sect_transpose(): lax.all_to_all(real_part, 'sect', split_axis=2, concat_axis=2, tiled=True)  34.2 us
    all_to_all x2, waiting for transfers between devices, sect_transpose(): lax.all_to_all(imag_part, 'sect', split_axis=2, concat_axis=2, tiled=True)  24.3 us
  transfers between devices with their start and end apart: 15, of which 14 were waited for; matrix products, arithmetic and copies ran while one was open for 22% of the time, Pallas kernels for 0%

commit v1 on v0

v1 whole, which is shorter than its diff:
```python
import math

import jax
import jax.numpy as jnp
import numpy as np
from jax import lax
from jax.experimental import pallas as pl
from jax.experimental.pallas import tpu as pltpu
from jax.sharding import PartitionSpec as P

BLOCK = 128
XROWS = 8
CHUNKS = 2
VMEM = 56 * 1024 * 1024

ewald_beta = 0.1
soft_square = 9.0


def split_table(table):
    table = jnp.asarray(np.asarray(table, np.float32))
    high = table.astype(jnp.bfloat16)
    low = (table - high.astype(jnp.float32)).astype(jnp.bfloat16)
    return high, low


def split(value):
    high = value.astype(jnp.bfloat16)
    low = (value - high.astype(jnp.float32)).astype(jnp.bfloat16)
    return high, low


def dot(left, right, right_dim=0):
    return lax.dot_general(
        left, right, (((1,), (right_dim,)), ((), ())), preferred_element_type=jnp.float32
    )


def dot3(left, right, right_dim=0):
    return (
        dot(left[0], right[0], right_dim)
        + dot(left[0], right[1], right_dim)
        + dot(left[1], right[0], right_dim)
    )


def spline(frac):
    inner = 1.0 - frac
    square = frac * frac
    cube = square * frac
    weights = (
        inner * inner * inner / 6.0,
        (3.0 * cube - 6.0 * square + 4.0) / 6.0,
        (-3.0 * cube + 3.0 * square + 3.0 * frac + 1.0) / 6.0,
        cube / 6.0,
    )
    slopes = (
        -inner * inner / 2.0,
        (3.0 * square - 4.0 * frac) / 2.0,
        (-3.0 * square + 2.0 * frac + 1.0) / 2.0,
        square / 2.0,
    )
    return weights, slopes


def turn(steps, mesh_size):
    part = steps * (1.0 / mesh_size)
    part = part - jnp.floor(part)
    half = math.pi * jnp.where(part > 0.5, part - 1.0, part)
    sq = half * half
    sin = half
    cos = jnp.ones_like(half)
    term = half
    for n in range(1, 7):
        term = term * sq * (-1.0 / ((2 * n) * (2 * n + 1)))
        sin = sin + term
    term = cos
    for n in range(1, 8):
        term = term * sq * (-1.0 / ((2 * n - 1) * (2 * n)))
        cos = cos + term
    return 1.0 - 2.0 * sin * sin, 2.0 * sin * cos


def place(offset, values):
    out = jnp.zeros_like(offset)
    for k in range(4):
        out = jnp.where(offset == float(k), values[k], out)
    return out


def basis_kernel(mesh_size, z_width, slots_padded, where_ref, atoms, wx, vx, zq, zv, bwh, bwl, bvh, bvl):
    def row(n):
        return atoms[n : n + 1, :]

    lanes = atoms.shape[1]
    charge = row(6)

    def rows(count):
        return lax.broadcasted_iota(jnp.int32, (count, lanes), 0).astype(jnp.float32)

    weights, slopes = spline(row(3))
    offset = rows(wx.shape[0]) - row(0)
    wx[...] = place(offset, weights)
    vx[...] = place(offset, slopes)
    weights, slopes = spline(row(4))
    offset = rows(mesh_size) - row(1)
    offset = jnp.where(offset < 0.0, offset + mesh_size, offset)
    high, low = split(place(offset, weights))
    bwh[...] = high
    bwl[...] = low
    high, low = split(place(offset, slopes))
    bvh[...] = high
    bvl[...] = low
    weights, slopes = spline(row(5))
    wave = rows(slots_padded) + (where_ref[1] * z_width).astype(jnp.float32)
    parts = [jnp.zeros_like(wave) for _ in range(4)]
    for k in range(4):
        cos, sin = turn(wave * (row(2) + float(k)), mesh_size)
        parts[0] = parts[0] + (charge * weights[k]) * cos
        parts[1] = parts[1] - (charge * weights[k]) * sin
        parts[2] = parts[2] + (charge * slopes[k]) * cos
        parts[3] = parts[3] - (charge * slopes[k]) * sin
    zq[0:slots_padded, :] = parts[0]
    zq[slots_padded:, :] = parts[1]
    zv[0:slots_padded, :] = parts[2]
    zv[slots_padded:, :] = parts[3]


def spread_kernel(first, count, slots_padded, wx, zq, bwh, bwl, rh, rl, ih, il, out, acc):
    step = pl.program_id(0)
    rows = count * wx.shape[0]
    wide = wx[...]
    pieces = []
    for c in range(2):
        for g in range(count):
            at = c * slots_padded + first + g
            pieces.append(wide * zq[at : at + 1, :])
    left = split(jnp.concatenate(pieces, axis=0))
    part = dot3(left, (bwh[...], bwl[...]), 1)

    @pl.when(step == 0)
    def _():
        acc[...] = part

    @pl.when(step != 0)
    def _():
        acc[...] += part

    @pl.when(step == pl.num_programs(0) - 1)
    def _():
        real = split(acc[0:rows, :])
        imag = split(acc[rows:, :])
        lines = dot3(real, (rh[...], rl[...])) + dot3(imag, (ih[...], il[...]))
        lanes = out.shape[3]
        for s in range(out.shape[0]):
            out[s] = lines[:, s * lanes : (s + 1) * lanes].reshape(out.shape[1:])


def influence_kernel(scale, where_ref, own, across, edge, flip, same, back, out):
    slot = pl.program_id(0)
    own_pair = split(jnp.concatenate([own[0], own[0]], axis=0))
    across_pair = split(across[0])
    turned = dot(flip[...], across_pair[0]) + dot(flip[...], across_pair[1])
    lines = lax.broadcasted_iota(jnp.int32, turned.shape, 0) % own.shape[1]
    turned = split(jnp.where(lines == 0, edge[0], turned))
    plain = dot(same[...], own_pair[0], 1) + dot(same[...], own_pair[1], 1)
    mirror = dot(back[...], turned[0], 1) + dot(back[...], turned[1], 1)
    last = slot == pl.num_programs(0) - 1
    upper = where_ref[2] == 1
    keep_own = jnp.where(jnp.logical_and(last, jnp.logical_not(upper)), 0.0, scale)
    keep_mirror = jnp.where(slot == 0, 0.0, keep_own)
    out[0] = plain * keep_own + mirror * keep_mirror


def filter_kernel(lines, factor, th, tl, out):
    sects, count, extent, lanes = lines.shape
    width = extent - XROWS
    mesh_size = sects * width
    table = (th[...], tl[...])
    columns = []
    for g in range(count):
        pieces = []
        for s in range(sects):
            body = lines[s, g]
            before = lines[(s - 1) % sects, g, width:extent, :]
            pieces.append(body[0:XROWS] + before)
            pieces.append(body[XROWS:width])
        columns.append(jnp.concatenate(pieces, axis=0))
    both = dot3(table, split(jnp.concatenate(columns, axis=1)))
    half = lanes // 2
    sign = jnp.where(
        lax.broadcasted_iota(jnp.int32, (mesh_size, lanes), 1) < half, 1.0, -1.0
    )
    columns = []
    for g in range(count):
        cos = both[0:mesh_size, g * lanes : (g + 1) * lanes]
        sin = both[mesh_size:, g * lanes : (g + 1) * lanes]
        columns.append((cos + sign * pltpu.roll(sin, half, 1)) * factor[g])
    both = dot3(table, split(jnp.concatenate(columns, axis=1)))
    for g in range(count):
        cos = both[0:mesh_size, g * lanes : (g + 1) * lanes]
        sin = both[mesh_size:, g * lanes : (g + 1) * lanes]
        field = cos - sign * pltpu.roll(sin, half, 1)
        for s in range(sects):
            after = ((s + 1) % sects) * width
            out[s, g, 0:width, :] = field[s * width : (s + 1) * width]
            out[s, g, width:extent, :] = field[after : after + XROWS]


def gather_kernel(first, count, slots_padded, lines, bh, bl, wx, vx, zq, zv, bwh, bwl, bvh, bvl, out, eh, el):
    sects, _, extent, lanes = lines.shape
    rows = count * extent
    mesh_size = bwh.shape[0]

    @pl.when(pl.program_id(0) == 0)
    def _():
        joined = jnp.concatenate([lines[s].reshape(rows, lanes) for s in range(sects)], axis=1)
        field = dot3(split(joined), (bh[...], bl[...]))
        field = jnp.concatenate([field[:, 0:mesh_size], field[:, mesh_size:]], axis=0)
        high, low = split(field)
        eh[...] = high
        el[...] = low

    left = (eh[...], el[...])
    along = dot3(left, (bwh[...], bwl[...]))
    slope = dot3(left, (bvh[...], bvl[...]))
    sums = [jnp.zeros(wx.shape, jnp.float32) for _ in range(3)]
    for c in range(2):
        for g in range(count):
            at = c * slots_padded + first + g
            low = (c * count + g) * extent
            line = along[low : low + extent]
            sums[0] = sums[0] + line * zq[at : at + 1, :]
            sums[1] = sums[1] + slope[low : low + extent] * zq[at : at + 1, :]
            sums[2] = sums[2] + line * zv[at : at + 1, :]
    out[0:1, :] = -jnp.sum(sums[0] * vx[...], axis=0, keepdims=True)
    out[1:2, :] = -jnp.sum(sums[1] * wx[...], axis=0, keepdims=True)
    out[2:3, :] = -jnp.sum(sums[2] * wx[...], axis=0, keepdims=True)
    out[3:, :] = jnp.zeros((out.shape[0] - 3, out.shape[1]), jnp.float32)


def params():
    return pltpu.CompilerParams(vmem_limit_bytes=VMEM)


def whole(array):
    return pl.BlockSpec(array.shape, lambda *_: (0,) * array.ndim)


def along_atoms(rows, step):
    return pl.BlockSpec((rows, step), lambda n: (0, n))


SMEM = pl.BlockSpec(memory_space=pltpu.SMEM)


def pair_kernel(centre, others, mesh_size):
    half_mesh = float(mesh_size // 2)
    displace = []
    for component in range(3):
        offset = centre[component][None, :, None] - others[component][:, None, :]
        wrapped = jnp.mod(offset + half_mesh, float(mesh_size)) - half_mesh
        displace.append(
            wrapped + (centre[component + 3][None, :, None] - others[component + 3][:, None, :])
        )
    square = (
        displace[0] * displace[0]
        + displace[1] * displace[1]
        + displace[2] * displace[2]
        + soft_square
    )
    distance = jnp.sqrt(square)
    kernel = (
        lax.erfc(ewald_beta * distance) / (square * distance)
        + 2.0
        * ewald_beta
        / math.sqrt(math.pi)
        * jnp.exp(-ewald_beta * ewald_beta * square)
        / square
    )
    coupling = centre[6][None, :, None] * others[6][:, None, :] * kernel
    return jnp.stack([jnp.sum(coupling * shift_vector, axis=(0, 2)) for shift_vector in displace])


def shards(cells, fracs, charges, pair_blocks, influence):
    sects = lax.axis_size("sect")
    doms = lax.axis_size("dom")
    sect = lax.axis_index("sect")
    dom = lax.axis_index("dom")
    z_width, x_width, mesh_size = influence.shape
    atom_count = charges.shape[2]
    block_count = atom_count // BLOCK
    listed_count = pair_blocks.shape[3]
    half = z_width // 2
    slots = half + 1
    slots_padded = -(-slots // 8) * 8
    extent = x_width + XROWS
    lanes = 2 * x_width
    total = doms * atom_count
    where_am_i = jnp.stack([sect, dom, (dom >= doms // 2).astype(jnp.int32)])

    packed = jnp.concatenate(
        [cells.astype(jnp.float32), fracs, charges[None], jnp.zeros_like(charges)[None]], axis=0
    ).reshape(8, block_count, BLOCK)
    packed = jnp.transpose(packed, (1, 0, 2))
    everyone = lax.all_gather(packed, ("sect", "dom"))
    row = lax.dynamic_index_in_dim(
        everyone.reshape(sects, doms, block_count, 8, BLOCK), sect, 0, keepdims=False
    )
    atoms = jnp.transpose(row, (2, 0, 1, 3)).reshape(8, total)
    first_cell = jnp.zeros((8, 1), jnp.float32).at[0, 0].set(1.0) * (sect * x_width).astype(jnp.float32)
    atoms = atoms - first_cell

    opposite = []
    edges = []
    for s in range(sects):
        for d in range(doms):
            opposite.append((s * doms + d, (sects - 1 - s) * doms + doms - 1 - d))
            edges.append((s * doms + d, ((sects - s) % sects) * doms + doms - 1 - d))
    across = lax.ppermute(influence[half:], ("sect", "dom"), opposite)
    edge = lax.ppermute(influence[half:, 0:1], ("sect", "dom"), edges)
    flip = np.zeros((2 * x_width, x_width), np.float32)
    for i in range(1, x_width):
        flip[i, x_width - i] = 1.0
        flip[x_width + i, x_width - i] = 1.0
    same = np.eye(mesh_size, dtype=np.float32)
    back = np.roll(same[::-1], 1, axis=0)
    flip, same, back = (jnp.asarray(m).astype(jnp.bfloat16) for m in (flip, same, back))
    factor = pl.pallas_call(
        lambda *refs: influence_kernel(float(mesh_size) ** -3, *refs),
        grid=(slots,),
        in_specs=[
            SMEM,
            pl.BlockSpec((1, x_width, mesh_size), lambda j: (j, 0, 0)),
            pl.BlockSpec((1, x_width, mesh_size), lambda j: (jnp.minimum(half - j, half - 1), 0, 0)),
            pl.BlockSpec((1, 1, mesh_size), lambda j: (jnp.minimum(half - j, half - 1), 0, 0)),
            whole(flip),
            whole(same),
            whole(back),
        ],
        out_specs=pl.BlockSpec((1, mesh_size, lanes), lambda j: (j, 0, 0)),
        out_shape=jax.ShapeDtypeStruct((slots, mesh_size, lanes), jnp.float32),
        compiler_params=params(),
        name="influence",
    )(where_am_i, influence, across, edge, flip, same, back)

    step = np.arange(mesh_size)
    angle = 2.0 * np.pi * (np.outer(step, step) % mesh_size) / mesh_size
    cos, sin = np.cos(angle), np.sin(angle)

    def by_sect(real, imag):
        real = real.reshape(mesh_size, sects, 1, x_width)
        imag = imag.reshape(mesh_size, sects, 1, x_width)
        return np.concatenate([real, imag], axis=2).reshape(mesh_size, 2 * mesh_size)

    rh, rl = split_table(by_sect(cos, -sin))
    ih, il = split_table(by_sect(sin, cos))
    bh, bl = split_table(np.concatenate([by_sect(cos, -sin).T, by_sect(sin, cos).T], axis=1))
    th, tl = split_table(np.concatenate([cos, sin], axis=0))

    atom_step = 512
    grid = (total // atom_step,)
    f32, bf16 = jnp.float32, jnp.bfloat16
    shapes = [
        ((extent, total), f32),
        ((extent, total), f32),
        ((2 * slots_padded, total), f32),
        ((2 * slots_padded, total), f32),
    ] + [((mesh_size, total), bf16)] * 4
    wx, vx, zq, zv, bwh, bwl, bvh, bvl = pl.pallas_call(
        lambda *refs: basis_kernel(mesh_size, z_width, slots_padded, *refs),
        grid=grid,
        in_specs=[SMEM, along_atoms(8, atom_step)],
        out_specs=[along_atoms(shape[0], atom_step) for shape, _ in shapes],
        out_shape=[jax.ShapeDtypeStruct(shape, dtype) for shape, dtype in shapes],
        compiler_params=params(),
        name="basis",
    )(where_am_i, atoms)

    firsts = [slots * n // CHUNKS for n in range(CHUNKS + 1)]
    counts = [b - a for a, b in zip(firsts, firsts[1:])]
    sent = []
    for first, count in zip(firsts, counts):
        shape = (sects, count, extent, lanes)
        lines = pl.pallas_call(
            lambda *refs, first=first, count=count: spread_kernel(first, count, slots_padded, *refs),
            grid=grid,
            in_specs=[
                along_atoms(extent, atom_step),
                along_atoms(2 * slots_padded, atom_step),
                along_atoms(mesh_size, atom_step),
                along_atoms(mesh_size, atom_step),
            ]
            + [whole(t) for t in (rh, rl, ih, il)],
            out_specs=pl.BlockSpec(shape, lambda n: (0, 0, 0, 0)),
            out_shape=jax.ShapeDtypeStruct(shape, f32),
            scratch_shapes=[pltpu.VMEM((2 * count * extent, mesh_size), f32)],
            compiler_params=params(),
            name="spread",
        )(wx, zq, bwh, bwl, rh, rl, ih, il)
        sent.append(lax.all_to_all(lines, "sect", split_axis=0, concat_axis=0, tiled=True))
    fields = []
    for lines, first, count in zip(sent, firsts, counts):
        field = pl.pallas_call(
            filter_kernel,
            grid=(1,),
            in_specs=[
                whole(lines),
                pl.BlockSpec((count, mesh_size, lanes), lambda n: (0, 0, 0)),
                whole(th),
                whole(tl),
            ],
            out_specs=whole(lines),
            out_shape=jax.ShapeDtypeStruct(lines.shape, f32),
            compiler_params=params(),
            name="filter",
        )(lines, factor[first : first + count], th, tl)
        fields.append(lax.all_to_all(field, "sect", split_axis=0, concat_axis=0, tiled=True))

    listed = pair_blocks[0, 0]
    neighbour = listed // block_count
    from_sect = (sect + neighbour // 3 - 1) % sects
    from_dom = (dom + neighbour % 3 - 1) % doms
    source = (from_sect * doms + from_dom) * block_count + listed % block_count
    pool = everyone.reshape(sects * doms * block_count, 8 * BLOCK)
    pick = (source.reshape(-1, 1) == jnp.arange(pool.shape[0], dtype=jnp.int32)[None]).astype(f32)
    chosen = lax.dot_general(
        pick, pool, (((1,), (0,)), ((), ())), precision=lax.Precision.HIGHEST, preferred_element_type=f32
    ).reshape(block_count, listed_count, 8, BLOCK)
    chosen = jnp.transpose(chosen, (0, 2, 1, 3))
    block_forces = jnp.stack(
        [pair_kernel(packed[b], chosen[b], mesh_size) for b in range(block_count)], axis=1
    )
    short_force = block_forces.reshape(3, atom_count)

    partial = None
    for lines, first, count in zip(fields, firsts, counts):
        forces = pl.pallas_call(
            lambda *refs, first=first, count=count: gather_kernel(first, count, slots_padded, *refs),
            grid=grid,
            in_specs=[whole(lines), whole(bh), whole(bl)]
            + [along_atoms(a.shape[0], atom_step) for a in (wx, vx, zq, zv, bwh, bwl, bvh, bvl)],
            out_specs=along_atoms(8, atom_step),
            out_shape=jax.ShapeDtypeStruct((8, total), f32),
            scratch_shapes=[pltpu.VMEM((2 * count * extent, mesh_size), bf16)] * 2,
            compiler_params=params(),
            name="gather",
        )(lines, bh, bl, wx, vx, zq, zv, bwh, bwl, bvh, bvl)
        partial = forces if partial is None else partial + forces
    by_dom = jnp.transpose(partial[:3].reshape(3, doms, atom_count), (1, 0, 2))
    mesh_force = lax.psum_scatter(by_dom, "dom", scatter_dimension=0, tiled=False)
    return (short_force + mesh_force).reshape(3, 1, 1, atom_count)


def solution(mesh):
    in_specs = (
        P(None, "sect", "dom", None),
        P(None, "sect", "dom", None),
        P("sect", "dom", None),
        P("sect", "dom", None, None),
        P("dom", "sect", None),
    )
    out_specs = P(None, "sect", "dom", None)
    return jax.shard_map(shards, mesh=mesh, in_specs=in_specs, out_specs=out_specs, check_vma=False)
```

time: 764 us -> 224 us (0.29); the launches traced: 752 us -> 222 us
  waiting for transfers between devices: 305 us -> 36.4 us
  matrix products: 187 us -> 1.18 us
  local copies, waits for them, and re-layouts: 146 us -> 11.3 us
  Pallas kernels: 0 us -> 74.7 us
  blocking collectives: 0 us -> 70.2 us
  starting transfers between devices: 63.9 us -> 16.3 us
  other arithmetic: 47.8 us -> 11.6 us
    all_to_all x11 -> x4, waiting for transfers between devices: 231 us -> 31.4 us  [the longest x2 27.8 us: shards(): lax.all_to_all(lines, 'sect', split_axis=0, concat_axis=0, tiled=True)]
    dot_general x23 -> x1, matrix products: 187 us -> 1.18 us  [shards(): lax.dot_general(pick, pool, (((1,), (0,)), ((), ())), precision=lax.Preci...]
    pallas_call x0 -> x8, Pallas kernels: none -> 74.7 us  [the longest x2 26.5 us: shards(): pl.pallas_call(lambda *refs, first=first, count=count: gather_kernel(firs...]
    ppermute x4 -> x2, waiting for transfers between devices: 74 us -> 4.96 us  [the longest x1 4.96 us: shards(): edge = lax.ppermute(influence[half:, 0:1], ('sect', 'dom'), edges)]
    unnamed x50 -> x77, local copies, waits for them, and re-layouts: 55.2 us -> 4.07 us
    all_gather x0 -> x1, blocking collectives: none -> 44.3 us  [shards(): everyone = lax.all_gather(packed, ('sect', 'dom'))]
    all_to_all x11 -> x4, starting transfers between devices: 59.3 us -> 16.3 us  [the longest x2 9.06 us: shards(): lax.all_to_all(field, 'sect', split_axis=0, concat_axis=0, tiled=True)]
    all_to_all x7 -> x0, other arithmetic: 34.9 us -> none  [the longest x1 9.51 us: dom_transpose(): lax.all_to_all(real_part, 'dom', split_axis=2, concat_axis=2, tiled=True)]
  transfers between devices with their start and end apart: 15 -> 6, of which waited for: 14 -> 3; matrix products, arithmetic and copies ran while one was open for 22% -> 7% of each run, Pallas kernels for 0% -> 21%
where the time goes in v1:
time: 224 us; the launch traced here: 222 us
  Pallas kernels  74.7 us (33%)
  blocking collectives  70.2 us (31%)
  waiting for transfers between devices  36.4 us (16%)
  starting transfers between devices  16.3 us (7%)
  other arithmetic  11.6 us (5%)
  local copies, waits for them, and re-layouts  11.3 us (5%)
    all_gather x1, blocking collectives, shards(): everyone = lax.all_gather(packed, ('sect', 'dom'))  44.3 us
    all_to_all x2, waiting for transfers between devices, shards(): lax.all_to_all(lines, 'sect', split_axis=0, concat_axis=0, tiled=True)  27.8 us
    pallas_call x2, Pallas kernels, shards(): pl.pallas_call(lambda *refs, first=first, count=count: gather_kernel(firs...  26.5 us
    unnamed x1, blocking collectives  25.9 us
    pallas_call x2, Pallas kernels, shards(): pl.pallas_call(lambda *refs, first=first, count=count: spread_kernel(firs...  18.2 us
    pallas_call x1, Pallas kernels, shards(): pl.pallas_call(lambda *refs: influence_kernel(float(mesh_size) ** (-3), *...  13.2 us
    pallas_call x2, Pallas kernels, shards(): pl.pallas_call(filter_kernel, grid=(1,), in_specs=[whole(lines), pl.Block...  11.2 us
    all_to_all x2, starting transfers between devices, shards(): lax.all_to_all(field, 'sect', split_axis=0, concat_axis=0, tiled=True)  9.06 us
  transfers between devices with their start and end apart: 6, of which 3 were waited for; matrix products, arithmetic and copies ran while one was open for 7% of the time, Pallas kernels for 21%

profile of v1, /device:TPU:0, one launch (start us, length us, event | category | flops | bytes accessed | tf_op | source)
XLA Modules:
  0.0 222.2 jit_solution(11589755965202226264)
XLA Ops:
  0.0 0.7 convert_element_type.53
  0.7 0.1 pad.20.clone
  0.8 0.8 maximum_bitcast_fusion
  1.5 0.6 copy-done.7
  2.1 44.3 %all-gather = f32[64,8,128]{2,1,0:T(8,128)S(1)} all-gather(f32[2,8,128]{2,1,0:T(8,128)S(1)} %copy.29), channel_id=2, replica_groups=mesh['sect'=4,'dom'=8] {'sect','dom'}, dimensions={0}, use_global_device_ids=true | all-gather | bytes 270336 | tf_op jit(solution)/shard_map/all_gather | solution.py:306
  46.4 0.7 broadcast_multiply_fusion
  47.1 0.7 broadcast_subtract_fusion.refs_1_
  47.7 0.6 pad_add_fusion.refs_0_
  48.4 5.7 %basis.1 = (f32[72,2048]{1,0:T(8,128)}, f32[72,2048]{1,0:T(8,128)}, f32[48,2048]{1,0:T(8,128)}, f32[48,2048]{1,0:T(8,128)}, bf16[256,2048]{1,0:T(8,128)(2,1)}, /...) custom-call(s32[3]{0:T(128)} %pad_add_fusion.refs_0_, ...), custom_call_target="tpu_custom_call" | custom-call | tf_op jit(solution)/shard_map/basis/pallas_call | solution.py:370
  54.1 8.8 %spread.2 = f32[4,8,72,128]{3,2,1,0:T(8,128)} custom-call(f32[72,2048]{1,0:T(8,128)} %get-tuple-element.25.refs_0_.refs_3_, f32[48,2048]{1,0:T(8,128)} %get-tuple-element.26.refs_1_.refs_5_, bf16[256,2048]{1,0:T(8,128)(2,1)} %get-tuple-element.27.refs_2_.refs_7_, bf16[256,2048]{1,0:T(8,128)(2,1)} %get-tuple-element.28.refs_3_.refs_8_, ...), custom_call_target="tpu_custom_call" | custom-call | tf_op jit(solution)/shard_map/spread/pallas_call | solution.py:385
  62.9 3.7 %all-to-all-start = ((f32[4,8,72,128]{3,2,1,0:T(8,128)}), f32[4,8,72,128]{3,2,1,0:T(8,128)S(1)}, u32[]{:S(2)}, u32[]{:S(2)}) async-start(f32[4,8,72,128]{3,2,1,0:T(8,128)} %spread.2), calls=%async_computation | async-start | bytes 2359296 | tf_op jit(solution)/shard_map/all_to_all | solution.py:401
  66.5 1.1 slice.203
  67.6 0.0 collective-permute-start
  67.6 9.4 %spread.3 = f32[4,9,72,128]{3,2,1,0:T(8,128)} custom-call(f32[72,2048]{1,0:T(8,128)} %get-tuple-element.25.refs_0_.refs_3_, f32[48,2048]{1,0:T(8,128)} %get-tuple-element.26.refs_1_.refs_5_, bf16[256,2048]{1,0:T(8,128)(2,1)} %get-tuple-element.27.refs_2_.refs_7_, bf16[256,2048]{1,0:T(8,128)(2,1)} %get-tuple-element.28.refs_3_.refs_8_, ...), custom_call_target="tpu_custom_call" | custom-call | tf_op jit(solution)/shard_map/spread/pallas_call | solution.py:385
  77.0 27.8 %all-to-all-done.lines = f32[4,8,72,128]{3,2,1,0:T(8,128)S(1)} async-done(((f32[4,8,72,128]{3,2,1,0:T(8,128)}), f32[4,8,72,128]{3,2,1,0:T(8,128)S(1)}, u32[]{:S(2)}, u32[]{:S(2)}) %all-to-all-start) | async-done | bytes 1179680 | tf_op jit(solution)/shard_map/all_to_all | solution.py:401
  104.8 1.0 copy-done.4
  105.8 3.5 %all-to-all-start.2 = ((f32[4,9,72,128]{3,2,1,0:T(8,128)}), f32[4,9,72,128]{3,2,1,0:T(8,128)S(1)}, u32[]{:S(2)}, u32[]{:S(2)}) async-start(f32[4,9,72,128]{3,2,1,0:T(8,128)} %spread.3), calls=%async_computation.2 | async-start | bytes 2654208 | tf_op jit(solution)/shard_map/all_to_all | solution.py:401
  109.4 0.1 collective-permute-start.1
  109.5 5.0 %collective-permute-done.1.refs_3_ = f32[16,1,256]{2,1,0:T(1,128)S(1)} collective-permute-done((f32[16,1,256]{2,1,0:T(1,128)S(1)}, f32[16,1,256]{2,1,0:T(1,128)S(1)}, u32[]{:S(2)}, u32[]{:S(2)}) %collective-permute-start.1) | collective-permute-done | bytes 16416 | tf_op jit(solution)/shard_map/ppermute | solution.py:321
  114.4 0.0 collective-permute-done.refs_2_
  114.4 0.6 copy-done.8
  115.0 13.2 %influence.1 = f32[17,256,128]{2,1,0:T(8,128)} custom-call(s32[3]{0:T(128)} %pad_add_fusion.refs_0_, f32[32,64,256]{2,1,0:T(8,128)} %refs_1_.1, f32[16,64,256]{2,1,0:T(8,128)} %collective-permute-done.refs_2_, f32[16,1,256]{2,1,0:T(1,128)} %copy-done.8, bf16[128,64]{1,0:T(8,128)(2,1)} %constant.240.refs_4_, bf16[256,256]{1,0:T(8,128)(2,1)} %constant.241.refs_5_, ...), custom_call_target="tpu_custom_call" | custom-call | tf_op jit(solution)/shard_map/influence/pallas_call | solution.py:329
  128.3 2.3 %slice.236.factor = f32[8,256,128]{2,1,0:T(8,128)} slice(f32[17,256,128]{2,1,0:T(8,128)} %influence.1), slice={[0:8], [0:256], [0:128]} | slice | bytes 2097152 | tf_op jit(solution)/shard_map/slice | solution.py:417
  130.6 4.9 %filter.2 = f32[4,8,72,128]{3,2,1,0:T(8,128)} custom-call(f32[4,8,72,128]{3,2,1,0:T(8,128)} %copy-done.4, f32[8,256,128]{2,1,0:T(8,128)} %slice.236.factor, bf16[512,256]{1,0:T(8,128)(2,1)} %constant.243.th, bf16[512,256]{1,0:T(8,128)(2,1)} %constant.246.tl), custom_call_target="tpu_custom_call" | custom-call | tf_op jit(solution)/shard_map/filter/pallas_call | solution.py:404
  135.4 0.0 all-to-all-done.2.lines
  135.4 5.3 %all-to-all-start.1 = ((f32[4,8,72,128]{3,2,1,0:T(8,128)}), f32[4,8,72,128]{3,2,1,0:T(8,128)}, u32[]{:S(2)}, u32[]{:S(2)}) async-start(f32[4,8,72,128]{3,2,1,0:T(8,128)} %filter.2), calls=%async_computation.1 | async-start | bytes 2359296 | tf_op jit(solution)/shard_map/all_to_all | solution.py:418
  140.8 0.7 fusion.66
  141.5 1.4 slice_bitcast_fusion.27
  142.9 1.2 convolution_bitcast_fusion
  144.1 0.7 slice_bitcast_fusion.13
  144.7 1.1 slice.237.factor
  145.9 6.3 %filter.3 = f32[4,9,72,128]{3,2,1,0:T(8,128)} custom-call(f32[4,9,72,128]{3,2,1,0:T(8,128)} %copy-done.1, f32[9,256,128]{2,1,0:T(8,128)} %slice.237.factor, bf16[512,256]{1,0:T(8,128)(2,1)} %constant.243.th, bf16[512,256]{1,0:T(8,128)(2,1)} %constant.246.tl), custom_call_target="tpu_custom_call" | custom-call | tf_op jit(solution)/shard_map/filter/pallas_call | solution.py:404
  152.3 0.0 copy-start.37
  152.3 0.0 copy-start.9
  152.3 0.0 copy-start.10
  152.3 0.0 copy-start.11
  152.3 0.0 copy-start.12
  152.3 0.0 copy-start.13
  152.3 0.0 copy-start.14
  152.3 0.0 copy-start.15
  152.3 0.0 copy-start.23
  152.4 3.6 %all-to-all-done.1.refs_0_ = f32[4,8,72,128]{3,2,1,0:T(8,128)} async-done(((f32[4,8,72,128]{3,2,1,0:T(8,128)}), f32[4,8,72,128]{3,2,1,0:T(8,128)}, u32[]{:S(2)}, u32[]{:S(2)}) %all-to-all-start.1) | async-done | bytes 1179680 | tf_op jit(solution)/shard_map/all_to_all | solution.py:418
  156.1 3.7 %all-to-all-start.3 = ((f32[4,9,72,128]{3,2,1,0:T(8,128)}), f32[4,9,72,128]{3,2,1,0:T(8,128)S(1)}, u32[]{:S(2)}, u32[]{:S(2)}) async-start(f32[4,9,72,128]{3,2,1,0:T(8,128)} %filter.3), calls=%async_computation.3 | async-start | bytes 2654208 | tf_op jit(solution)/shard_map/all_to_all | solution.py:418
  159.9 3.0 %multiply_reduce_fusion.2 = (f32[128]{0:T(128)S(1)}, f32[128]{0:T(128)S(1)}, f32[128]{0:T(128)S(1)}) fusion(f32[8,128]{1,0:T(8,128)S(1)} %copy-done.20, f32[128]{0:T(128)S(1)} %copy-done.34, f32[8,128]{1,0:T(8,128)S(1)} %copy-done.21, f32[128]{0:T(128)S(1)} %copy-done.35, f32[8,128]{1,0:T(8,128)S(1)} %copy-done.16, f32[128]{0:T(128)S(1)} %copy-done.30, ...), kind=kLoop, calls=%fused_computation.35 | loop fusion | flops 14941824 | bytes 33792 | tf_op jit(solution)/shard_map/reduce_sum | solution.py:282
  162.9 0.6 dynamic-slice.6
  163.6 0.0 copy-done.9
  163.6 0.0 copy-done.13
  163.6 0.0 copy-done.14
  163.6 0.0 copy-done.15
  163.6 0.0 copy-done.23
  163.6 0.0 copy-done.24
  163.6 0.0 copy-done.25
  163.6 0.0 copy-done.26
  163.6 0.0 copy-done.27
  163.7 0.0 copy-done.28
  163.7 3.0 %multiply_reduce_fusion.5 = (f32[128]{0:T(128)S(1)}, f32[128]{0:T(128)S(1)}, f32[128]{0:T(128)S(1)}) fusion(f32[8,128]{1,0:T(8,128)S(1)} %copy-done.14, f32[128]{0:T(128)S(1)} %copy-done.28, f32[8,128]{1,0:T(8,128)S(1)} %copy-done.15, f32[128]{0:T(128)S(1)} %copy-done.29, f32[8,128]{1,0:T(8,128)S(1)} %copy-done.10, f32[128]{0:T(128)S(1)} %copy-done.24, ...), kind=kLoop, calls=%fused_computation.63 | loop fusion | flops 14941824 | bytes 33792 | tf_op jit(solution)/shard_map/reduce_sum | solution.py:282
  166.7 12.6 %gather.2 = f32[8,2048]{1,0:T(8,128)} custom-call(f32[4,8,72,128]{3,2,1,0:T(8,128)} %all-to-all-done.1.refs_0_, bf16[512,512]{1,0:T(8,128)(2,1)} %constant.247.refs_1_, bf16[512,512]{1,0:T(8,128)(2,1)} %constant.250.refs_2_, f32[72,2048]{1,0:T(8,128)} %get-tuple-element.25.refs_0_.refs_3_, f32[72,2048]{1,0:T(8,128)} %get-tuple-element.29.refs_4_, ...), custom_call_target="tpu_custom_call" | custom-call | tf_op jit(solution)/shard_map/gather/pallas_call | solution.py:438
  179.3 0.0 all-to-all-done.3.refs_0_
  179.3 1.1 copy-done.2
  180.4 13.9 %gather.3 = f32[8,2048]{1,0:T(8,128)} custom-call(f32[4,9,72,128]{3,2,1,0:T(8,128)} %copy-done.2, bf16[512,512]{1,0:T(8,128)(2,1)} %constant.247.refs_1_, bf16[512,512]{1,0:T(8,128)(2,1)} %constant.250.refs_2_, f32[72,2048]{1,0:T(8,128)} %get-tuple-element.25.refs_0_.refs_3_, f32[72,2048]{1,0:T(8,128)} %get-tuple-element.29.refs_4_, ...), custom_call_target="tpu_custom_call" | custom-call | tf_op jit(solution)/shard_map/gather/pallas_call | solution.py:438
  194.2 0.8 slice_add_fusion
  195.1 25.9 %all-reduce = f32[8,3,256]{2,1,0:T(4,128)S(1)} all-reduce(f32[8,3,256]{2,1,0:T(4,128)S(1)} %bitcast.134), channel_id=3, replica_groups=mesh['sect'=4,'dom'=8] {'dom'}, use_global_device_ids=true, to_apply=%region_6.7.clone | all-reduce | flops 6144 | bytes 49152
  221.0 0.6 fusion.61
  221.7 0.6 copy.32
  (57 shorter events, 0.1 us)
Async XLA Ops:
  1.5 0.6 copy-start.7
  46.4 16.5 %copy-start.5 = (f32[64,8,128]{2,1,0:T(8,128)}, f32[64,8,128]{2,1,0:T(8,128)S(1)}, u32[]{:S(2)}) copy-start(f32[64,8,128]{2,1,0:T(8,128)S(1)} %all-gather) | copy-start | bytes 786436
  62.9 3.7 %copy-start.3 = (f32[32,64,256]{2,1,0:T(8,128)S(1)}, f32[32,64,256]{2,1,0:T(8,128)}, u32[]{:S(2)}) copy-start(f32[32,64,256]{2,1,0:T(8,128)} %refs_1_.1) | copy-start | bytes 6291460
  62.9 42.0 %all-to-all-start = ((f32[4,8,72,128]{3,2,1,0:T(8,128)}), f32[4,8,72,128]{3,2,1,0:T(8,128)S(1)}, u32[]{:S(2)}, u32[]{:S(2)}) async-start(f32[4,8,72,128]{3,2,1,0:T(8,128)} %spread.2), calls=%async_computation | async-start | bytes 2359296 | tf_op jit(solution)/shard_map/all_to_all | solution.py:401
  67.6 46.8 %collective-permute-start = (f32[16,64,256]{2,1,0:T(8,128)}, f32[16,64,256]{2,1,0:T(8,128)}, u32[]{:S(2)}, u32[]{:S(2)}) collective-permute-start(f32[16,64,256]{2,1,0:T(8,128)} %slice.203), channel_id=1, source_target_pairs={{0,31},{1,30},{2,29},{3,28},{4,27},{5,26},{6,25},{7,24},{8,23},{9,... | collective-permute-start | bytes 3145736 | tf_op jit(solution)/shard_map/ppermute | solution.py:320
  104.8 1.0 copy-start.4
  105.8 29.6 %all-to-all-start.2 = ((f32[4,9,72,128]{3,2,1,0:T(8,128)}), f32[4,9,72,128]{3,2,1,0:T(8,128)S(1)}, u32[]{:S(2)}, u32[]{:S(2)}) async-start(f32[4,9,72,128]{3,2,1,0:T(8,128)} %spread.3), calls=%async_computation.2 | async-start | bytes 2654208 | tf_op jit(solution)/shard_map/all_to_all | solution.py:401
  109.4 5.0 %collective-permute-start.1 = (f32[16,1,256]{2,1,0:T(1,128)S(1)}, f32[16,1,256]{2,1,0:T(1,128)S(1)}, u32[]{:S(2)}, u32[]{:S(2)}) collective-permute-start(f32[16,1,256]{2,1,0:T(1,128)S(1)} %slice.204), channel_id=1, source_target_pairs={{0,7},{1,6},{2,5},{3,4},{4,3},{5,2},{6,1},{7,0},{8,31},{9,30},{10,... | collective-permute-start | bytes 49160 | tf_op jit(solution)/shard_map/ppermute | solution.py:321
  114.4 0.6 copy-start.8
  135.4 9.3 %copy-start = (f32[17,256,128]{2,1,0:T(8,128)S(1)}, f32[17,256,128]{2,1,0:T(8,128)}, u32[]{:S(2)}) copy-start(f32[17,256,128]{2,1,0:T(8,128)} %influence.1) | copy-start | bytes 6684676
  135.4 8.6 %copy-start.1 = (f32[4,9,72,128]{3,2,1,0:T(8,128)}, f32[4,9,72,128]{3,2,1,0:T(8,128)S(1)}, u32[]{:S(2)}) copy-start(f32[4,9,72,128]{3,2,1,0:T(8,128)S(1)} %all-to-all-done.2.lines) | copy-start | bytes 3981316
  135.4 20.6 %all-to-all-start.1 = ((f32[4,8,72,128]{3,2,1,0:T(8,128)}), f32[4,8,72,128]{3,2,1,0:T(8,128)}, u32[]{:S(2)}, u32[]{:S(2)}) async-start(f32[4,8,72,128]{3,2,1,0:T(8,128)} %filter.2), calls=%async_computation.1 | async-start | bytes 2359296 | tf_op jit(solution)/shard_map/all_to_all | solution.py:418
  152.2 7.6 %copy-start.16 = (f32[8,128]{1,0:T(8,128)S(1)}, f32[8,128]{1,0:T(8,128)}, u32[]{:S(2)}) copy-start(f32[8,128]{1,0:T(8,128)} %get-tuple-element.40) | copy-start | bytes 12292
  152.2 7.7 %copy-start.17 = (f32[8,128]{1,0:T(8,128)S(1)}, f32[8,128]{1,0:T(8,128)}, u32[]{:S(2)}) copy-start(f32[8,128]{1,0:T(8,128)} %get-tuple-element.41) | copy-start | bytes 12292
  152.2 7.7 %copy-start.18 = (f32[8,128]{1,0:T(8,128)S(1)}, f32[8,128]{1,0:T(8,128)}, u32[]{:S(2)}) copy-start(f32[8,128]{1,0:T(8,128)} %get-tuple-element.42) | copy-start | bytes 12292
  152.2 7.7 %copy-start.19 = (f32[8,128]{1,0:T(8,128)S(1)}, f32[8,128]{1,0:T(8,128)}, u32[]{:S(2)}) copy-start(f32[8,128]{1,0:T(8,128)} %get-tuple-element.43) | copy-start | bytes 12292
  152.2 7.7 %copy-start.20 = (f32[8,128]{1,0:T(8,128)S(1)}, f32[8,128]{1,0:T(8,128)}, u32[]{:S(2)}) copy-start(f32[8,128]{1,0:T(8,128)} %get-tuple-element.44) | copy-start | bytes 12292
  152.2 7.7 %copy-start.21 = (f32[8,128]{1,0:T(8,128)S(1)}, f32[8,128]{1,0:T(8,128)}, u32[]{:S(2)}) copy-start(f32[8,128]{1,0:T(8,128)} %get-tuple-element.45) | copy-start | bytes 12292
  152.2 7.7 %copy-start.22 = (f32[8,128]{1,0:T(8,128)S(1)}, f32[8,128]{1,0:T(8,128)}, u32[]{:S(2)}) copy-start(f32[8,128]{1,0:T(8,128)} %get-tuple-element.46) | copy-start | bytes 12292
  152.2 7.7 %copy-start.30 = (f32[128]{0:T(128)S(1)}, f32[128]{0:T(128)}, u32[]{:S(2)}) copy-start(f32[128]{0:T(128)} %get-tuple-element.54) | copy-start | bytes 1540
  152.2 7.7 %copy-start.31 = (f32[128]{0:T(128)S(1)}, f32[128]{0:T(128)}, u32[]{:S(2)}) copy-start(f32[128]{0:T(128)} %get-tuple-element.55) | copy-start | bytes 1540
  152.2 7.7 %copy-start.32 = (f32[128]{0:T(128)S(1)}, f32[128]{0:T(128)}, u32[]{:S(2)}) copy-start(f32[128]{0:T(128)} %get-tuple-element.56) | copy-start | bytes 1540
  152.2 7.7 %copy-start.33 = (f32[128]{0:T(128)S(1)}, f32[128]{0:T(128)}, u32[]{:S(2)}) copy-start(f32[128]{0:T(128)} %get-tuple-element.57) | copy-start | bytes 1540
  152.2 7.7 %copy-start.34 = (f32[128]{0:T(128)S(1)}, f32[128]{0:T(128)}, u32[]{:S(2)}) copy-start(f32[128]{0:T(128)} %get-tuple-element.58) | copy-start | bytes 1540
  152.2 7.7 %copy-start.35 = (f32[128]{0:T(128)S(1)}, f32[128]{0:T(128)}, u32[]{:S(2)}) copy-start(f32[128]{0:T(128)} %get-tuple-element.59) | copy-start | bytes 1540
  152.3 7.7 %copy-start.36 = (f32[128]{0:T(128)S(1)}, f32[128]{0:T(128)}, u32[]{:S(2)}) copy-start(f32[128]{0:T(128)} %get-tuple-element.60) | copy-start | bytes 1540
  152.3 10.6 %copy-start.37 = (u32[32]{0:T(128)S(1)}, u32[32]{0:T(128)}, u32[]{:S(2)}) copy-start(u32[32]{0:T(128)} %constant.253) | copy-start | bytes 388
  152.3 11.3 %copy-start.9 = (f32[8,128]{1,0:T(8,128)S(1)}, f32[8,128]{1,0:T(8,128)}, u32[]{:S(2)}) copy-start(f32[8,128]{1,0:T(8,128)} %get-tuple-element.39) | copy-start | bytes 12292
  152.3 11.3 %copy-start.10 = (f32[8,128]{1,0:T(8,128)S(1)}, f32[8,128]{1,0:T(8,128)}, u32[]{:S(2)}) copy-start(f32[8,128]{1,0:T(8,128)} %get-tuple-element.47) | copy-start | bytes 12292
  152.3 11.3 %copy-start.11 = (f32[8,128]{1,0:T(8,128)S(1)}, f32[8,128]{1,0:T(8,128)}, u32[]{:S(2)}) copy-start(f32[8,128]{1,0:T(8,128)} %get-tuple-element.48) | copy-start | bytes 12292
  152.3 11.3 %copy-start.12 = (f32[8,128]{1,0:T(8,128)S(1)}, f32[8,128]{1,0:T(8,128)}, u32[]{:S(2)}) copy-start(f32[8,128]{1,0:T(8,128)} %get-tuple-element.49) | copy-start | bytes 12292
  152.3 11.3 %copy-start.13 = (f32[8,128]{1,0:T(8,128)S(1)}, f32[8,128]{1,0:T(8,128)}, u32[]{:S(2)}) copy-start(f32[8,128]{1,0:T(8,128)} %get-tuple-element.50) | copy-start | bytes 12292
  152.3 11.3 %copy-start.14 = (f32[8,128]{1,0:T(8,128)S(1)}, f32[8,128]{1,0:T(8,128)}, u32[]{:S(2)}) copy-start(f32[8,128]{1,0:T(8,128)} %get-tuple-element.51) | copy-start | bytes 12292
  152.3 11.3 %copy-start.15 = (f32[8,128]{1,0:T(8,128)S(1)}, f32[8,128]{1,0:T(8,128)}, u32[]{:S(2)}) copy-start(f32[8,128]{1,0:T(8,128)} %get-tuple-element.52) | copy-start | bytes 12292
  152.3 11.3 %copy-start.23 = (f32[128]{0:T(128)S(1)}, f32[128]{0:T(128)}, u32[]{:S(2)}) copy-start(f32[128]{0:T(128)} %get-tuple-element.53) | copy-start | bytes 1540
  152.4 11.3 %copy-start.24 = (f32[128]{0:T(128)S(1)}, f32[128]{0:T(128)}, u32[]{:S(2)}) copy-start(f32[128]{0:T(128)} %get-tuple-element.61) | copy-start | bytes 1540
  152.4 11.3 %copy-start.25 = (f32[128]{0:T(128)S(1)}, f32[128]{0:T(128)}, u32[]{:S(2)}) copy-start(f32[128]{0:T(128)} %get-tuple-element.62) | copy-start | bytes 1540
  152.4 11.3 %copy-start.26 = (f32[128]{0:T(128)S(1)}, f32[128]{0:T(128)}, u32[]{:S(2)}) copy-start(f32[128]{0:T(128)} %get-tuple-element.63) | copy-start | bytes 1540
  152.4 11.3 %copy-start.27 = (f32[128]{0:T(128)S(1)}, f32[128]{0:T(128)}, u32[]{:S(2)}) copy-start(f32[128]{0:T(128)} %get-tuple-element.64) | copy-start | bytes 1540
  152.4 11.3 %copy-start.28 = (f32[128]{0:T(128)S(1)}, f32[128]{0:T(128)}, u32[]{:S(2)}) copy-start(f32[128]{0:T(128)} %get-tuple-element.65) | copy-start | bytes 1540
  152.4 11.3 %copy-start.29 = (f32[128]{0:T(128)S(1)}, f32[128]{0:T(128)}, u32[]{:S(2)}) copy-start(f32[128]{0:T(128)} %get-tuple-element.66) | copy-start | bytes 1540
  156.1 23.2 %all-to-all-start.3 = ((f32[4,9,72,128]{3,2,1,0:T(8,128)}), f32[4,9,72,128]{3,2,1,0:T(8,128)S(1)}, u32[]{:S(2)}, u32[]{:S(2)}) async-start(f32[4,9,72,128]{3,2,1,0:T(8,128)} %filter.3), calls=%async_computation.3 | async-start | bytes 2654208 | tf_op jit(solution)/shard_map/all_to_all | solution.py:418
  179.3 15.0 %copy-start.6 = (f32[8,2048]{1,0:T(8,128)S(1)}, f32[8,2048]{1,0:T(8,128)}, u32[]{:S(2)}) copy-start(f32[8,2048]{1,0:T(8,128)} %gather.2) | copy-start | bytes 196612
  179.3 1.1 copy-start.2

commit v2 on v1

--- a/solution.py
+++ b/solution.py
@@ -88,7 +88,11 @@
     return out
 
 
-def basis_kernel(mesh_size, z_width, slots_padded, where_ref, atoms, wx, vx, zq, zv, bwh, bwl, bvh, bvl):
+def basis_kernel(mesh_size, x_width, z_width, slots_padded, where_ref, blocks, wx, vx, zq, zv, bwh, bwl, bvh, bvl):
+    atoms = jnp.concatenate(
+        [blocks[d, b] for d in range(blocks.shape[0]) for b in range(blocks.shape[1])], axis=1
+    )
+
     def row(n):
         return atoms[n : n + 1, :]
 
@@ -99,7 +103,7 @@
         return lax.broadcasted_iota(jnp.int32, (count, lanes), 0).astype(jnp.float32)
 
     weights, slopes = spline(row(3))
-    offset = rows(wx.shape[0]) - row(0)
+    offset = rows(wx.shape[0]) - (row(0) - (where_ref[0] * x_width).astype(jnp.float32))
     wx[...] = place(offset, weights)
     vx[...] = place(offset, slopes)
     weights, slopes = spline(row(4))
@@ -156,20 +160,30 @@
             out[s] = lines[:, s * lanes : (s + 1) * lanes].reshape(out.shape[1:])
 
 
-def influence_kernel(scale, where_ref, own, across, edge, flip, same, back, out):
-    slot = pl.program_id(0)
-    own_pair = split(jnp.concatenate([own[0], own[0]], axis=0))
-    across_pair = split(across[0])
-    turned = dot(flip[...], across_pair[0]) + dot(flip[...], across_pair[1])
-    lines = lax.broadcasted_iota(jnp.int32, turned.shape, 0) % own.shape[1]
-    turned = split(jnp.where(lines == 0, edge[0], turned))
-    plain = dot(same[...], own_pair[0], 1) + dot(same[...], own_pair[1], 1)
+def influence_kernel(first, half, scale, where_ref, own, across, edge, flip, same, back, out):
+    count, _, lanes = out.shape
+    width = own.shape[1]
+    lowest = half - max(first + count - 1, 1)
+    plain = [own[first + g] for g in range(count) for _ in range(2)]
+    plain = split(jnp.concatenate(plain, axis=0))
+    pieces = []
+    for g in range(count):
+        at = half - max(first + g, 1)
+        pair = split(across[at - lowest])
+        turned = dot(flip[...], pair[0]) + dot(flip[...], pair[1])
+        lines = lax.broadcasted_iota(jnp.int32, turned.shape, 0) % width
+        pieces.append(jnp.where(lines == 0, edge[at], turned))
+    turned = split(jnp.concatenate(pieces, axis=0))
+    plain = dot(same[...], plain[0], 1) + dot(same[...], plain[1], 1)
     mirror = dot(back[...], turned[0], 1) + dot(back[...], turned[1], 1)
-    last = slot == pl.num_programs(0) - 1
-    upper = where_ref[2] == 1
-    keep_own = jnp.where(jnp.logical_and(last, jnp.logical_not(upper)), 0.0, scale)
-    keep_mirror = jnp.where(slot == 0, 0.0, keep_own)
-    out[0] = plain * keep_own + mirror * keep_mirror
+    for g in range(count):
+        keep = scale
+        if first + g == half:
+            keep = jnp.where(where_ref[2] == 1, scale, 0.0)
+        value = plain[:, g * lanes : (g + 1) * lanes]
+        if first + g > 0:
+            value = value + mirror[:, g * lanes : (g + 1) * lanes]
+        out[g] = value * keep
 
 
 def filter_kernel(lines, factor, th, tl, out):
@@ -207,7 +221,8 @@
             out[s, g, width:extent, :] = field[after : after + XROWS]
 
 
-def gather_kernel(first, count, slots_padded, lines, bh, bl, wx, vx, zq, zv, bwh, bwl, bvh, bvl, out, eh, el):
+def gather_kernel(first, count, slots_padded, lines, bh, bl, wx, vx, zq, zv, bwh, bwl, bvh, bvl, *rest):
+    *earlier, out, eh, el = rest
     sects, _, extent, lanes = lines.shape
     rows = count * extent
     mesh_size = bwh.shape[0]
@@ -233,10 +248,19 @@
             sums[0] = sums[0] + line * zq[at : at + 1, :]
             sums[1] = sums[1] + slope[low : low + extent] * zq[at : at + 1, :]
             sums[2] = sums[2] + line * zv[at : at + 1, :]
-    out[0:1, :] = -jnp.sum(sums[0] * vx[...], axis=0, keepdims=True)
-    out[1:2, :] = -jnp.sum(sums[1] * wx[...], axis=0, keepdims=True)
-    out[2:3, :] = -jnp.sum(sums[2] * wx[...], axis=0, keepdims=True)
-    out[3:, :] = jnp.zeros((out.shape[0] - 3, out.shape[1]), jnp.float32)
+    forces = [
+        -jnp.sum(total * shape[...], axis=0, keepdims=True)
+        for total, shape in zip(sums, (vx, wx, wx))
+    ]
+    result = jnp.concatenate(forces + [jnp.zeros_like(forces[0])], axis=0)
+    width = out.shape[2]
+    for d in range(out.shape[0]):
+        part = result[:, d * width : (d + 1) * width]
+        out[d] = part + earlier[0][d] if earlier else part
+
+
+def cost(micros):
+    return pl.CostEstimate(flops=int(micros * 1.0e9), transcendentals=0, bytes_accessed=int(micros * 1.0e5))
 
 
 def params():
@@ -303,22 +327,14 @@
         [cells.astype(jnp.float32), fracs, charges[None], jnp.zeros_like(charges)[None]], axis=0
     ).reshape(8, block_count, BLOCK)
     packed = jnp.transpose(packed, (1, 0, 2))
-    everyone = lax.all_gather(packed, ("sect", "dom"))
-    row = lax.dynamic_index_in_dim(
-        everyone.reshape(sects, doms, block_count, 8, BLOCK), sect, 0, keepdims=False
-    )
-    atoms = jnp.transpose(row, (2, 0, 1, 3)).reshape(8, total)
-    first_cell = jnp.zeros((8, 1), jnp.float32).at[0, 0].set(1.0) * (sect * x_width).astype(jnp.float32)
-    atoms = atoms - first_cell
-
-    opposite = []
+    row = lax.all_to_all(
+        jnp.broadcast_to(packed[None], (doms,) + packed.shape), "dom", 0, 0, tiled=True
+    )
+
     edges = []
     for s in range(sects):
         for d in range(doms):
-            opposite.append((s * doms + d, (sects - 1 - s) * doms + doms - 1 - d))
             edges.append((s * doms + d, ((sects - s) % sects) * doms + doms - 1 - d))
-    across = lax.ppermute(influence[half:], ("sect", "dom"), opposite)
-    edge = lax.ppermute(influence[half:, 0:1], ("sect", "dom"), edges)
     flip = np.zeros((2 * x_width, x_width), np.float32)
     for i in range(1, x_width):
         flip[i, x_width - i] = 1.0
@@ -326,23 +342,19 @@
     same = np.eye(mesh_size, dtype=np.float32)
     back = np.roll(same[::-1], 1, axis=0)
     flip, same, back = (jnp.asarray(m).astype(jnp.bfloat16) for m in (flip, same, back))
-    factor = pl.pallas_call(
-        lambda *refs: influence_kernel(float(mesh_size) ** -3, *refs),
-        grid=(slots,),
-        in_specs=[
-            SMEM,
-            pl.BlockSpec((1, x_width, mesh_size), lambda j: (j, 0, 0)),
-            pl.BlockSpec((1, x_width, mesh_size), lambda j: (jnp.minimum(half - j, half - 1), 0, 0)),
-            pl.BlockSpec((1, 1, mesh_size), lambda j: (jnp.minimum(half - j, half - 1), 0, 0)),
-            whole(flip),
-            whole(same),
-            whole(back),
-        ],
-        out_specs=pl.BlockSpec((1, mesh_size, lanes), lambda j: (j, 0, 0)),
-        out_shape=jax.ShapeDtypeStruct((slots, mesh_size, lanes), jnp.float32),
-        compiler_params=params(),
-        name="influence",
-    )(where_am_i, influence, across, edge, flip, same, back)
+    firsts = [slots * n // CHUNKS for n in range(CHUNKS + 1)]
+    counts = [b - a for a, b in zip(firsts, firsts[1:])]
+    planes = []
+    for first, count in zip(firsts, counts):
+        lowest = half - max(first + count - 1, 1)
+        highest = half - max(first, 1)
+        planes.append(influence[half + lowest : half + highest + 1])
+    sect_flip = [(s, sects - 1 - s) for s in range(sects)]
+    dom_flip = [(d, doms - 1 - d) for d in range(doms)]
+    planes = [
+        lax.ppermute(p, *(("dom", dom_flip) if n % 2 else ("sect", sect_flip)))
+        for n, p in enumerate(planes)
+    ]
 
     step = np.arange(mesh_size)
     angle = 2.0 * np.pi * (np.outer(step, step) % mesh_size) / mesh_size
@@ -368,17 +380,19 @@
         ((2 * slots_padded, total), f32),
     ] + [((mesh_size, total), bf16)] * 4
     wx, vx, zq, zv, bwh, bwl, bvh, bvl = pl.pallas_call(
-        lambda *refs: basis_kernel(mesh_size, z_width, slots_padded, *refs),
+        lambda *refs: basis_kernel(mesh_size, x_width, z_width, slots_padded, *refs),
         grid=grid,
-        in_specs=[SMEM, along_atoms(8, atom_step)],
+        in_specs=[
+            SMEM,
+            pl.BlockSpec((atom_step // atom_count, block_count, 8, BLOCK), lambda n: (n, 0, 0, 0)),
+        ],
         out_specs=[along_atoms(shape[0], atom_step) for shape, _ in shapes],
         out_shape=[jax.ShapeDtypeStruct(shape, dtype) for shape, dtype in shapes],
         compiler_params=params(),
+        cost_estimate=cost(6),
         name="basis",
-    )(where_am_i, atoms)
-
-    firsts = [slots * n // CHUNKS for n in range(CHUNKS + 1)]
-    counts = [b - a for a, b in zip(firsts, firsts[1:])]
+    )(where_am_i, row)
+
     sent = []
     for first, count in zip(firsts, counts):
         shape = (sects, count, extent, lanes)
@@ -396,33 +410,62 @@
             out_shape=jax.ShapeDtypeStruct(shape, f32),
             scratch_shapes=[pltpu.VMEM((2 * count * extent, mesh_size), f32)],
             compiler_params=params(),
+            cost_estimate=cost(9),
             name="spread",
         )(wx, zq, bwh, bwl, rh, rl, ih, il)
-        sent.append(lax.all_to_all(lines, "sect", split_axis=0, concat_axis=0, tiled=True))
+        sent.append(lines)
+    corner, beside, planes, sent[0] = lax.optimization_barrier(
+        (influence[half:, 0:1], row, planes, sent[0])
+    )
+    planes = [
+        lax.ppermute(p, *(("sect", sect_flip) if n % 2 else ("dom", dom_flip)))
+        for n, p in enumerate(planes)
+    ]
+    edge = lax.ppermute(corner, ("sect", "dom"), edges)
+    ahead = [(s, (s + 1) % sects) for s in range(sects)]
+    behind = [(b, a) for a, b in ahead]
+    near = [lax.ppermute(beside, "sect", ahead), lax.ppermute(beside, "sect", behind)]
+    sent = [lax.all_to_all(lines, "sect", split_axis=0, concat_axis=0, tiled=True) for lines in sent]
+    planes[0], edge, sent[0] = lax.optimization_barrier((planes[0], edge, sent[0]))
+    factors = [
+        pl.pallas_call(
+            lambda *refs, first=first: influence_kernel(first, half, float(mesh_size) ** -3, *refs),
+            in_specs=[SMEM] + [pl.BlockSpec(memory_space=pltpu.VMEM)] * 6,
+            out_specs=pl.BlockSpec(memory_space=pltpu.VMEM),
+            out_shape=jax.ShapeDtypeStruct((count, mesh_size, lanes), f32),
+            compiler_params=params(),
+            cost_estimate=cost(3.5),
+            name="influence",
+        )(where_am_i, influence, mirror, edge, flip, same, back)
+        for first, count, mirror in zip(firsts, counts, planes)
+    ]
     fields = []
-    for lines, first, count in zip(sent, firsts, counts):
+    for lines, factor in zip(sent, factors):
         field = pl.pallas_call(
             filter_kernel,
             grid=(1,),
             in_specs=[
                 whole(lines),
-                pl.BlockSpec((count, mesh_size, lanes), lambda n: (0, 0, 0)),
+                whole(factor),
                 whole(th),
                 whole(tl),
             ],
             out_specs=whole(lines),
             out_shape=jax.ShapeDtypeStruct(lines.shape, f32),
             compiler_params=params(),
+            cost_estimate=cost(5.5),
             name="filter",
-        )(lines, factor[first : first + count], th, tl)
-        fields.append(lax.all_to_all(field, "sect", split_axis=0, concat_axis=0, tiled=True))
+        )(lines, factor, th, tl)
+        fields.append(field)
+    near, row, packed, fields[0] = lax.optimization_barrier((near, row, packed, fields[0]))
+    fields = [lax.all_to_all(field, "sect", split_axis=0, concat_axis=0, tiled=True) for field in fields]
 
     listed = pair_blocks[0, 0]
     neighbour = listed // block_count
-    from_sect = (sect + neighbour // 3 - 1) % sects
+    near = jnp.stack([near[0], row, near[1]])
     from_dom = (dom + neighbour % 3 - 1) % doms
-    source = (from_sect * doms + from_dom) * block_count + listed % block_count
-    pool = everyone.reshape(sects * doms * block_count, 8 * BLOCK)
+    source = (neighbour // 3 * doms + from_dom) * block_count + listed % block_count
+    pool = near.reshape(3 * doms * block_count, 8 * BLOCK)
     pick = (source.reshape(-1, 1) == jnp.arange(pool.shape[0], dtype=jnp.int32)[None]).astype(f32)
     chosen = lax.dot_general(
         pick, pool, (((1,), (0,)), ((), ())), precision=lax.Precision.HIGHEST, preferred_element_type=f32
@@ -433,22 +476,24 @@
     )
     short_force = block_forces.reshape(3, atom_count)
 
-    partial = None
+    earlier = []
+    by_dom = pl.BlockSpec((atom_step // atom_count, 4, atom_count), lambda n: (n, 0, 0))
     for lines, first, count in zip(fields, firsts, counts):
-        forces = pl.pallas_call(
+        earlier = [pl.pallas_call(
             lambda *refs, first=first, count=count: gather_kernel(first, count, slots_padded, *refs),
             grid=grid,
             in_specs=[whole(lines), whole(bh), whole(bl)]
-            + [along_atoms(a.shape[0], atom_step) for a in (wx, vx, zq, zv, bwh, bwl, bvh, bvl)],
-            out_specs=along_atoms(8, atom_step),
-            out_shape=jax.ShapeDtypeStruct((8, total), f32),
+            + [along_atoms(a.shape[0], atom_step) for a in (wx, vx, zq, zv, bwh, bwl, bvh, bvl)]
+            + [by_dom] * len(earlier),
+            out_specs=by_dom,
+            out_shape=jax.ShapeDtypeStruct((doms, 4, atom_count), f32),
             scratch_shapes=[pltpu.VMEM((2 * count * extent, mesh_size), bf16)] * 2,
             compiler_params=params(),
+            cost_estimate=cost(13),
             name="gather",
-        )(lines, bh, bl, wx, vx, zq, zv, bwh, bwl, bvh, bvl)
-        partial = forces if partial is None else partial + forces
-    by_dom = jnp.transpose(partial[:3].reshape(3, doms, atom_count), (1, 0, 2))
-    mesh_force = lax.psum_scatter(by_dom, "dom", scatter_dimension=0, tiled=False)
+        )(lines, bh, bl, wx, vx, zq, zv, bwh, bwl, bvh, bvl, *earlier)]
+    shares = lax.all_to_all(earlier[0], "dom", 0, 0, tiled=True)
+    mesh_force = jnp.sum(shares, axis=0)[:3]
     return (short_force + mesh_force).reshape(3, 1, 1, atom_count)
 
 

time: 224 us -> 154 us (0.69)
  blocking collectives: 70.2 us -> 0 us
  starting transfers between devices: 16.3 us -> 41.8 us
  waiting for transfers between devices: 36.4 us -> 24.3 us
  Pallas kernels: 74.7 us -> 69.5 us
  other arithmetic: 11.6 us -> 8.09 us
    all_gather x1 -> x0, blocking collectives: 44.3 us -> none  [shards(): everyone = lax.all_gather(packed, ('sect', 'dom'))]
    unnamed x1 -> x0, blocking collectives: 25.9 us -> none
    all_to_all x2, waiting for transfers between devices: 27.8 us -> 6.42 us  [shards(): lax.all_to_all(lines, 'sect', split_axis=0, concat_axis=0, tiled=True)]
    ppermute x2 -> x7, starting transfers between devices: 0.07 us -> 14.7 us  [the longest x2 6.17 us: shards(): lax.ppermute(p, *(('dom', dom_flip) if n % 2 else ('sect', sect_flip)))]
    all_to_all x0 -> x2, starting transfers between devices: none -> 12.6 us  [the longest x1 6.33 us: shards(): lax.all_to_all(jnp.broadcast_to(packed[None], (doms,) + packed.shape), 'd...]
    all_to_all x2, waiting for transfers between devices: 3.65 us -> 9.77 us  [shards(): lax.all_to_all(field, 'sect', split_axis=0, concat_axis=0, tiled=True)]
    all_to_all x0 -> x2, waiting for transfers between devices: none -> 5.73 us  [the longest x1 5.73 us: shards(): shares = lax.all_to_all(earlier[0], 'dom', 0, 0, tiled=True)]
    pallas_call x4 -> x5, Pallas kernels: 30.1 us -> 24.8 us  [the longest x2 11.2 us: shards(): pl.pallas_call(filter_kernel, grid=(1,), in_specs=[whole(lines), whole(fa...]
  transfers between devices with their start and end apart: 6 -> 13, of which waited for: 3 -> 5; matrix products, arithmetic and copies ran while one was open for 7% -> 6% of each run, Pallas kernels for 21% -> 36%
where the time goes in v2:
time: 154 us; the launch traced here: 153 us
  Pallas kernels  69.5 us (45%)
  starting transfers between devices  41.8 us (27%)
  waiting for transfers between devices  24.3 us (16%)
  local copies, waits for them, and re-layouts  9.2 us (6%)
  other arithmetic  8.09 us (5%)
    pallas_call x2, Pallas kernels, shards(): pl.pallas_call(lambda *refs, first=first, count=count: gather_kernel(firs...  26.5 us
    pallas_call x2, Pallas kernels, shards(): pl.pallas_call(lambda *refs, first=first, count=count: spread_kernel(firs...  18.1 us
    pallas_call x2, Pallas kernels, shards(): pl.pallas_call(filter_kernel, grid=(1,), in_specs=[whole(lines), whole(fa...  11.2 us
    all_to_all x2, waiting for transfers between devices, shards(): lax.all_to_all(field, 'sect', split_axis=0, concat_axis=0, tiled=True)  9.77 us
    pallas_call x2, Pallas kernels, shards(): pl.pallas_call(lambda *refs, first=first: influence_kernel(first, half, f...  7.76 us
    all_to_all x2, starting transfers between devices, shards(): lax.all_to_all(field, 'sect', split_axis=0, concat_axis=0, tiled=True)  7.29 us
    all_to_all x2, starting transfers between devices, shards(): lax.all_to_all(lines, 'sect', split_axis=0, concat_axis=0, tiled=True)  7.25 us
    all_to_all x2, waiting for transfers between devices, shards(): lax.all_to_all(lines, 'sect', split_axis=0, concat_axis=0, tiled=True)  6.42 us
  transfers between devices with their start and end apart: 13, of which 5 were waited for; matrix products, arithmetic and copies ran while one was open for 6% of the time, Pallas kernels for 36%

profile of v2, /device:TPU:0, one launch (start us, length us, event | category | flops | bytes accessed | tf_op | source)
XLA Modules:
  0.0 153.3 jit_solution(756890524049511442)
XLA Ops:
  0.0 0.7 convert_element_type.50
  0.7 0.7 copy.21
  1.4 0.1 pad.17.clone
  1.5 0.7 maximum_bitcast_fusion
  2.2 0.6 broadcast_in_dim.2
  2.8 6.3 %all-to-all-start = ((f32[8,2,8,128]{3,2,1,0:T(8,128)}), f32[8,2,8,128]{3,2,1,0:T(8,128)S(1)}, u32[]{:S(2)}, u32[]{:S(2)}) async-start(f32[8,2,8,128]{3,2,1,0:T(8,128)} %broadcast_in_dim.2), calls=%async_computation | async-start | bytes 131072 | tf_op jit(solution)/shard_map/all_to_all | solution.py:330
  9.2 1.1 slice.158
  10.3 3.6 %collective-permute-start.1 = (f32[9,64,256]{2,1,0:T(8,128)S(1)}, f32[9,64,256]{2,1,0:T(8,128)S(1)}, u32[]{:S(2)}, u32[]{:S(2)}) collective-permute-start(f32[9,64,256]{2,1,0:T(8,128)S(1)} %slice.158), channel_id=1, source_target_pairs={{0,7},{1,6},{2,5},{3,4},{4,3},{5,2},{6,1},{7,0},{8,15},{9,14},{10,... | collective-permute-start | bytes 1769480 | tf_op jit(solution)/shard_map/ppermute | solution.py:355
  13.9 1.0 slice.157
  15.0 2.5 %collective-permute-start = (f32[7,64,256]{2,1,0:T(8,128)S(1)}, f32[7,64,256]{2,1,0:T(8,128)S(1)}, u32[]{:S(2)}, u32[]{:S(2)}) collective-permute-start(f32[7,64,256]{2,1,0:T(8,128)S(1)} %slice.157), channel_id=1, source_target_pairs={{0,24},{8,16},{16,8},{24,0},{1,25},{9,17},{17,9},{25,1},{2,26},{10... | collective-permute-start | bytes 1376264 | tf_op jit(solution)/shard_map/ppermute | solution.py:355
  17.5 0.9 slice.156
  18.4 0.6 pad_add_fusion.refs_0_
  19.1 0.0 all-to-all-done.refs_1_
  19.1 0.0 copy-start.4
  19.1 0.6 copy-done.4
  19.7 5.8 %basis.1 = (f32[72,2048]{1,0:T(8,128)}, f32[72,2048]{1,0:T(8,128)}, f32[48,2048]{1,0:T(8,128)}, f32[48,2048]{1,0:T(8,128)}, bf16[256,2048]{1,0:T(8,128)(2,1)}, /...) custom-call(s32[3]{0:T(128)} %pad_add_fusion.refs_0_, f32[8,2,8,128]{3,2,1,0:T(8,128)} %copy-done.4), custom_call_target="tpu_custom_call" | custom-call | flops 6000000000 | bytes 600000 | tf_op jit(solution)/shard_map/basis/pallas_call | solution.py:382
  25.5 8.7 %spread.2 = f32[4,8,72,128]{3,2,1,0:T(8,128)} custom-call(f32[72,2048]{1,0:T(8,128)} %get-tuple-element.26.refs_0_.refs_3_, f32[48,2048]{1,0:T(8,128)} %get-tuple-element.27.refs_1_.refs_5_, bf16[256,2048]{1,0:T(8,128)(2,1)} %get-tuple-element.28.refs_2_.refs_7_, bf16[256,2048]{1,0:T(8,128)(2,1)} %get-tuple-element.29.refs_3_.refs_8_, ...), custom_call_target="tpu_custom_call" | custom-call | flops 8999999488 | bytes 900000 | tf_op jit(solution)/shard_map/spread/pallas_call | solution.py:399
  34.2 0.0 copy-start.6
  34.2 0.0 collective-permute-done
  34.3 0.0 copy-start.7
  34.3 0.0 collective-permute-done.1
  34.3 0.8 copy-done.7
  35.1 3.5 %all-to-all-start.1 = ((f32[4,8,72,128]{3,2,1,0:T(8,128)}), f32[4,8,72,128]{3,2,1,0:T(8,128)S(1)}, u32[]{:S(2)}, u32[]{:S(2)}) async-start(f32[4,8,72,128]{3,2,1,0:T(8,128)} %spread.2), calls=%async_computation.1 | async-start | bytes 2359296 | tf_op jit(solution)/shard_map/all_to_all | solution.py:428
  38.6 0.0 copy-done.6
  38.7 0.0 copy-start.5
  38.7 0.1 collective-permute-start.4
  38.7 3.5 %collective-permute-start.5 = (f32[16,1,256]{2,1,0:T(1,128)S(1)}, f32[16,1,256]{2,1,0:T(1,128)S(1)}, u32[]{:S(2)}, u32[]{:S(2)}) collective-permute-start(f32[16,1,256]{2,1,0:T(1,128)S(1)} %slice.156), channel_id=1, source_target_pairs={{0,7},{1,6},{2,5},{3,4},{4,3},{5,2},{6,1},{7,0},{8,31},{9,30},{10,... | collective-permute-start | bytes 49160 | tf_op jit(solution)/shard_map/ppermute | solution.py:424
  42.3 9.4 %spread.3 = f32[4,9,72,128]{3,2,1,0:T(8,128)} custom-call(f32[72,2048]{1,0:T(8,128)} %get-tuple-element.26.refs_0_.refs_3_, f32[48,2048]{1,0:T(8,128)} %get-tuple-element.27.refs_1_.refs_5_, bf16[256,2048]{1,0:T(8,128)(2,1)} %get-tuple-element.28.refs_2_.refs_7_, bf16[256,2048]{1,0:T(8,128)(2,1)} %get-tuple-element.29.refs_3_.refs_8_, ...), custom_call_target="tpu_custom_call" | custom-call | flops 8999999488 | bytes 900000 | tf_op jit(solution)/shard_map/spread/pallas_call | solution.py:399
  51.7 0.0 copy-done.5
  51.7 2.9 %collective-permute-start.2 = (f32[8,2,8,128]{3,2,1,0:T(8,128)S(1)}, f32[8,2,8,128]{3,2,1,0:T(8,128)S(1)}, u32[]{:S(2)}, u32[]{:S(2)}) collective-permute-start(f32[8,2,8,128]{3,2,1,0:T(8,128)S(1)} %copy-done.5), channel_id=1, source_target_pairs={{0,8},{8,16},{16,24},{24,0},{1,9},{9,17},{17,25},{25,1},{2,10},{10... | collective-permute-start | bytes 196616 | tf_op jit(solution)/shard_map/ppermute | solution.py:427
  54.6 0.1 collective-permute-start.3
  54.6 2.0 %collective-permute-start.6 = (f32[9,64,256]{2,1,0:T(8,128)S(1)}, f32[9,64,256]{2,1,0:T(8,128)}, u32[]{:S(2)}, u32[]{:S(2)}) collective-permute-start(f32[9,64,256]{2,1,0:T(8,128)S(1)} %collective-permute-done.1), channel_id=1, source_target_pairs={{0,24},{8,16},{16,8},{24,0},{1,25},{9,17},{17,9},{25,1},{2,26},{10... | collective-permute-start | bytes 1769480 | tf_op jit(solution)/shard_map/ppermute | solution.py:421
  56.6 0.0 all-to-all-done.1.lines
  56.6 0.0 copy-start.2
  56.6 3.7 %all-to-all-start.2 = ((f32[4,9,72,128]{3,2,1,0:T(8,128)}), f32[4,9,72,128]{3,2,1,0:T(8,128)S(1)}, u32[]{:S(2)}, u32[]{:S(2)}) async-start(f32[4,9,72,128]{3,2,1,0:T(8,128)} %spread.3), calls=%async_computation.2 | async-start | bytes 2654208 | tf_op jit(solution)/shard_map/all_to_all | solution.py:428
  60.3 0.0 collective-permute-done.5.refs_3_
  60.3 0.0 copy-start.8
  60.3 0.0 collective-permute-done.4.refs_2_
  60.3 0.6 copy-done.8
  60.9 3.8 %influence.2.factor = f32[8,256,128]{2,1,0:T(8,128)} custom-call(s32[3]{0:T(128)} %pad_add_fusion.refs_0_, f32[32,64,256]{2,1,0:T(8,128)} %refs_1_.3, f32[7,64,256]{2,1,0:T(8,128)} %collective-permute-done.4.refs_2_, f32[16,1,256]{2,1,0:T(1,128)} %copy-done.8, bf16[128,64]{1,0:T(8,128)(2,1)} %constant.188.refs_4_, bf16[256,256]{1,0:T(8,128)(2,1)} %constant.189.refs_5_, ...), custom_call_target="tpu_custom_call" | custom-call | flops 3500000000 | bytes 350000 | tf_op jit(solution)/shard_map/influence/pallas_call | solution.py:431
  64.7 0.0 copy-done.2
  64.7 4.9 %filter.2 = f32[4,8,72,128]{3,2,1,0:T(8,128)} custom-call(f32[4,8,72,128]{3,2,1,0:T(8,128)} %copy-done.2, f32[8,256,128]{2,1,0:T(8,128)} %influence.2.factor, bf16[512,256]{1,0:T(8,128)(2,1)} %constant.191.th, bf16[512,256]{1,0:T(8,128)(2,1)} %constant.194.tl), custom_call_target="tpu_custom_call" | custom-call | flops 5500000256 | bytes 550000 | tf_op jit(solution)/shard_map/filter/pallas_call | solution.py:444
  69.6 0.0 collective-permute-done.2
  69.6 0.0 collective-permute-done.3
  69.7 0.2 convolution_bitcast_fusion
  69.9 2.4 %collective-permute-done.6.refs_2_ = f32[9,64,256]{2,1,0:T(8,128)} collective-permute-done((f32[9,64,256]{2,1,0:T(8,128)S(1)}, f32[9,64,256]{2,1,0:T(8,128)}, u32[]{:S(2)}, u32[]{:S(2)}) %collective-permute-start.6) | collective-permute-done | bytes 589856 | tf_op jit(solution)/shard_map/ppermute | solution.py:421
  72.3 4.0 %influence.3.factor = f32[9,256,128]{2,1,0:T(8,128)} custom-call(s32[3]{0:T(128)} %pad_add_fusion.refs_0_, f32[32,64,256]{2,1,0:T(8,128)} %refs_1_.3, f32[9,64,256]{2,1,0:T(8,128)} %collective-permute-done.6.refs_2_, f32[16,1,256]{2,1,0:T(1,128)} %copy-done.8, bf16[128,64]{1,0:T(8,128)(2,1)} %constant.188.refs_4_, bf16[256,256]{1,0:T(8,128)(2,1)} %constant.189.refs_5_, ...), custom_call_target="tpu_custom_call" | custom-call | flops 3500000000 | bytes 350000 | tf_op jit(solution)/shard_map/influence/pallas_call | solution.py:431
  76.3 3.0 %multiply_reduce_fusion.2 = (f32[128]{0:T(128)S(1)}, f32[128]{0:T(128)S(1)}, f32[128]{0:T(128)S(1)}) fusion(f32[8,128]{1,0:T(8,128)S(1)} %get-tuple-element.58, f32[128]{0:T(128)S(1)} %get-tuple-element.72, f32[8,128]{1,0:T(8,128)S(1)} %get-tuple-element.59, f32[128]{0:T(128)S(1)} %get-tuple-element.73, f32[8,128]{1,0:T(8,128)S(1)} %get-tuple-element.54, ...), kind=kLoop, calls=%fused_computation.35 | loop fusion | flops 14941824 | bytes 33792 | tf_op jit(solution)/shard_map/reduce_sum | solution.py:306
  79.3 6.4 %all-to-all-done.2.lines = f32[4,9,72,128]{3,2,1,0:T(8,128)S(1)} async-done(((f32[4,9,72,128]{3,2,1,0:T(8,128)}), f32[4,9,72,128]{3,2,1,0:T(8,128)S(1)}, u32[]{:S(2)}, u32[]{:S(2)}) %all-to-all-start.2) | async-done | bytes 1327136 | tf_op jit(solution)/shard_map/all_to_all | solution.py:428
  85.7 0.0 copy-start
  85.7 3.7 %all-to-all-start.4 = ((f32[4,8,72,128]{3,2,1,0:T(8,128)}), f32[4,8,72,128]{3,2,1,0:T(8,128)S(1)}, u32[]{:S(2)}, u32[]{:S(2)}) async-start(f32[4,8,72,128]{3,2,1,0:T(8,128)} %filter.2), calls=%async_computation.4 | async-start | bytes 2359296 | tf_op jit(solution)/shard_map/all_to_all | solution.py:461
  89.4 0.0 copy-done
  89.4 6.3 %filter.3 = f32[4,9,72,128]{3,2,1,0:T(8,128)} custom-call(f32[4,9,72,128]{3,2,1,0:T(8,128)} %copy-done, f32[9,256,128]{2,1,0:T(8,128)} %influence.3.factor, bf16[512,256]{1,0:T(8,128)(2,1)} %constant.191.th, bf16[512,256]{1,0:T(8,128)(2,1)} %constant.194.tl), custom_call_target="tpu_custom_call" | custom-call | flops 5500000256 | bytes 550000 | tf_op jit(solution)/shard_map/filter/pallas_call | solution.py:444
  95.8 3.0 %multiply_reduce_fusion.5 = (f32[128]{0:T(128)S(1)}, f32[128]{0:T(128)S(1)}, f32[128]{0:T(128)S(1)}) fusion(f32[8,128]{1,0:T(8,128)S(1)} %get-tuple-element.65, f32[128]{0:T(128)S(1)} %get-tuple-element.79, f32[8,128]{1,0:T(8,128)S(1)} %get-tuple-element.66, f32[128]{0:T(128)S(1)} %get-tuple-element.80, f32[8,128]{1,0:T(8,128)S(1)} %get-tuple-element.61, ...), kind=kLoop, calls=%fused_computation.63 | loop fusion | flops 14941824 | bytes 33792 | tf_op jit(solution)/shard_map/reduce_sum | solution.py:306
  98.7 5.8 %all-to-all-done.4.refs_0_ = f32[4,8,72,128]{3,2,1,0:T(8,128)S(1)} async-done(((f32[4,8,72,128]{3,2,1,0:T(8,128)}), f32[4,8,72,128]{3,2,1,0:T(8,128)S(1)}, u32[]{:S(2)}, u32[]{:S(2)}) %all-to-all-start.4) | async-done | bytes 1179680 | tf_op jit(solution)/shard_map/all_to_all | solution.py:461
  104.5 1.0 copy-done.3
  105.6 3.5 %all-to-all-start.3 = ((f32[4,9,72,128]{3,2,1,0:T(8,128)}), f32[4,9,72,128]{3,2,1,0:T(8,128)S(1)}, u32[]{:S(2)}, u32[]{:S(2)}) async-start(f32[4,9,72,128]{3,2,1,0:T(8,128)} %filter.3), calls=%async_computation.3 | async-start | bytes 2654208 | tf_op jit(solution)/shard_map/all_to_all | solution.py:461
  109.1 12.6 %gather.2.refs_11_ = f32[8,4,256]{2,1,0:T(4,128)} custom-call(f32[4,8,72,128]{3,2,1,0:T(8,128)} %copy-done.3, bf16[512,512]{1,0:T(8,128)(2,1)} %constant.195.refs_1_, bf16[512,512]{1,0:T(8,128)(2,1)} %constant.198.refs_2_, f32[72,2048]{1,0:T(8,128)} %get-tuple-element.26.refs_0_.refs_3_, f32[72,2048]{1,0:T(8,128)} %get-tuple-element.42.refs_4_, ...), custom_call_target="tpu_custom_call" | custom-call | flops 12999999488 | bytes 1300000 | tf_op jit(solution)/shard_map/gather/pallas_call | solution.py:482
  121.7 3.9 %all-to-all-done.3.refs_0_ = f32[4,9,72,128]{3,2,1,0:T(8,128)S(1)} async-done(((f32[4,9,72,128]{3,2,1,0:T(8,128)}), f32[4,9,72,128]{3,2,1,0:T(8,128)S(1)}, u32[]{:S(2)}, u32[]{:S(2)}) %all-to-all-start.3) | async-done | bytes 1327136 | tf_op jit(solution)/shard_map/all_to_all | solution.py:461
  125.7 1.1 copy-done.1
  126.8 13.9 %gather.3 = f32[8,4,256]{2,1,0:T(4,128)} custom-call(f32[4,9,72,128]{3,2,1,0:T(8,128)} %copy-done.1, bf16[512,512]{1,0:T(8,128)(2,1)} %constant.195.refs_1_, bf16[512,512]{1,0:T(8,128)(2,1)} %constant.198.refs_2_, f32[72,2048]{1,0:T(8,128)} %get-tuple-element.26.refs_0_.refs_3_, f32[72,2048]{1,0:T(8,128)} %get-tuple-element.42.refs_4_, ...), custom_call_target="tpu_custom_call" | custom-call | flops 12999999488 | bytes 1300000 | tf_op jit(solution)/shard_map/gather/pallas_call | solution.py:482
  140.7 6.3 %all-to-all-start.5 = ((f32[8,4,256]{2,1,0:T(4,128)}), f32[8,4,256]{2,1,0:T(4,128)S(1)}, u32[]{:S(2)}, u32[]{:S(2)}) async-start(f32[8,4,256]{2,1,0:T(4,128)} %gather.3), calls=%async_computation.5 | async-start | bytes 65536 | tf_op jit(solution)/shard_map/all_to_all | solution.py:495
  147.0 5.7 %all-to-all-done.5 = f32[8,4,256]{2,1,0:T(4,128)S(1)} async-done(((f32[8,4,256]{2,1,0:T(4,128)}), f32[8,4,256]{2,1,0:T(4,128)S(1)}, u32[]{:S(2)}, u32[]{:S(2)}) %all-to-all-start.5) | async-done | bytes 32800 | tf_op jit(solution)/shard_map/all_to_all | solution.py:495
  152.8 0.6 reshape.205
  (10 shorter events, 0.1 us)
Async XLA Ops:
  2.8 16.2 %all-to-all-start = ((f32[8,2,8,128]{3,2,1,0:T(8,128)}), f32[8,2,8,128]{3,2,1,0:T(8,128)S(1)}, u32[]{:S(2)}, u32[]{:S(2)}) async-start(f32[8,2,8,128]{3,2,1,0:T(8,128)} %broadcast_in_dim.2), calls=%async_computation | async-start | bytes 131072 | tf_op jit(solution)/shard_map/all_to_all | solution.py:330
  10.3 24.0 %collective-permute-start.1 = (f32[9,64,256]{2,1,0:T(8,128)S(1)}, f32[9,64,256]{2,1,0:T(8,128)S(1)}, u32[]{:S(2)}, u32[]{:S(2)}) collective-permute-start(f32[9,64,256]{2,1,0:T(8,128)S(1)} %slice.158), channel_id=1, source_target_pairs={{0,7},{1,6},{2,5},{3,4},{4,3},{5,2},{6,1},{7,0},{8,15},{9,14},{10,... | collective-permute-start | bytes 1769480 | tf_op jit(solution)/shard_map/ppermute | solution.py:355
  15.0 19.3 %collective-permute-start = (f32[7,64,256]{2,1,0:T(8,128)S(1)}, f32[7,64,256]{2,1,0:T(8,128)S(1)}, u32[]{:S(2)}, u32[]{:S(2)}) collective-permute-start(f32[7,64,256]{2,1,0:T(8,128)S(1)} %slice.157), channel_id=1, source_target_pairs={{0,24},{8,16},{16,8},{24,0},{1,25},{9,17},{17,9},{25,1},{2,26},{10... | collective-permute-start | bytes 1376264 | tf_op jit(solution)/shard_map/ppermute | solution.py:355
  19.1 0.6 copy-start.4
  34.2 4.4 %copy-start.6 = (s32[1,1,2,8]{3,2,1,0:T(2,128)S(1)}, s32[1,1,2,8]{3,2,1,0:T(2,128)}, u32[]{:S(2)}) copy-start(s32[1,1,2,8]{3,2,1,0:T(2,128)} %param.15) | copy-start | bytes 196
  34.3 0.8 copy-start.7
  35.1 21.5 %all-to-all-start.1 = ((f32[4,8,72,128]{3,2,1,0:T(8,128)}), f32[4,8,72,128]{3,2,1,0:T(8,128)S(1)}, u32[]{:S(2)}, u32[]{:S(2)}) async-start(f32[4,8,72,128]{3,2,1,0:T(8,128)} %spread.2), calls=%async_computation.1 | async-start | bytes 2359296 | tf_op jit(solution)/shard_map/all_to_all | solution.py:428
  38.7 13.0 %copy-start.5 = (f32[8,2,8,128]{3,2,1,0:T(8,128)S(1)}, f32[8,2,8,128]{3,2,1,0:T(8,128)}, u32[]{:S(2)}) copy-start(f32[8,2,8,128]{3,2,1,0:T(8,128)} %copy-done.4) | copy-start | bytes 196612
  38.7 21.7 %collective-permute-start.4 = (f32[7,64,256]{2,1,0:T(8,128)}, f32[7,64,256]{2,1,0:T(8,128)}, u32[]{:S(2)}, u32[]{:S(2)}) collective-permute-start(f32[7,64,256]{2,1,0:T(8,128)} %copy-done.7), channel_id=1, source_target_pairs={{0,7},{1,6},{2,5},{3,4},{4,3},{5,2},{6,1},{7,0},{8,15},{9,14},{10,... | collective-permute-start | bytes 1376264 | tf_op jit(solution)/shard_map/ppermute | solution.py:421
  38.7 21.6 %collective-permute-start.5 = (f32[16,1,256]{2,1,0:T(1,128)S(1)}, f32[16,1,256]{2,1,0:T(1,128)S(1)}, u32[]{:S(2)}, u32[]{:S(2)}) collective-permute-start(f32[16,1,256]{2,1,0:T(1,128)S(1)} %slice.156), channel_id=1, source_target_pairs={{0,7},{1,6},{2,5},{3,4},{4,3},{5,2},{6,1},{7,0},{8,31},{9,30},{10,... | collective-permute-start | bytes 49160 | tf_op jit(solution)/shard_map/ppermute | solution.py:424
  51.7 17.9 %collective-permute-start.2 = (f32[8,2,8,128]{3,2,1,0:T(8,128)S(1)}, f32[8,2,8,128]{3,2,1,0:T(8,128)S(1)}, u32[]{:S(2)}, u32[]{:S(2)}) collective-permute-start(f32[8,2,8,128]{3,2,1,0:T(8,128)S(1)} %copy-done.5), channel_id=1, source_target_pairs={{0,8},{8,16},{16,24},{24,0},{1,9},{9,17},{17,25},{25,1},{2,10},{10... | collective-permute-start | bytes 196616 | tf_op jit(solution)/shard_map/ppermute | solution.py:427
  54.6 15.1 %collective-permute-start.3 = (f32[8,2,8,128]{3,2,1,0:T(8,128)S(1)}, f32[8,2,8,128]{3,2,1,0:T(8,128)S(1)}, u32[]{:S(2)}, u32[]{:S(2)}) collective-permute-start(f32[8,2,8,128]{3,2,1,0:T(8,128)S(1)} %copy-done.5), channel_id=1, source_target_pairs={{8,0},{16,8},{24,16},{0,24},{9,1},{17,9},{25,17},{1,25},{10,2},{18... | collective-permute-start | bytes 196616 | tf_op jit(solution)/shard_map/ppermute | solution.py:427
  54.6 17.7 %collective-permute-start.6 = (f32[9,64,256]{2,1,0:T(8,128)S(1)}, f32[9,64,256]{2,1,0:T(8,128)}, u32[]{:S(2)}, u32[]{:S(2)}) collective-permute-start(f32[9,64,256]{2,1,0:T(8,128)S(1)} %collective-permute-done.1), channel_id=1, source_target_pairs={{0,24},{8,16},{16,8},{24,0},{1,25},{9,17},{17,9},{25,1},{2,26},{10... | collective-permute-start | bytes 1769480 | tf_op jit(solution)/shard_map/ppermute | solution.py:421
  56.6 8.1 %copy-start.2 = (f32[4,8,72,128]{3,2,1,0:T(8,128)}, f32[4,8,72,128]{3,2,1,0:T(8,128)S(1)}, u32[]{:S(2)}) copy-start(f32[4,8,72,128]{3,2,1,0:T(8,128)S(1)} %all-to-all-done.1.lines) | copy-start | bytes 3538948
  56.6 29.1 %all-to-all-start.2 = ((f32[4,9,72,128]{3,2,1,0:T(8,128)}), f32[4,9,72,128]{3,2,1,0:T(8,128)S(1)}, u32[]{:S(2)}, u32[]{:S(2)}) async-start(f32[4,9,72,128]{3,2,1,0:T(8,128)} %spread.3), calls=%async_computation.2 | async-start | bytes 2654208 | tf_op jit(solution)/shard_map/all_to_all | solution.py:428
  60.3 0.6 copy-start.8
  85.7 3.8 %copy-start = (f32[4,9,72,128]{3,2,1,0:T(8,128)}, f32[4,9,72,128]{3,2,1,0:T(8,128)S(1)}, u32[]{:S(2)}) copy-start(f32[4,9,72,128]{3,2,1,0:T(8,128)S(1)} %all-to-all-done.2.lines) | copy-start | bytes 3981316
  85.7 18.9 %all-to-all-start.4 = ((f32[4,8,72,128]{3,2,1,0:T(8,128)}), f32[4,8,72,128]{3,2,1,0:T(8,128)S(1)}, u32[]{:S(2)}, u32[]{:S(2)}) async-start(f32[4,8,72,128]{3,2,1,0:T(8,128)} %filter.2), calls=%async_computation.4 | async-start | bytes 2359296 | tf_op jit(solution)/shard_map/all_to_all | solution.py:461
  104.5 1.1 copy-start.3
  105.6 20.1 %all-to-all-start.3 = ((f32[4,9,72,128]{3,2,1,0:T(8,128)}), f32[4,9,72,128]{3,2,1,0:T(8,128)S(1)}, u32[]{:S(2)}, u32[]{:S(2)}) async-start(f32[4,9,72,128]{3,2,1,0:T(8,128)} %filter.3), calls=%async_computation.3 | async-start | bytes 2654208 | tf_op jit(solution)/shard_map/all_to_all | solution.py:461
  125.7 1.1 copy-start.1
  140.7 12.1 %all-to-all-start.5 = ((f32[8,4,256]{2,1,0:T(4,128)}), f32[8,4,256]{2,1,0:T(4,128)S(1)}, u32[]{:S(2)}, u32[]{:S(2)}) async-start(f32[8,4,256]{2,1,0:T(4,128)} %gather.3), calls=%async_computation.5 | async-start | bytes 65536 | tf_op jit(solution)/shard_map/all_to_all | solution.py:495

commit v3 on v2

--- a/solution.py
+++ b/solution.py
@@ -12,6 +12,8 @@
 XROWS = 8
 CHUNKS = 2
 VMEM = 56 * 1024 * 1024
+SPREAD_GROUP = 5
+GATHER_GROUP = 5
 
 ewald_beta = 0.1
 soft_square = 9.0
@@ -37,11 +39,9 @@
 
 
 def dot3(left, right, right_dim=0):
-    return (
-        dot(left[0], right[0], right_dim)
-        + dot(left[0], right[1], right_dim)
-        + dot(left[1], right[0], right_dim)
-    )
+    left = jnp.concatenate([left[0], left[0], left[1]], axis=1)
+    right = jnp.concatenate([right[0], right[1], right[0]], axis=right_dim)
+    return dot(left, right, right_dim)
 
 
 def spline(frac):
@@ -82,13 +82,22 @@
 
 
 def place(offset, values):
-    out = jnp.zeros_like(offset)
+    out = jnp.zeros(offset.shape, jnp.float32)
     for k in range(4):
-        out = jnp.where(offset == float(k), values[k], out)
+        out = jnp.where(offset == k, values[k], out)
     return out
 
 
-def basis_kernel(mesh_size, x_width, z_width, slots_padded, where_ref, blocks, wx, vx, zq, zv, bwh, bwl, bvh, bvl):
+def pack_kernel(cells, fracs, charges, out):
+    rows = [cells[n, 0].astype(jnp.float32) for n in range(3)] + [fracs[n, 0] for n in range(3)]
+    atoms = jnp.concatenate(rows + [charges[0], jnp.zeros_like(charges[0])], axis=0)
+    for b in range(out.shape[1]):
+        part = atoms[:, b * BLOCK : (b + 1) * BLOCK]
+        for d in range(out.shape[0]):
+            out[d, b] = part
+
+
+def basis_kernel(which, mesh_size, x_width, z_width, slots_padded, where_ref, blocks, along_x, along_z, high_y, low_y):
     atoms = jnp.concatenate(
         [blocks[d, b] for d in range(blocks.shape[0]) for b in range(blocks.shape[1])], axis=1
     )
@@ -102,58 +111,60 @@
     def rows(count):
         return lax.broadcasted_iota(jnp.int32, (count, lanes), 0).astype(jnp.float32)
 
-    weights, slopes = spline(row(3))
-    offset = rows(wx.shape[0]) - (row(0) - (where_ref[0] * x_width).astype(jnp.float32))
-    wx[...] = place(offset, weights)
-    vx[...] = place(offset, slopes)
-    weights, slopes = spline(row(4))
-    offset = rows(mesh_size) - row(1)
-    offset = jnp.where(offset < 0.0, offset + mesh_size, offset)
-    high, low = split(place(offset, weights))
-    bwh[...] = high
-    bwl[...] = low
-    high, low = split(place(offset, slopes))
-    bvh[...] = high
-    bvl[...] = low
-    weights, slopes = spline(row(5))
+    values = spline(row(3))[which]
+    offset = rows(along_x.shape[0]) - (row(0) - (where_ref[0] * x_width).astype(jnp.float32))
+    along_x[...] = place(offset, values)
+    values = spline(row(4))[which]
+    offset = lax.broadcasted_iota(jnp.int32, (mesh_size, lanes), 0) - row(1).astype(jnp.int32)
+    high, low = split(place(offset & (mesh_size - 1), values))
+    high_y[...] = high
+    low_y[...] = low
+    values = spline(row(5))[which]
     wave = rows(slots_padded) + (where_ref[1] * z_width).astype(jnp.float32)
-    parts = [jnp.zeros_like(wave) for _ in range(4)]
+    real = jnp.zeros_like(wave)
+    imag = jnp.zeros_like(wave)
+    cos, sin = turn(wave * row(2), mesh_size)
+    by_cos, by_sin = turn(wave[:, 0:128], mesh_size)
+    by_cos = jnp.concatenate([by_cos] * (lanes // 128), axis=1)
+    by_sin = jnp.concatenate([by_sin] * (lanes // 128), axis=1)
     for k in range(4):
-        cos, sin = turn(wave * (row(2) + float(k)), mesh_size)
-        parts[0] = parts[0] + (charge * weights[k]) * cos
-        parts[1] = parts[1] - (charge * weights[k]) * sin
-        parts[2] = parts[2] + (charge * slopes[k]) * cos
-        parts[3] = parts[3] - (charge * slopes[k]) * sin
-    zq[0:slots_padded, :] = parts[0]
-    zq[slots_padded:, :] = parts[1]
-    zv[0:slots_padded, :] = parts[2]
-    zv[slots_padded:, :] = parts[3]
-
-
-def spread_kernel(first, count, slots_padded, wx, zq, bwh, bwl, rh, rl, ih, il, out, acc):
+        if k:
+            cos, sin = cos * by_cos - sin * by_sin, sin * by_cos + cos * by_sin
+        real = real + (charge * values[k]) * cos
+        imag = imag - (charge * values[k]) * sin
+    along_z[0:slots_padded, :] = real
+    along_z[slots_padded:, :] = imag
+
+
+def groups(count, size):
+    return [(low, min(low + size, count)) for low in range(0, count, size)]
+
+
+def spread_kernel(first, count, slots_padded, wx, zq, bwh, bwl, rh, rl, ih, il, out, *sums):
     step = pl.program_id(0)
-    rows = count * wx.shape[0]
     wide = wx[...]
-    pieces = []
-    for c in range(2):
-        for g in range(count):
-            at = c * slots_padded + first + g
-            pieces.append(wide * zq[at : at + 1, :])
-    left = split(jnp.concatenate(pieces, axis=0))
-    part = dot3(left, (bwh[...], bwl[...]), 1)
+    extent = wide.shape[0]
+    right = (bwh[...], bwl[...])
 
     @pl.when(step == 0)
     def _():
-        acc[...] = part
-
-    @pl.when(step != 0)
-    def _():
-        acc[...] += part
+        for acc in sums:
+            acc[...] = jnp.zeros_like(acc)
+
+    for low, high in groups(count, SPREAD_GROUP):
+        pieces = []
+        for c in range(2):
+            for g in range(low, high):
+                at = c * slots_padded + first + g
+                pieces.append(wide * zq[at : at + 1, :])
+        part = dot3(split(jnp.concatenate(pieces, axis=0)), right, 1)
+        rows = (high - low) * extent
+        for c in range(2):
+            sums[c][low * extent : high * extent, :] += part[c * rows : (c + 1) * rows]
 
     @pl.when(step == pl.num_programs(0) - 1)
     def _():
-        real = split(acc[0:rows, :])
-        imag = split(acc[rows:, :])
+        real, imag = (split(acc[...]) for acc in sums)
         lines = dot3(real, (rh[...], rl[...])) + dot3(imag, (ih[...], il[...]))
         lanes = out.shape[3]
         for s in range(out.shape[0]):
@@ -231,23 +242,31 @@
     def _():
         joined = jnp.concatenate([lines[s].reshape(rows, lanes) for s in range(sects)], axis=1)
         field = dot3(split(joined), (bh[...], bl[...]))
-        field = jnp.concatenate([field[:, 0:mesh_size], field[:, mesh_size:]], axis=0)
-        high, low = split(field)
+        pieces = []
+        for g in range(count):
+            for c in range(2):
+                line = field[g * extent : (g + 1) * extent, c * mesh_size : (c + 1) * mesh_size]
+                pieces.append(line)
+        high, low = split(jnp.concatenate(pieces, axis=0))
         eh[...] = high
         el[...] = low
 
-    left = (eh[...], el[...])
-    along = dot3(left, (bwh[...], bwl[...]))
-    slope = dot3(left, (bvh[...], bvl[...]))
+    weights = (bwh[...], bwl[...])
+    slopes = (bvh[...], bvl[...])
     sums = [jnp.zeros(wx.shape, jnp.float32) for _ in range(3)]
-    for c in range(2):
-        for g in range(count):
-            at = c * slots_padded + first + g
-            low = (c * count + g) * extent
-            line = along[low : low + extent]
-            sums[0] = sums[0] + line * zq[at : at + 1, :]
-            sums[1] = sums[1] + slope[low : low + extent] * zq[at : at + 1, :]
-            sums[2] = sums[2] + line * zv[at : at + 1, :]
+    for low, high in groups(count, GATHER_GROUP):
+        part = slice(2 * low * extent, 2 * high * extent)
+        left = (eh[part, :], el[part, :])
+        along = dot3(left, weights)
+        slope = dot3(left, slopes)
+        for g in range(low, high):
+            for c in range(2):
+                at = c * slots_padded + first + g
+                base = (2 * (g - low) + c) * extent
+                line = along[base : base + extent]
+                sums[0] = sums[0] + line * zq[at : at + 1, :]
+                sums[1] = sums[1] + slope[base : base + extent] * zq[at : at + 1, :]
+                sums[2] = sums[2] + line * zv[at : at + 1, :]
     forces = [
         -jnp.sum(total * shape[...], axis=0, keepdims=True)
         for total, shape in zip(sums, (vx, wx, wx))
@@ -276,6 +295,11 @@
 
 
 SMEM = pl.BlockSpec(memory_space=pltpu.SMEM)
+IN_VMEM = pl.BlockSpec(memory_space=pltpu.VMEM)
+
+
+def near_core(array):
+    return pltpu.with_memory_space_constraint(array, pltpu.VMEM)
 
 
 def pair_kernel(centre, others, mesh_size):
@@ -323,13 +347,14 @@
     total = doms * atom_count
     where_am_i = jnp.stack([sect, dom, (dom >= doms // 2).astype(jnp.int32)])
 
-    packed = jnp.concatenate(
-        [cells.astype(jnp.float32), fracs, charges[None], jnp.zeros_like(charges)[None]], axis=0
-    ).reshape(8, block_count, BLOCK)
-    packed = jnp.transpose(packed, (1, 0, 2))
-    row = lax.all_to_all(
-        jnp.broadcast_to(packed[None], (doms,) + packed.shape), "dom", 0, 0, tiled=True
-    )
+    f32, bf16 = jnp.float32, jnp.bfloat16
+    copies = pl.pallas_call(
+        pack_kernel,
+        out_shape=jax.ShapeDtypeStruct((doms, block_count, 8, BLOCK), f32),
+        name="pack",
+    )(cells, fracs, charges)
+    row = lax.all_to_all(copies, "dom", 0, 0, tiled=True)
+    packed = copies[0]
 
     edges = []
     for s in range(sects):
@@ -342,7 +367,7 @@
     same = np.eye(mesh_size, dtype=np.float32)
     back = np.roll(same[::-1], 1, axis=0)
     flip, same, back = (jnp.asarray(m).astype(jnp.bfloat16) for m in (flip, same, back))
-    firsts = [slots * n // CHUNKS for n in range(CHUNKS + 1)]
+    firsts = [-(-slots * n // CHUNKS) for n in range(CHUNKS + 1)]
     counts = [b - a for a, b in zip(firsts, firsts[1:])]
     planes = []
     for first, count in zip(firsts, counts):
@@ -351,10 +376,7 @@
         planes.append(influence[half + lowest : half + highest + 1])
     sect_flip = [(s, sects - 1 - s) for s in range(sects)]
     dom_flip = [(d, doms - 1 - d) for d in range(doms)]
-    planes = [
-        lax.ppermute(p, *(("dom", dom_flip) if n % 2 else ("sect", sect_flip)))
-        for n, p in enumerate(planes)
-    ]
+    planes = [lax.ppermute(p, "sect", sect_flip) for p in planes]
 
     step = np.arange(mesh_size)
     angle = 2.0 * np.pi * (np.outer(step, step) % mesh_size) / mesh_size
@@ -372,26 +394,31 @@
 
     atom_step = 512
     grid = (total // atom_step,)
-    f32, bf16 = jnp.float32, jnp.bfloat16
     shapes = [
         ((extent, total), f32),
-        ((extent, total), f32),
         ((2 * slots_padded, total), f32),
-        ((2 * slots_padded, total), f32),
-    ] + [((mesh_size, total), bf16)] * 4
-    wx, vx, zq, zv, bwh, bwl, bvh, bvl = pl.pallas_call(
-        lambda *refs: basis_kernel(mesh_size, x_width, z_width, slots_padded, *refs),
-        grid=grid,
-        in_specs=[
-            SMEM,
-            pl.BlockSpec((atom_step // atom_count, block_count, 8, BLOCK), lambda n: (n, 0, 0, 0)),
-        ],
-        out_specs=[along_atoms(shape[0], atom_step) for shape, _ in shapes],
-        out_shape=[jax.ShapeDtypeStruct(shape, dtype) for shape, dtype in shapes],
-        compiler_params=params(),
-        cost_estimate=cost(6),
-        name="basis",
-    )(where_am_i, row)
+        ((mesh_size, total), bf16),
+        ((mesh_size, total), bf16),
+    ]
+
+    def basis(which, blocks):
+        return pl.pallas_call(
+            lambda *refs: basis_kernel(which, mesh_size, x_width, z_width, slots_padded, *refs),
+            grid=grid,
+            in_specs=[
+                SMEM,
+                pl.BlockSpec(
+                    (atom_step // atom_count, block_count, 8, BLOCK), lambda n: (n, 0, 0, 0)
+                ),
+            ],
+            out_specs=[along_atoms(shape[0], atom_step) for shape, _ in shapes],
+            out_shape=[jax.ShapeDtypeStruct(shape, dtype) for shape, dtype in shapes],
+            compiler_params=params(),
+            cost_estimate=cost(4),
+            name="basis",
+        )(where_am_i, blocks)
+
+    wx, zq, bwh, bwl = basis(0, row)
 
     sent = []
     for first, count in zip(firsts, counts):
@@ -408,45 +435,49 @@
             + [whole(t) for t in (rh, rl, ih, il)],
             out_specs=pl.BlockSpec(shape, lambda n: (0, 0, 0, 0)),
             out_shape=jax.ShapeDtypeStruct(shape, f32),
-            scratch_shapes=[pltpu.VMEM((2 * count * extent, mesh_size), f32)],
+            scratch_shapes=[pltpu.VMEM((count * extent, mesh_size), f32)] * 2,
             compiler_params=params(),
             cost_estimate=cost(9),
             name="spread",
         )(wx, zq, bwh, bwl, rh, rl, ih, il)
         sent.append(lines)
-    corner, beside, planes, sent[0] = lax.optimization_barrier(
-        (influence[half:, 0:1], row, planes, sent[0])
-    )
-    planes = [
-        lax.ppermute(p, *(("sect", sect_flip) if n % 2 else ("dom", dom_flip)))
-        for n, p in enumerate(planes)
-    ]
+    corner, beside, planes[0], sent[0] = lax.optimization_barrier(
+        (influence[half:, 0:1], row, planes[0], sent[0])
+    )
+    vx, zv, bvh, bvl = basis(1, beside)
+    planes[0] = lax.ppermute(planes[0], "dom", dom_flip)
     edge = lax.ppermute(corner, ("sect", "dom"), edges)
+    sent = [lax.all_to_all(lines, "sect", split_axis=0, concat_axis=0, tiled=True) for lines in sent]
+    planes[1:], beside, sent[0] = lax.optimization_barrier((planes[1:], beside, sent[0]))
+    planes[1:] = [lax.ppermute(p, "dom", dom_flip) for p in planes[1:]]
+    planes[0], edge, sent[0] = lax.optimization_barrier((planes[0], edge, sent[0]))
     ahead = [(s, (s + 1) % sects) for s in range(sects)]
     behind = [(b, a) for a, b in ahead]
     near = [lax.ppermute(beside, "sect", ahead), lax.ppermute(beside, "sect", behind)]
-    sent = [lax.all_to_all(lines, "sect", split_axis=0, concat_axis=0, tiled=True) for lines in sent]
-    planes[0], edge, sent[0] = lax.optimization_barrier((planes[0], edge, sent[0]))
-    factors = [
-        pl.pallas_call(
-            lambda *refs, first=first: influence_kernel(first, half, float(mesh_size) ** -3, *refs),
+
+    def folded(first, count, mirror):
+        return pl.pallas_call(
+            lambda *refs: influence_kernel(first, half, float(mesh_size) ** -3, *refs),
             in_specs=[SMEM] + [pl.BlockSpec(memory_space=pltpu.VMEM)] * 6,
             out_specs=pl.BlockSpec(memory_space=pltpu.VMEM),
             out_shape=jax.ShapeDtypeStruct((count, mesh_size, lanes), f32),
             compiler_params=params(),
             cost_estimate=cost(3.5),
             name="influence",
-        )(where_am_i, influence, mirror, edge, flip, same, back)
-        for first, count, mirror in zip(firsts, counts, planes)
-    ]
+        )(where_am_i, influence, mirror, near_core(edge), flip, same, back)
+
+    factors = [folded(firsts[0], counts[0], planes[0])]
+    for n in range(1, CHUNKS):
+        factors.append(folded(firsts[n], counts[n], planes[n]))
     fields = []
+    near, row, packed, sent[-1] = lax.optimization_barrier((near, row, packed, sent[-1]))
     for lines, factor in zip(sent, factors):
         field = pl.pallas_call(
             filter_kernel,
             grid=(1,),
             in_specs=[
-                whole(lines),
-                whole(factor),
+                IN_VMEM,
+                IN_VMEM,
                 whole(th),
                 whole(tl),
             ],
@@ -455,9 +486,8 @@
             compiler_params=params(),
             cost_estimate=cost(5.5),
             name="filter",
-        )(lines, factor, th, tl)
+        )(near_core(lines), factor, th, tl)
         fields.append(field)
-    near, row, packed, fields[0] = lax.optimization_barrier((near, row, packed, fields[0]))
     fields = [lax.all_to_all(field, "sect", split_axis=0, concat_axis=0, tiled=True) for field in fields]
 
     listed = pair_blocks[0, 0]
@@ -482,7 +512,7 @@
         earlier = [pl.pallas_call(
             lambda *refs, first=first, count=count: gather_kernel(first, count, slots_padded, *refs),
             grid=grid,
-            in_specs=[whole(lines), whole(bh), whole(bl)]
+            in_specs=[IN_VMEM, whole(bh), whole(bl)]
             + [along_atoms(a.shape[0], atom_step) for a in (wx, vx, zq, zv, bwh, bwl, bvh, bvl)]
             + [by_dom] * len(earlier),
             out_specs=by_dom,
@@ -491,7 +521,7 @@
             compiler_params=params(),
             cost_estimate=cost(13),
             name="gather",
-        )(lines, bh, bl, wx, vx, zq, zv, bwh, bwl, bvh, bvl, *earlier)]
+        )(near_core(lines), bh, bl, wx, vx, zq, zv, bwh, bwl, bvh, bvl, *earlier)]
     shares = lax.all_to_all(earlier[0], "dom", 0, 0, tiled=True)
     mesh_force = jnp.sum(shares, axis=0)[:3]
     return (short_force + mesh_force).reshape(3, 1, 1, atom_count)

time: 154 us -> 137 us (0.89)
  waiting for transfers between devices: 24.3 us -> 17 us
  local copies, waits for them, and re-layouts: 9.2 us -> 4.14 us
  starting transfers between devices: 41.8 us -> 37.8 us
    all_to_all x2, waiting for transfers between devices: 9.77 us -> 5.58 us  [shards(): lax.all_to_all(field, 'sect', split_axis=0, concat_axis=0, tiled=True)]
    unnamed x18 -> x6, local copies, waits for them, and re-layouts: 4.13 us -> 0.63 us
    ppermute x1, starting transfers between devices: 0.06 us -> 2.98 us  [shards(): lax.ppermute(beside, 'sect', behind)]
    ppermute x1, starting transfers between devices: 2.88 us -> 0.01 us  [shards(): lax.ppermute(beside, 'sect', ahead)]
    ppermute x1, starting transfers between devices: 3.53 us -> 0.69 us  [shards(): edge = lax.ppermute(corner, ('sect', 'dom'), edges)]
    ppermute x4, waiting for transfers between devices: 2.39 us -> 0.01 us  [the longest x2 0.01 us: shards(): planes = [lax.ppermute(p, 'sect', sect_flip) for p in planes]]
    all_to_all x1, starting transfers between devices: 6.32 us -> 4.54 us  [shards(): shares = lax.all_to_all(earlier[0], 'dom', 0, 0, tiled=True)]
    pallas_call x5 -> x7, Pallas kernels: 24.8 us -> 26.5 us  [the longest x2 9.11 us: shards(): pl.pallas_call(filter_kernel, grid=(1,), in_specs=[IN_VMEM, IN_VMEM, whol...]
  transfers between devices with their start and end apart: 13 -> 13, of which waited for: 5 -> 4; matrix products, arithmetic and copies ran while one was open for 6% -> 7% of each run, Pallas kernels for 36% -> 41%
where the time goes in v3:
time: 137 us; the launch traced here: 135 us
  Pallas kernels  69.5 us (51%)
  starting transfers between devices  37.8 us (28%)
  waiting for transfers between devices  17 us (12%)
  other arithmetic  6.67 us (5%)
  local copies, waits for them, and re-layouts  4.14 us (3%)
    pallas_call x2, Pallas kernels, shards(): pl.pallas_call(lambda *refs, first=first, count=count: gather_kernel(firs...  25.2 us
    pallas_call x2, Pallas kernels, shards(): pl.pallas_call(lambda *refs, first=first, count=count: spread_kernel(firs...  17.8 us
    pallas_call x2, Pallas kernels, shards(): pl.pallas_call(filter_kernel, grid=(1,), in_specs=[IN_VMEM, IN_VMEM, whol...  9.11 us
    pallas_call x2, Pallas kernels, basis(): pl.pallas_call(lambda *refs: basis_kernel(which, mesh_size, x_width, z_wi...  8.13 us
    pallas_call x2, Pallas kernels, folded(): pl.pallas_call(lambda *refs: influence_kernel(first, half, float(mesh_siz...  7.89 us
    all_to_all x2, starting transfers between devices, shards(): lax.all_to_all(field, 'sect', split_axis=0, concat_axis=0, tiled=True)  7.67 us
    all_to_all x2, starting transfers between devices, shards(): lax.all_to_all(lines, 'sect', split_axis=0, concat_axis=0, tiled=True)  7.54 us
    all_to_all x1, starting transfers between devices, shards(): row = lax.all_to_all(copies, 'dom', 0, 0, tiled=True)  6.33 us
  transfers between devices with their start and end apart: 13, of which 4 were waited for; matrix products, arithmetic and copies ran while one was open for 7% of the time, Pallas kernels for 41%

profile of v3, /device:TPU:0, one launch (start us, length us, event | category | flops | bytes accessed | tf_op | source)
XLA Modules:
  0.0 135.4 jit_solution(11164577916182014131)
XLA Ops:
  0.0 1.3 pack.1
  1.3 6.3 %all-to-all-start = ((f32[8,2,8,128]{3,2,1,0:T(8,128)}), f32[8,2,8,128]{3,2,1,0:T(8,128)S(1)}, u32[]{:S(2)}, u32[]{:S(2)}) async-start(f32[8,2,8,128]{3,2,1,0:T(8,128)} %pack.1), calls=%async_computation | async-start | bytes 131072 | tf_op jit(solution)/shard_map/all_to_all | solution.py:356
  7.7 1.3 fusion.66
  9.0 2.5 %collective-permute-start.1 = (f32[8,64,256]{2,1,0:T(8,128)S(1)}, f32[8,64,256]{2,1,0:T(8,128)}, u32[]{:S(2)}, u32[]{:S(2)}) collective-permute-start(f32[8,64,256]{2,1,0:T(8,128)S(1)} %get-tuple-element.57), channel_id=1, source_target_pairs={{0,24},{8,16},{16,8},{24,0},{1,25},{9,17},{17,9},{25,1},{2,26},{10... | collective-permute-start | bytes 1572872 | tf_op jit(solution)/shard_map/ppermute | solution.py:379
  11.5 0.5 collective-permute-start
  12.0 0.7 slice_bitcast_fusion
  12.7 0.9 slice.160
  13.6 0.7 pad_add_fusion.refs_0_
  14.2 0.0 all-to-all-done.refs_1_
  14.2 0.0 copy-start
  14.2 0.6 copy-done
  14.9 4.1 %basis.2 = (f32[72,2048]{1,0:T(8,128)}, f32[48,2048]{1,0:T(8,128)}, bf16[256,2048]{1,0:T(8,128)(2,1)}, bf16[256,2048]{1,0:T(8,128)(2,1)}) custom-call(s32[3]{0:T(128)} %pad_add_fusion.refs_0_, f32[8,2,8,128]{3,2,1,0:T(8,128)} %copy-done), custom_call_target="tpu_custom_call" | custom-call | flops 4000000000 | bytes 400000 | tf_op jit(solution)/shard_map/basis/pallas_call | solution.py:405
  18.9 9.2 %spread.2 = f32[4,9,72,128]{3,2,1,0:T(8,128)} custom-call(f32[72,2048]{1,0:T(8,128)} %get-tuple-element.28.refs_0_.refs_3_, f32[48,2048]{1,0:T(8,128)} %get-tuple-element.29.refs_1_.refs_5_, bf16[256,2048]{1,0:T(8,128)(2,1)} %get-tuple-element.30.refs_2_.refs_7_, bf16[256,2048]{1,0:T(8,128)(2,1)} %get-tuple-element.31.refs_3_.refs_8_, ...), custom_call_target="tpu_custom_call" | custom-call | flops 8999999488 | bytes 900000 | tf_op jit(solution)/shard_map/spread/pallas_call | solution.py:426
  28.1 0.0 copy-start.2
  28.1 0.0 collective-permute-done.1
  28.1 3.7 %all-to-all-start.1 = ((f32[4,9,72,128]{3,2,1,0:T(8,128)}), f32[4,9,72,128]{3,2,1,0:T(8,128)S(1)}, u32[]{:S(2)}, u32[]{:S(2)}) async-start(f32[4,9,72,128]{3,2,1,0:T(8,128)} %spread.2), calls=%async_computation.1 | async-start | bytes 2654208 | tf_op jit(solution)/shard_map/all_to_all | solution.py:450
  31.9 0.0 copy-done.2
  31.9 2.9 %collective-permute-start.5 = (f32[8,64,256]{2,1,0:T(8,128)}, f32[8,64,256]{2,1,0:T(8,128)}, u32[]{:S(2)}, u32[]{:S(2)}) collective-permute-start(f32[8,64,256]{2,1,0:T(8,128)} %collective-permute-done.1), channel_id=1, source_target_pairs={{0,7},{1,6},{2,5},{3,4},{4,3},{5,2},{6,1},{7,0},{8,15},{9,14},{10,... | collective-permute-start | bytes 1572872 | tf_op jit(solution)/shard_map/ppermute | solution.py:448
  34.8 8.6 %spread.3 = f32[4,8,72,128]{3,2,1,0:T(8,128)} custom-call(f32[72,2048]{1,0:T(8,128)} %get-tuple-element.28.refs_0_.refs_3_, f32[48,2048]{1,0:T(8,128)} %get-tuple-element.29.refs_1_.refs_5_, bf16[256,2048]{1,0:T(8,128)(2,1)} %get-tuple-element.30.refs_2_.refs_7_, bf16[256,2048]{1,0:T(8,128)(2,1)} %get-tuple-element.31.refs_3_.refs_8_, ...), custom_call_target="tpu_custom_call" | custom-call | flops 8999999488 | bytes 900000 | tf_op jit(solution)/shard_map/spread/pallas_call | solution.py:426
  43.5 0.7 collective-permute-start.6
  44.1 5.7 %all-to-all-done.1.lines = f32[4,9,72,128]{3,2,1,0:T(8,128)S(1)} async-done(((f32[4,9,72,128]{3,2,1,0:T(8,128)}), f32[4,9,72,128]{3,2,1,0:T(8,128)S(1)}, u32[]{:S(2)}, u32[]{:S(2)}) %all-to-all-start.1) | async-done | bytes 1327136 | tf_op jit(solution)/shard_map/all_to_all | solution.py:450
  49.8 3.8 %all-to-all-start.2 = ((f32[4,8,72,128]{3,2,1,0:T(8,128)}), f32[4,8,72,128]{3,2,1,0:T(8,128)S(1)}, u32[]{:S(2)}, u32[]{:S(2)}) async-start(f32[4,8,72,128]{3,2,1,0:T(8,128)} %spread.3), calls=%async_computation.2 | async-start | bytes 2359296 | tf_op jit(solution)/shard_map/all_to_all | solution.py:450
  53.6 0.0 copy-start.1
  53.6 4.1 %basis.3 = (f32[72,2048]{1,0:T(8,128)}, f32[48,2048]{1,0:T(8,128)}, bf16[256,2048]{1,0:T(8,128)(2,1)}, bf16[256,2048]{1,0:T(8,128)(2,1)}) custom-call(s32[3]{0:T(128)} %pad_add_fusion.refs_0_, f32[8,2,8,128]{3,2,1,0:T(8,128)} %copy-done), custom_call_target="tpu_custom_call" | custom-call | flops 4000000000 | bytes 400000 | tf_op jit(solution)/shard_map/basis/pallas_call | solution.py:405
  57.7 0.0 collective-permute-done
  57.7 0.0 copy-done.1
  57.7 3.0 %collective-permute-start.3 = (f32[8,2,8,128]{3,2,1,0:T(8,128)S(1)}, f32[8,2,8,128]{3,2,1,0:T(8,128)S(1)}, u32[]{:S(2)}, u32[]{:S(2)}) collective-permute-start(f32[8,2,8,128]{3,2,1,0:T(8,128)S(1)} %copy-done.1), channel_id=1, source_target_pairs={{8,0},{16,8},{24,16},{0,24},{9,1},{17,9},{25,17},{1,25},{10,2},{18... | collective-permute-start | bytes 196616 | tf_op jit(solution)/shard_map/ppermute | solution.py:456
  60.7 0.0 collective-permute-start.2
  60.7 2.1 %collective-permute-start.4 = (f32[8,64,256]{2,1,0:T(8,128)}, f32[8,64,256]{2,1,0:T(8,128)}, u32[]{:S(2)}, u32[]{:S(2)}) collective-permute-start(f32[8,64,256]{2,1,0:T(8,128)} %collective-permute-done), channel_id=1, source_target_pairs={{0,7},{1,6},{2,5},{3,4},{4,3},{5,2},{6,1},{7,0},{8,15},{9,14},{10,... | collective-permute-start | bytes 1572872 | tf_op jit(solution)/shard_map/ppermute | solution.py:452
  62.8 0.0 collective-permute-done.6.refs_3_
  62.8 0.0 collective-permute-done.5.refs_2_
  62.8 4.0 %influence.3.factor = f32[9,256,128]{2,1,0:T(8,128)} custom-call(s32[3]{0:T(128)} %pad_add_fusion.refs_0_, f32[32,64,256]{2,1,0:T(8,128)} %refs_1_.3, f32[8,64,256]{2,1,0:T(8,128)} %collective-permute-done.5.refs_2_, f32[16,1,256]{2,1,0:T(1,128)S(1)} %collective-permute-done.6.refs_3_, bf16[128,64]{1,0:T(8,128)(2,1)} %constant.187.refs_4_, ...), custom_call_target="tpu_custom_call" | custom-call | flops 3500000000 | bytes 350000 | tf_op jit(solution)/shard_map/influence/pallas_call | solution.py:459
  66.8 4.8 %filter.3 = f32[4,9,72,128]{3,2,1,0:T(8,128)} custom-call(f32[4,9,72,128]{3,2,1,0:T(8,128)S(1)} %all-to-all-done.1.lines, f32[9,256,128]{2,1,0:T(8,128)} %influence.3.factor, bf16[512,256]{1,0:T(8,128)(2,1)} %constant.190.th, bf16[512,256]{1,0:T(8,128)(2,1)} %constant.193.tl), custom_call_target="tpu_custom_call" | custom-call | flops 5500000256 | bytes 550000 | tf_op jit(solution)/shard_map/filter/pallas_call | solution.py:475
  71.6 0.0 all-to-all-done.2.lines
  71.7 3.9 %all-to-all-start.4 = ((f32[4,9,72,128]{3,2,1,0:T(8,128)}), f32[4,9,72,128]{3,2,1,0:T(8,128)S(1)}, u32[]{:S(2)}, u32[]{:S(2)}) async-start(f32[4,9,72,128]{3,2,1,0:T(8,128)} %filter.3), calls=%async_computation.4 | async-start | bytes 2654208 | tf_op jit(solution)/shard_map/all_to_all | solution.py:491
  75.6 0.0 collective-permute-done.3
  75.6 0.0 collective-permute-done.2
  75.6 0.2 convolution_bitcast_fusion
  75.9 3.0 %multiply_reduce_fusion.2 = (f32[128]{0:T(128)S(1)}, f32[128]{0:T(128)S(1)}, f32[128]{0:T(128)S(1)}) fusion(f32[8,128]{1,0:T(8,128)S(1)} %get-tuple-element.64, f32[128]{0:T(128)S(1)} %get-tuple-element.78, f32[8,128]{1,0:T(8,128)S(1)} %get-tuple-element.65, f32[128]{0:T(128)S(1)} %get-tuple-element.79, f32[8,128]{1,0:T(8,128)S(1)} %get-tuple-element.60, ...), kind=kLoop, calls=%fused_computation.35 | loop fusion | flops 14941824 | bytes 33792 | tf_op jit(solution)/shard_map/reduce_sum | solution.py:330
  78.8 3.0 %multiply_reduce_fusion.5 = (f32[128]{0:T(128)S(1)}, f32[128]{0:T(128)S(1)}, f32[128]{0:T(128)S(1)}) fusion(f32[8,128]{1,0:T(8,128)S(1)} %get-tuple-element.71, f32[128]{0:T(128)S(1)} %get-tuple-element.85, f32[8,128]{1,0:T(8,128)S(1)} %get-tuple-element.72, f32[128]{0:T(128)S(1)} %get-tuple-element.86, f32[8,128]{1,0:T(8,128)S(1)} %get-tuple-element.67, ...), kind=kLoop, calls=%fused_computation.63 | loop fusion | flops 14941824 | bytes 33792 | tf_op jit(solution)/shard_map/reduce_sum | solution.py:330
  81.8 0.0 collective-permute-done.4.refs_2_
  81.8 3.9 %influence.2.factor = f32[8,256,128]{2,1,0:T(8,128)} custom-call(s32[3]{0:T(128)} %pad_add_fusion.refs_0_, f32[32,64,256]{2,1,0:T(8,128)} %refs_1_.3, f32[8,64,256]{2,1,0:T(8,128)} %collective-permute-done.4.refs_2_, f32[16,1,256]{2,1,0:T(1,128)S(1)} %collective-permute-done.6.refs_3_, bf16[128,64]{1,0:T(8,128)(2,1)} %constant.187.refs_4_, ...), custom_call_target="tpu_custom_call" | custom-call | flops 3500000000 | bytes 350000 | tf_op jit(solution)/shard_map/influence/pallas_call | solution.py:459
  85.7 4.3 %filter.2 = f32[4,8,72,128]{3,2,1,0:T(8,128)} custom-call(f32[4,8,72,128]{3,2,1,0:T(8,128)S(1)} %all-to-all-done.2.lines, f32[8,256,128]{2,1,0:T(8,128)} %influence.2.factor, bf16[512,256]{1,0:T(8,128)(2,1)} %constant.190.th, bf16[512,256]{1,0:T(8,128)(2,1)} %constant.193.tl), custom_call_target="tpu_custom_call" | custom-call | flops 5500000256 | bytes 550000 | tf_op jit(solution)/shard_map/filter/pallas_call | solution.py:475
  90.0 3.0 %all-to-all-done.4.refs_0_ = f32[4,9,72,128]{3,2,1,0:T(8,128)S(1)} async-done(((f32[4,9,72,128]{3,2,1,0:T(8,128)}), f32[4,9,72,128]{3,2,1,0:T(8,128)S(1)}, u32[]{:S(2)}, u32[]{:S(2)}) %all-to-all-start.4) | async-done | bytes 1327136 | tf_op jit(solution)/shard_map/all_to_all | solution.py:491
  93.0 3.7 %all-to-all-start.3 = ((f32[4,8,72,128]{3,2,1,0:T(8,128)}), f32[4,8,72,128]{3,2,1,0:T(8,128)S(1)}, u32[]{:S(2)}, u32[]{:S(2)}) async-start(f32[4,8,72,128]{3,2,1,0:T(8,128)} %filter.2), calls=%async_computation.3 | async-start | bytes 2359296 | tf_op jit(solution)/shard_map/all_to_all | solution.py:491
  96.7 13.1 %gather.2.refs_11_ = f32[8,4,256]{2,1,0:T(4,128)} custom-call(f32[4,9,72,128]{3,2,1,0:T(8,128)S(1)} %all-to-all-done.4.refs_0_, bf16[512,512]{1,0:T(8,128)(2,1)} %constant.194.refs_1_, bf16[512,512]{1,0:T(8,128)(2,1)} %constant.197.refs_2_, f32[72,2048]{1,0:T(8,128)} %get-tuple-element.28.refs_0_.refs_3_, f32[72,2048]{1,0:T(8,128)} %get-tuple-element.45.refs_4_, ...), custom_call_target="tpu_custom_call" | custom-call | flops 12999999488 | bytes 1300000 | tf_op jit(solution)/shard_map/gather/pallas_call | solution.py:512
  109.8 2.6 %all-to-all-done.3.refs_0_ = f32[4,8,72,128]{3,2,1,0:T(8,128)S(1)} async-done(((f32[4,8,72,128]{3,2,1,0:T(8,128)}), f32[4,8,72,128]{3,2,1,0:T(8,128)S(1)}, u32[]{:S(2)}, u32[]{:S(2)}) %all-to-all-start.3) | async-done | bytes 1179680 | tf_op jit(solution)/shard_map/all_to_all | solution.py:491
  112.4 12.1 %gather.3 = f32[8,4,256]{2,1,0:T(4,128)} custom-call(f32[4,8,72,128]{3,2,1,0:T(8,128)S(1)} %all-to-all-done.3.refs_0_, bf16[512,512]{1,0:T(8,128)(2,1)} %constant.194.refs_1_, bf16[512,512]{1,0:T(8,128)(2,1)} %constant.197.refs_2_, f32[72,2048]{1,0:T(8,128)} %get-tuple-element.28.refs_0_.refs_3_, f32[72,2048]{1,0:T(8,128)} %get-tuple-element.45.refs_4_, ...), custom_call_target="tpu_custom_call" | custom-call | flops 12999999488 | bytes 1300000 | tf_op jit(solution)/shard_map/gather/pallas_call | solution.py:512
  124.5 4.5 %all-to-all-start.5 = ((f32[8,4,256]{2,1,0:T(4,128)}), f32[8,4,256]{2,1,0:T(4,128)S(1)}, u32[]{:S(2)}, u32[]{:S(2)}) async-start(f32[8,4,256]{2,1,0:T(4,128)} %gather.3), calls=%async_computation.5 | async-start | bytes 65536 | tf_op jit(solution)/shard_map/all_to_all | solution.py:525
  129.1 5.7 %all-to-all-done.5 = f32[8,4,256]{2,1,0:T(4,128)S(1)} async-done(((f32[8,4,256]{2,1,0:T(4,128)}), f32[8,4,256]{2,1,0:T(4,128)S(1)}, u32[]{:S(2)}, u32[]{:S(2)}) %all-to-all-start.5) | async-done | bytes 32800 | tf_op jit(solution)/shard_map/all_to_all | solution.py:525
  134.8 0.6 reshape.198
  (7 shorter events, 0.1 us)
Async XLA Ops:
  1.3 12.9 %all-to-all-start = ((f32[8,2,8,128]{3,2,1,0:T(8,128)}), f32[8,2,8,128]{3,2,1,0:T(8,128)S(1)}, u32[]{:S(2)}, u32[]{:S(2)}) async-start(f32[8,2,8,128]{3,2,1,0:T(8,128)} %pack.1), calls=%async_computation | async-start | bytes 131072 | tf_op jit(solution)/shard_map/all_to_all | solution.py:356
  9.0 19.2 %collective-permute-start.1 = (f32[8,64,256]{2,1,0:T(8,128)S(1)}, f32[8,64,256]{2,1,0:T(8,128)}, u32[]{:S(2)}, u32[]{:S(2)}) collective-permute-start(f32[8,64,256]{2,1,0:T(8,128)S(1)} %get-tuple-element.57), channel_id=1, source_target_pairs={{0,24},{8,16},{16,8},{24,0},{1,25},{9,17},{17,9},{25,1},{2,26},{10... | collective-permute-start | bytes 1572872 | tf_op jit(solution)/shard_map/ppermute | solution.py:379
  11.5 46.2 %collective-permute-start = (f32[8,64,256]{2,1,0:T(8,128)S(1)}, f32[8,64,256]{2,1,0:T(8,128)}, u32[]{:S(2)}, u32[]{:S(2)}) collective-permute-start(f32[8,64,256]{2,1,0:T(8,128)S(1)} %get-tuple-element.58), channel_id=1, source_target_pairs={{0,24},{8,16},{16,8},{24,0},{1,25},{9,17},{17,9},{25,1},{2,26},{10... | collective-permute-start | bytes 1572872 | tf_op jit(solution)/shard_map/ppermute | solution.py:379
  14.2 0.6 copy-start
  28.1 3.7 %copy-start.2 = (s32[1,1,2,8]{3,2,1,0:T(2,128)S(1)}, s32[1,1,2,8]{3,2,1,0:T(2,128)}, u32[]{:S(2)}) copy-start(s32[1,1,2,8]{3,2,1,0:T(2,128)} %param.15) | copy-start | bytes 196
  28.1 21.7 %all-to-all-start.1 = ((f32[4,9,72,128]{3,2,1,0:T(8,128)}), f32[4,9,72,128]{3,2,1,0:T(8,128)S(1)}, u32[]{:S(2)}, u32[]{:S(2)}) async-start(f32[4,9,72,128]{3,2,1,0:T(8,128)} %spread.2), calls=%async_computation.1 | async-start | bytes 2654208 | tf_op jit(solution)/shard_map/all_to_all | solution.py:450
  31.9 30.9 %collective-permute-start.5 = (f32[8,64,256]{2,1,0:T(8,128)}, f32[8,64,256]{2,1,0:T(8,128)}, u32[]{:S(2)}, u32[]{:S(2)}) collective-permute-start(f32[8,64,256]{2,1,0:T(8,128)} %collective-permute-done.1), channel_id=1, source_target_pairs={{0,7},{1,6},{2,5},{3,4},{4,3},{5,2},{6,1},{7,0},{8,15},{9,14},{10,... | collective-permute-start | bytes 1572872 | tf_op jit(solution)/shard_map/ppermute | solution.py:448
  43.5 19.3 %collective-permute-start.6 = (f32[16,1,256]{2,1,0:T(1,128)S(1)}, f32[16,1,256]{2,1,0:T(1,128)S(1)}, u32[]{:S(2)}, u32[]{:S(2)}) collective-permute-start(f32[16,1,256]{2,1,0:T(1,128)S(1)} %slice.160), channel_id=1, source_target_pairs={{0,7},{1,6},{2,5},{3,4},{4,3},{5,2},{6,1},{7,0},{8,31},{9,30},{10,... | collective-permute-start | bytes 49160 | tf_op jit(solution)/shard_map/ppermute | solution.py:449
  49.8 21.8 %all-to-all-start.2 = ((f32[4,8,72,128]{3,2,1,0:T(8,128)}), f32[4,8,72,128]{3,2,1,0:T(8,128)S(1)}, u32[]{:S(2)}, u32[]{:S(2)}) async-start(f32[4,8,72,128]{3,2,1,0:T(8,128)} %spread.3), calls=%async_computation.2 | async-start | bytes 2359296 | tf_op jit(solution)/shard_map/all_to_all | solution.py:450
  53.6 4.1 %copy-start.1 = (f32[8,2,8,128]{3,2,1,0:T(8,128)S(1)}, f32[8,2,8,128]{3,2,1,0:T(8,128)}, u32[]{:S(2)}) copy-start(f32[8,2,8,128]{3,2,1,0:T(8,128)} %copy-done) | copy-start | bytes 196612
  57.7 17.9 %collective-permute-start.3 = (f32[8,2,8,128]{3,2,1,0:T(8,128)S(1)}, f32[8,2,8,128]{3,2,1,0:T(8,128)S(1)}, u32[]{:S(2)}, u32[]{:S(2)}) collective-permute-start(f32[8,2,8,128]{3,2,1,0:T(8,128)S(1)} %copy-done.1), channel_id=1, source_target_pairs={{8,0},{16,8},{24,16},{0,24},{9,1},{17,9},{25,17},{1,25},{10,2},{18... | collective-permute-start | bytes 196616 | tf_op jit(solution)/shard_map/ppermute | solution.py:456
  60.7 14.9 %collective-permute-start.2 = (f32[8,2,8,128]{3,2,1,0:T(8,128)S(1)}, f32[8,2,8,128]{3,2,1,0:T(8,128)S(1)}, u32[]{:S(2)}, u32[]{:S(2)}) collective-permute-start(f32[8,2,8,128]{3,2,1,0:T(8,128)S(1)} %copy-done.1), channel_id=1, source_target_pairs={{0,8},{8,16},{16,24},{24,0},{1,9},{9,17},{17,25},{25,1},{2,10},{10... | collective-permute-start | bytes 196616 | tf_op jit(solution)/shard_map/ppermute | solution.py:456
  60.7 21.1 %collective-permute-start.4 = (f32[8,64,256]{2,1,0:T(8,128)}, f32[8,64,256]{2,1,0:T(8,128)}, u32[]{:S(2)}, u32[]{:S(2)}) collective-permute-start(f32[8,64,256]{2,1,0:T(8,128)} %collective-permute-done), channel_id=1, source_target_pairs={{0,7},{1,6},{2,5},{3,4},{4,3},{5,2},{6,1},{7,0},{8,15},{9,14},{10,... | collective-permute-start | bytes 1572872 | tf_op jit(solution)/shard_map/ppermute | solution.py:452
  71.7 21.3 %all-to-all-start.4 = ((f32[4,9,72,128]{3,2,1,0:T(8,128)}), f32[4,9,72,128]{3,2,1,0:T(8,128)S(1)}, u32[]{:S(2)}, u32[]{:S(2)}) async-start(f32[4,9,72,128]{3,2,1,0:T(8,128)} %filter.3), calls=%async_computation.4 | async-start | bytes 2654208 | tf_op jit(solution)/shard_map/all_to_all | solution.py:491
  93.0 19.5 %all-to-all-start.3 = ((f32[4,8,72,128]{3,2,1,0:T(8,128)}), f32[4,8,72,128]{3,2,1,0:T(8,128)S(1)}, u32[]{:S(2)}, u32[]{:S(2)}) async-start(f32[4,8,72,128]{3,2,1,0:T(8,128)} %filter.2), calls=%async_computation.3 | async-start | bytes 2359296 | tf_op jit(solution)/shard_map/all_to_all | solution.py:491
  124.5 10.3 %all-to-all-start.5 = ((f32[8,4,256]{2,1,0:T(4,128)}), f32[8,4,256]{2,1,0:T(4,128)S(1)}, u32[]{:S(2)}, u32[]{:S(2)}) async-start(f32[8,4,256]{2,1,0:T(4,128)} %gather.3), calls=%async_computation.5 | async-start | bytes 65536 | tf_op jit(solution)/shard_map/all_to_all | solution.py:525

commit v4 on v3

--- a/solution.py
+++ b/solution.py
@@ -175,26 +175,25 @@
     count, _, lanes = out.shape
     width = own.shape[1]
     lowest = half - max(first + count - 1, 1)
+    both_flip = jnp.concatenate([flip[...]] * 2, axis=1)
+    mirror = []
+    for g in range(count):
+        at = half - max(first + g, 1)
+        pair = jnp.concatenate(split(across[at - lowest]), axis=0)
+        turned = dot(both_flip, pair)
+        lines = lax.broadcasted_iota(jnp.int32, turned.shape, 0) % width
+        turned = jnp.where(lines == 0, edge[at], turned)
+        mirror.append(turned if first + g > 0 else jnp.zeros_like(turned))
     plain = [own[first + g] for g in range(count) for _ in range(2)]
     plain = split(jnp.concatenate(plain, axis=0))
-    pieces = []
-    for g in range(count):
-        at = half - max(first + g, 1)
-        pair = split(across[at - lowest])
-        turned = dot(flip[...], pair[0]) + dot(flip[...], pair[1])
-        lines = lax.broadcasted_iota(jnp.int32, turned.shape, 0) % width
-        pieces.append(jnp.where(lines == 0, edge[at], turned))
-    turned = split(jnp.concatenate(pieces, axis=0))
-    plain = dot(same[...], plain[0], 1) + dot(same[...], plain[1], 1)
-    mirror = dot(back[...], turned[0], 1) + dot(back[...], turned[1], 1)
+    mirror = split(jnp.concatenate(mirror, axis=0))
+    left = jnp.concatenate([same[...]] * 2 + [back[...]] * 2, axis=1)
+    values = dot(left, jnp.concatenate(plain + mirror, axis=1), 1)
     for g in range(count):
         keep = scale
         if first + g == half:
             keep = jnp.where(where_ref[2] == 1, scale, 0.0)
-        value = plain[:, g * lanes : (g + 1) * lanes]
-        if first + g > 0:
-            value = value + mirror[:, g * lanes : (g + 1) * lanes]
-        out[g] = value * keep
+        out[g] = values[:, g * lanes : (g + 1) * lanes] * keep
 
 
 def filter_kernel(lines, factor, th, tl, out):
@@ -414,7 +413,7 @@
             out_specs=[along_atoms(shape[0], atom_step) for shape, _ in shapes],
             out_shape=[jax.ShapeDtypeStruct(shape, dtype) for shape, dtype in shapes],
             compiler_params=params(),
-            cost_estimate=cost(4),
+            cost_estimate=cost(0.1 if which else 4),
             name="basis",
         )(where_am_i, blocks)
 
@@ -445,6 +444,7 @@
         (influence[half:, 0:1], row, planes[0], sent[0])
     )
     vx, zv, bvh, bvl = basis(1, beside)
+    vx, sent[-1] = lax.optimization_barrier((vx, sent[-1]))
     planes[0] = lax.ppermute(planes[0], "dom", dom_flip)
     edge = lax.ppermute(corner, ("sect", "dom"), edges)
     sent = [lax.all_to_all(lines, "sect", split_axis=0, concat_axis=0, tiled=True) for lines in sent]

time: 137 us -> 133 us (0.971)
  waiting for transfers between devices: 17 us -> 13.1 us
    all_to_all x2, waiting for transfers between devices: 5.58 us -> 3.11 us  [shards(): lax.all_to_all(field, 'sect', split_axis=0, concat_axis=0, tiled=True)]
    all_to_all x2, waiting for transfers between devices: 5.68 us -> 4.18 us  [shards(): lax.all_to_all(lines, 'sect', split_axis=0, concat_axis=0, tiled=True)]
  transfers between devices with their start and end apart: 13 -> 13, of which waited for: 4 -> 6; matrix products, arithmetic and copies ran while one was open for 7% -> 7% of each run, Pallas kernels for 41% -> 43%
where the time goes in v4:
time: 133 us; the launch traced here: 131 us
  Pallas kernels  69.3 us (52%)
  starting transfers between devices  37.8 us (28%)
  waiting for transfers between devices  13.1 us (10%)
  other arithmetic  6.67 us (5%)
  local copies, waits for them, and re-layouts  4.14 us (3%)
    pallas_call x2, Pallas kernels, shards(): pl.pallas_call(lambda *refs, first=first, count=count: gather_kernel(firs...  25.2 us
    pallas_call x2, Pallas kernels, shards(): pl.pallas_call(lambda *refs, first=first, count=count: spread_kernel(firs...  17.8 us
    pallas_call x2, Pallas kernels, shards(): pl.pallas_call(filter_kernel, grid=(1,), in_specs=[IN_VMEM, IN_VMEM, whol...  9.12 us
    pallas_call x2, Pallas kernels, basis(): pl.pallas_call(lambda *refs: basis_kernel(which, mesh_size, x_width, z_wi...  8.1 us
    pallas_call x2, Pallas kernels, folded(): pl.pallas_call(lambda *refs: influence_kernel(first, half, float(mesh_siz...  7.73 us
    all_to_all x2, starting transfers between devices, shards(): lax.all_to_all(lines, 'sect', split_axis=0, concat_axis=0, tiled=True)  7.57 us
    all_to_all x2, starting transfers between devices, shards(): lax.all_to_all(field, 'sect', split_axis=0, concat_axis=0, tiled=True)  7.47 us
    all_to_all x1, starting transfers between devices, shards(): row = lax.all_to_all(copies, 'dom', 0, 0, tiled=True)  6.33 us
  transfers between devices with their start and end apart: 13, of which 6 were waited for; matrix products, arithmetic and copies ran while one was open for 7% of the time, Pallas kernels for 43%

profile of v4, /device:TPU:0, one launch (start us, length us, event | category | flops | bytes accessed | tf_op | source)
XLA Modules:
  0.0 131.4 jit_solution(13642845434052177965)
XLA Ops:
  0.0 1.3 %pack.1 = f32[8,2,8,128]{3,2,1,0:T(8,128)} custom-call(s32[3,1,1,256]{3,2,1,0:T(1,128)} %cells.1, f32[3,1,1,256]{3,2,1,0:T(1,128)} %fracs.1, f32[1,1,256]{2,1,0:T(1,128)} %charges.1), custom_call_target="tpu_custom_call" | custom-call | tf_op jit(solution)/shard_map/pack/pallas_call | solution.py:350
  1.3 6.3 %all-to-all-start = ((f32[8,2,8,128]{3,2,1,0:T(8,128)}), f32[8,2,8,128]{3,2,1,0:T(8,128)S(1)}, u32[]{:S(2)}, u32[]{:S(2)}) async-start(f32[8,2,8,128]{3,2,1,0:T(8,128)} %pack.1), calls=%async_computation | async-start | bytes 131072 | tf_op jit(solution)/shard_map/all_to_all | solution.py:355
  7.7 1.3 fusion.66
  9.0 2.5 %collective-permute-start.1 = (f32[8,64,256]{2,1,0:T(8,128)S(1)}, f32[8,64,256]{2,1,0:T(8,128)}, u32[]{:S(2)}, u32[]{:S(2)}) collective-permute-start(f32[8,64,256]{2,1,0:T(8,128)S(1)} %get-tuple-element.61), channel_id=1, source_target_pairs={{0,24},{8,16},{16,8},{24,0},{1,25},{9,17},{17,9},{25,1},{2,26},{10... | collective-permute-start | bytes 1572872 | tf_op jit(solution)/shard_map/ppermute | solution.py:378
  11.5 0.5 collective-permute-start
  12.0 0.9 slice.160
  12.9 0.7 pad_add_fusion.refs_0_
  13.5 0.1 all-to-all-done.refs_1_
  13.6 0.0 copy-start
  13.6 0.6 copy-done
  14.2 4.1 %basis.2 = (f32[72,2048]{1,0:T(8,128)}, f32[48,2048]{1,0:T(8,128)}, bf16[256,2048]{1,0:T(8,128)(2,1)}, bf16[256,2048]{1,0:T(8,128)(2,1)}) custom-call(s32[3]{0:T(128)} %pad_add_fusion.refs_0_, f32[8,2,8,128]{3,2,1,0:T(8,128)} %copy-done), custom_call_target="tpu_custom_call" | custom-call | flops 4000000000 | bytes 400000 | tf_op jit(solution)/shard_map/basis/pallas_call | solution.py:404
  18.3 9.2 %spread.2 = f32[4,9,72,128]{3,2,1,0:T(8,128)} custom-call(f32[72,2048]{1,0:T(8,128)} %get-tuple-element.30.refs_0_.refs_3_, f32[48,2048]{1,0:T(8,128)} %get-tuple-element.31.refs_1_.refs_5_, bf16[256,2048]{1,0:T(8,128)(2,1)} %get-tuple-element.32.refs_2_.refs_7_, bf16[256,2048]{1,0:T(8,128)(2,1)} %get-tuple-element.33.refs_3_.refs_8_, ...), custom_call_target="tpu_custom_call" | custom-call | flops 8999999488 | bytes 900000 | tf_op jit(solution)/shard_map/spread/pallas_call | solution.py:425
  27.5 0.0 collective-permute-done.1
  27.5 3.7 %all-to-all-start.1 = ((f32[4,9,72,128]{3,2,1,0:T(8,128)}), f32[4,9,72,128]{3,2,1,0:T(8,128)S(1)}, u32[]{:S(2)}, u32[]{:S(2)}) async-start(f32[4,9,72,128]{3,2,1,0:T(8,128)} %spread.2), calls=%async_computation.1 | async-start | bytes 2654208 | tf_op jit(solution)/shard_map/all_to_all | solution.py:450
  31.2 0.7 slice_bitcast_fusion
  31.9 2.8 %collective-permute-start.5 = (f32[8,64,256]{2,1,0:T(8,128)}, f32[8,64,256]{2,1,0:T(8,128)}, u32[]{:S(2)}, u32[]{:S(2)}) collective-permute-start(f32[8,64,256]{2,1,0:T(8,128)} %collective-permute-done.1), channel_id=1, source_target_pairs={{0,7},{1,6},{2,5},{3,4},{4,3},{5,2},{6,1},{7,0},{8,15},{9,14},{10,... | collective-permute-start | bytes 1572872 | tf_op jit(solution)/shard_map/ppermute | solution.py:448
  34.7 8.6 %spread.3 = f32[4,8,72,128]{3,2,1,0:T(8,128)} custom-call(f32[72,2048]{1,0:T(8,128)} %get-tuple-element.30.refs_0_.refs_3_, f32[48,2048]{1,0:T(8,128)} %get-tuple-element.31.refs_1_.refs_5_, bf16[256,2048]{1,0:T(8,128)(2,1)} %get-tuple-element.32.refs_2_.refs_7_, bf16[256,2048]{1,0:T(8,128)(2,1)} %get-tuple-element.33.refs_3_.refs_8_, ...), custom_call_target="tpu_custom_call" | custom-call | flops 8999999488 | bytes 900000 | tf_op jit(solution)/shard_map/spread/pallas_call | solution.py:425
  43.3 0.0 copy-start.2
  43.3 0.0 copy-start.1
  43.3 0.8 collective-permute-start.6
  44.2 4.0 %basis.3 = (f32[72,2048]{1,0:T(8,128)}, f32[48,2048]{1,0:T(8,128)}, bf16[256,2048]{1,0:T(8,128)(2,1)}, bf16[256,2048]{1,0:T(8,128)(2,1)}) custom-call(s32[3]{0:T(128)} %pad_add_fusion.refs_0_, f32[8,2,8,128]{3,2,1,0:T(8,128)} %copy-done), custom_call_target="tpu_custom_call" | custom-call | flops 100000000 | bytes 10000 | tf_op jit(solution)/shard_map/basis/pallas_call | solution.py:404
  48.2 1.6 %all-to-all-done.1.lines = f32[4,9,72,128]{3,2,1,0:T(8,128)S(1)} async-done(((f32[4,9,72,128]{3,2,1,0:T(8,128)}), f32[4,9,72,128]{3,2,1,0:T(8,128)S(1)}, u32[]{:S(2)}, u32[]{:S(2)}) %all-to-all-start.1) | async-done | bytes 1327136 | tf_op jit(solution)/shard_map/all_to_all | solution.py:450
  49.8 3.8 %all-to-all-start.2 = ((f32[4,8,72,128]{3,2,1,0:T(8,128)}), f32[4,8,72,128]{3,2,1,0:T(8,128)S(1)}, u32[]{:S(2)}, u32[]{:S(2)}) async-start(f32[4,8,72,128]{3,2,1,0:T(8,128)} %spread.3), calls=%async_computation.2 | async-start | bytes 2359296 | tf_op jit(solution)/shard_map/all_to_all | solution.py:450
  53.7 0.0 copy-done.2
  53.7 0.0 collective-permute-done
  53.7 0.0 copy-done.1
  53.7 3.0 %collective-permute-start.3 = (f32[8,2,8,128]{3,2,1,0:T(8,128)S(1)}, f32[8,2,8,128]{3,2,1,0:T(8,128)S(1)}, u32[]{:S(2)}, u32[]{:S(2)}) collective-permute-start(f32[8,2,8,128]{3,2,1,0:T(8,128)S(1)} %copy-done.1), channel_id=1, source_target_pairs={{8,0},{16,8},{24,16},{0,24},{9,1},{17,9},{25,17},{1,25},{10,2},{18... | collective-permute-start | bytes 196616 | tf_op jit(solution)/shard_map/ppermute | solution.py:456
  56.7 0.0 collective-permute-start.2
  56.7 2.1 %collective-permute-start.4 = (f32[8,64,256]{2,1,0:T(8,128)}, f32[8,64,256]{2,1,0:T(8,128)}, u32[]{:S(2)}, u32[]{:S(2)}) collective-permute-start(f32[8,64,256]{2,1,0:T(8,128)} %collective-permute-done), channel_id=1, source_target_pairs={{0,7},{1,6},{2,5},{3,4},{4,3},{5,2},{6,1},{7,0},{8,15},{9,14},{10,... | collective-permute-start | bytes 1572872 | tf_op jit(solution)/shard_map/ppermute | solution.py:452
  58.8 0.0 collective-permute-done.6.refs_3_
  58.8 0.0 collective-permute-done.5.refs_2_
  58.8 4.0 %influence.3.factor = f32[9,256,128]{2,1,0:T(8,128)} custom-call(s32[3]{0:T(128)} %pad_add_fusion.refs_0_, f32[32,64,256]{2,1,0:T(8,128)} %refs_1_.3, f32[8,64,256]{2,1,0:T(8,128)} %collective-permute-done.5.refs_2_, f32[16,1,256]{2,1,0:T(1,128)S(1)} %collective-permute-done.6.refs_3_, bf16[128,64]{1,0:T(8,128)(2,1)} %constant.187.refs_4_, ...), custom_call_target="tpu_custom_call" | custom-call | flops 3500000000 | bytes 350000 | tf_op jit(solution)/shard_map/influence/pallas_call | solution.py:459
  62.8 4.8 %filter.3 = f32[4,9,72,128]{3,2,1,0:T(8,128)} custom-call(f32[4,9,72,128]{3,2,1,0:T(8,128)S(1)} %all-to-all-done.1.lines, f32[9,256,128]{2,1,0:T(8,128)} %influence.3.factor, bf16[512,256]{1,0:T(8,128)(2,1)} %constant.190.th, bf16[512,256]{1,0:T(8,128)(2,1)} %constant.193.tl), custom_call_target="tpu_custom_call" | custom-call | flops 5500000256 | bytes 550000 | tf_op jit(solution)/shard_map/filter/pallas_call | solution.py:475
  67.6 2.6 %all-to-all-done.2.lines = f32[4,8,72,128]{3,2,1,0:T(8,128)S(1)} async-done(((f32[4,8,72,128]{3,2,1,0:T(8,128)}), f32[4,8,72,128]{3,2,1,0:T(8,128)S(1)}, u32[]{:S(2)}, u32[]{:S(2)}) %all-to-all-start.2) | async-done | bytes 1179680 | tf_op jit(solution)/shard_map/all_to_all | solution.py:450
  70.1 3.7 %all-to-all-start.4 = ((f32[4,9,72,128]{3,2,1,0:T(8,128)}), f32[4,9,72,128]{3,2,1,0:T(8,128)S(1)}, u32[]{:S(2)}, u32[]{:S(2)}) async-start(f32[4,9,72,128]{3,2,1,0:T(8,128)} %filter.3), calls=%async_computation.4 | async-start | bytes 2654208 | tf_op jit(solution)/shard_map/all_to_all | solution.py:491
  73.8 0.0 collective-permute-done.3
  73.9 0.0 collective-permute-done.2
  73.9 0.2 convolution_bitcast_fusion
  74.2 3.0 %multiply_reduce_fusion.2 = (f32[128]{0:T(128)S(1)}, f32[128]{0:T(128)S(1)}, f32[128]{0:T(128)S(1)}) fusion(f32[8,128]{1,0:T(8,128)S(1)} %get-tuple-element.68, f32[128]{0:T(128)S(1)} %get-tuple-element.82, f32[8,128]{1,0:T(8,128)S(1)} %get-tuple-element.69, f32[128]{0:T(128)S(1)} %get-tuple-element.83, f32[8,128]{1,0:T(8,128)S(1)} %get-tuple-element.64, ...), kind=kLoop, calls=%fused_computation.35 | loop fusion | flops 14941824 | bytes 33792 | tf_op jit(solution)/shard_map/reduce_sum | solution.py:329
  77.1 3.0 %multiply_reduce_fusion.5 = (f32[128]{0:T(128)S(1)}, f32[128]{0:T(128)S(1)}, f32[128]{0:T(128)S(1)}) fusion(f32[8,128]{1,0:T(8,128)S(1)} %get-tuple-element.75, f32[128]{0:T(128)S(1)} %get-tuple-element.89, f32[8,128]{1,0:T(8,128)S(1)} %get-tuple-element.76, f32[128]{0:T(128)S(1)} %get-tuple-element.90, f32[8,128]{1,0:T(8,128)S(1)} %get-tuple-element.71, ...), kind=kLoop, calls=%fused_computation.63 | loop fusion | flops 14941824 | bytes 33792 | tf_op jit(solution)/shard_map/reduce_sum | solution.py:329
  80.1 0.0 collective-permute-done.4.refs_2_
  80.1 3.8 %influence.2.factor = f32[8,256,128]{2,1,0:T(8,128)} custom-call(s32[3]{0:T(128)} %pad_add_fusion.refs_0_, f32[32,64,256]{2,1,0:T(8,128)} %refs_1_.3, f32[8,64,256]{2,1,0:T(8,128)} %collective-permute-done.4.refs_2_, f32[16,1,256]{2,1,0:T(1,128)S(1)} %collective-permute-done.6.refs_3_, bf16[128,64]{1,0:T(8,128)(2,1)} %constant.187.refs_4_, ...), custom_call_target="tpu_custom_call" | custom-call | flops 3500000000 | bytes 350000 | tf_op jit(solution)/shard_map/influence/pallas_call | solution.py:459
  83.9 4.3 %filter.2 = f32[4,8,72,128]{3,2,1,0:T(8,128)} custom-call(f32[4,8,72,128]{3,2,1,0:T(8,128)S(1)} %all-to-all-done.2.lines, f32[8,256,128]{2,1,0:T(8,128)} %influence.2.factor, bf16[512,256]{1,0:T(8,128)(2,1)} %constant.190.th, bf16[512,256]{1,0:T(8,128)(2,1)} %constant.193.tl), custom_call_target="tpu_custom_call" | custom-call | flops 5500000256 | bytes 550000 | tf_op jit(solution)/shard_map/filter/pallas_call | solution.py:475
  88.2 2.1 %all-to-all-done.4.refs_0_ = f32[4,9,72,128]{3,2,1,0:T(8,128)S(1)} async-done(((f32[4,9,72,128]{3,2,1,0:T(8,128)}), f32[4,9,72,128]{3,2,1,0:T(8,128)S(1)}, u32[]{:S(2)}, u32[]{:S(2)}) %all-to-all-start.4) | async-done | bytes 1327136 | tf_op jit(solution)/shard_map/all_to_all | solution.py:491
  90.3 3.7 %all-to-all-start.3 = ((f32[4,8,72,128]{3,2,1,0:T(8,128)}), f32[4,8,72,128]{3,2,1,0:T(8,128)S(1)}, u32[]{:S(2)}, u32[]{:S(2)}) async-start(f32[4,8,72,128]{3,2,1,0:T(8,128)} %filter.2), calls=%async_computation.3 | async-start | bytes 2359296 | tf_op jit(solution)/shard_map/all_to_all | solution.py:491
  94.0 13.1 %gather.2.refs_11_ = f32[8,4,256]{2,1,0:T(4,128)} custom-call(f32[4,9,72,128]{3,2,1,0:T(8,128)S(1)} %all-to-all-done.4.refs_0_, bf16[512,512]{1,0:T(8,128)(2,1)} %constant.194.refs_1_, bf16[512,512]{1,0:T(8,128)(2,1)} %constant.197.refs_2_, f32[72,2048]{1,0:T(8,128)} %get-tuple-element.30.refs_0_.refs_3_, f32[72,2048]{1,0:T(8,128)} %get-tuple-element.49.refs_4_, ...), custom_call_target="tpu_custom_call" | custom-call | flops 12999999488 | bytes 1300000 | tf_op jit(solution)/shard_map/gather/pallas_call | solution.py:512
  107.1 1.0 all-to-all-done.3.refs_0_
  108.1 12.1 %gather.3 = f32[8,4,256]{2,1,0:T(4,128)} custom-call(f32[4,8,72,128]{3,2,1,0:T(8,128)S(1)} %all-to-all-done.3.refs_0_, bf16[512,512]{1,0:T(8,128)(2,1)} %constant.194.refs_1_, bf16[512,512]{1,0:T(8,128)(2,1)} %constant.197.refs_2_, f32[72,2048]{1,0:T(8,128)} %get-tuple-element.30.refs_0_.refs_3_, f32[72,2048]{1,0:T(8,128)} %get-tuple-element.49.refs_4_, ...), custom_call_target="tpu_custom_call" | custom-call | flops 12999999488 | bytes 1300000 | tf_op jit(solution)/shard_map/gather/pallas_call | solution.py:512
  120.2 4.8 %all-to-all-start.5 = ((f32[8,4,256]{2,1,0:T(4,128)}), f32[8,4,256]{2,1,0:T(4,128)S(1)}, u32[]{:S(2)}, u32[]{:S(2)}) async-start(f32[8,4,256]{2,1,0:T(4,128)} %gather.3), calls=%async_computation.5 | async-start | bytes 65536 | tf_op jit(solution)/shard_map/all_to_all | solution.py:525
  125.0 5.7 %all-to-all-done.5 = f32[8,4,256]{2,1,0:T(4,128)S(1)} async-done(((f32[8,4,256]{2,1,0:T(4,128)}), f32[8,4,256]{2,1,0:T(4,128)S(1)}, u32[]{:S(2)}, u32[]{:S(2)}) %all-to-all-start.5) | async-done | bytes 32800 | tf_op jit(solution)/shard_map/all_to_all | solution.py:525
  130.8 0.6 reshape.198
  (7 shorter events, 0.1 us)
Async XLA Ops:
  1.3 12.2 %all-to-all-start = ((f32[8,2,8,128]{3,2,1,0:T(8,128)}), f32[8,2,8,128]{3,2,1,0:T(8,128)S(1)}, u32[]{:S(2)}, u32[]{:S(2)}) async-start(f32[8,2,8,128]{3,2,1,0:T(8,128)} %pack.1), calls=%async_computation | async-start | bytes 131072 | tf_op jit(solution)/shard_map/all_to_all | solution.py:355
  9.0 18.5 %collective-permute-start.1 = (f32[8,64,256]{2,1,0:T(8,128)S(1)}, f32[8,64,256]{2,1,0:T(8,128)}, u32[]{:S(2)}, u32[]{:S(2)}) collective-permute-start(f32[8,64,256]{2,1,0:T(8,128)S(1)} %get-tuple-element.61), channel_id=1, source_target_pairs={{0,24},{8,16},{16,8},{24,0},{1,25},{9,17},{17,9},{25,1},{2,26},{10... | collective-permute-start | bytes 1572872 | tf_op jit(solution)/shard_map/ppermute | solution.py:378
  11.5 42.2 %collective-permute-start = (f32[8,64,256]{2,1,0:T(8,128)S(1)}, f32[8,64,256]{2,1,0:T(8,128)}, u32[]{:S(2)}, u32[]{:S(2)}) collective-permute-start(f32[8,64,256]{2,1,0:T(8,128)S(1)} %get-tuple-element.62), channel_id=1, source_target_pairs={{0,24},{8,16},{16,8},{24,0},{1,25},{9,17},{17,9},{25,1},{2,26},{10... | collective-permute-start | bytes 1572872 | tf_op jit(solution)/shard_map/ppermute | solution.py:378
  13.6 0.6 copy-start
  27.5 22.3 %all-to-all-start.1 = ((f32[4,9,72,128]{3,2,1,0:T(8,128)}), f32[4,9,72,128]{3,2,1,0:T(8,128)S(1)}, u32[]{:S(2)}, u32[]{:S(2)}) async-start(f32[4,9,72,128]{3,2,1,0:T(8,128)} %spread.2), calls=%async_computation.1 | async-start | bytes 2654208 | tf_op jit(solution)/shard_map/all_to_all | solution.py:450
  31.9 26.9 %collective-permute-start.5 = (f32[8,64,256]{2,1,0:T(8,128)}, f32[8,64,256]{2,1,0:T(8,128)}, u32[]{:S(2)}, u32[]{:S(2)}) collective-permute-start(f32[8,64,256]{2,1,0:T(8,128)} %collective-permute-done.1), channel_id=1, source_target_pairs={{0,7},{1,6},{2,5},{3,4},{4,3},{5,2},{6,1},{7,0},{8,15},{9,14},{10,... | collective-permute-start | bytes 1572872 | tf_op jit(solution)/shard_map/ppermute | solution.py:448
  43.3 10.3 %copy-start.2 = (s32[1,1,2,8]{3,2,1,0:T(2,128)S(1)}, s32[1,1,2,8]{3,2,1,0:T(2,128)}, u32[]{:S(2)}) copy-start(s32[1,1,2,8]{3,2,1,0:T(2,128)} %param.15) | copy-start | bytes 196
  43.3 10.4 %copy-start.1 = (f32[8,2,8,128]{3,2,1,0:T(8,128)S(1)}, f32[8,2,8,128]{3,2,1,0:T(8,128)}, u32[]{:S(2)}) copy-start(f32[8,2,8,128]{3,2,1,0:T(8,128)} %copy-done) | copy-start | bytes 196612
  43.3 15.4 %collective-permute-start.6 = (f32[16,1,256]{2,1,0:T(1,128)S(1)}, f32[16,1,256]{2,1,0:T(1,128)S(1)}, u32[]{:S(2)}, u32[]{:S(2)}) collective-permute-start(f32[16,1,256]{2,1,0:T(1,128)S(1)} %slice.160), channel_id=1, source_target_pairs={{0,7},{1,6},{2,5},{3,4},{4,3},{5,2},{6,1},{7,0},{8,31},{9,30},{10,... | collective-permute-start | bytes 49160 | tf_op jit(solution)/shard_map/ppermute | solution.py:449
  49.8 20.3 %all-to-all-start.2 = ((f32[4,8,72,128]{3,2,1,0:T(8,128)}), f32[4,8,72,128]{3,2,1,0:T(8,128)S(1)}, u32[]{:S(2)}, u32[]{:S(2)}) async-start(f32[4,8,72,128]{3,2,1,0:T(8,128)} %spread.3), calls=%async_computation.2 | async-start | bytes 2359296 | tf_op jit(solution)/shard_map/all_to_all | solution.py:450
  53.7 20.1 %collective-permute-start.3 = (f32[8,2,8,128]{3,2,1,0:T(8,128)S(1)}, f32[8,2,8,128]{3,2,1,0:T(8,128)S(1)}, u32[]{:S(2)}, u32[]{:S(2)}) collective-permute-start(f32[8,2,8,128]{3,2,1,0:T(8,128)S(1)} %copy-done.1), channel_id=1, source_target_pairs={{8,0},{16,8},{24,16},{0,24},{9,1},{17,9},{25,17},{1,25},{10,2},{18... | collective-permute-start | bytes 196616 | tf_op jit(solution)/shard_map/ppermute | solution.py:456
  56.7 17.2 %collective-permute-start.2 = (f32[8,2,8,128]{3,2,1,0:T(8,128)S(1)}, f32[8,2,8,128]{3,2,1,0:T(8,128)S(1)}, u32[]{:S(2)}, u32[]{:S(2)}) collective-permute-start(f32[8,2,8,128]{3,2,1,0:T(8,128)S(1)} %copy-done.1), channel_id=1, source_target_pairs={{0,8},{8,16},{16,24},{24,0},{1,9},{9,17},{17,25},{25,1},{2,10},{10... | collective-permute-start | bytes 196616 | tf_op jit(solution)/shard_map/ppermute | solution.py:456
  56.7 23.4 %collective-permute-start.4 = (f32[8,64,256]{2,1,0:T(8,128)}, f32[8,64,256]{2,1,0:T(8,128)}, u32[]{:S(2)}, u32[]{:S(2)}) collective-permute-start(f32[8,64,256]{2,1,0:T(8,128)} %collective-permute-done), channel_id=1, source_target_pairs={{0,7},{1,6},{2,5},{3,4},{4,3},{5,2},{6,1},{7,0},{8,15},{9,14},{10,... | collective-permute-start | bytes 1572872 | tf_op jit(solution)/shard_map/ppermute | solution.py:452
  70.1 20.2 %all-to-all-start.4 = ((f32[4,9,72,128]{3,2,1,0:T(8,128)}), f32[4,9,72,128]{3,2,1,0:T(8,128)S(1)}, u32[]{:S(2)}, u32[]{:S(2)}) async-start(f32[4,9,72,128]{3,2,1,0:T(8,128)} %filter.3), calls=%async_computation.4 | async-start | bytes 2654208 | tf_op jit(solution)/shard_map/all_to_all | solution.py:491
  90.3 17.9 %all-to-all-start.3 = ((f32[4,8,72,128]{3,2,1,0:T(8,128)}), f32[4,8,72,128]{3,2,1,0:T(8,128)S(1)}, u32[]{:S(2)}, u32[]{:S(2)}) async-start(f32[4,8,72,128]{3,2,1,0:T(8,128)} %filter.2), calls=%async_computation.3 | async-start | bytes 2359296 | tf_op jit(solution)/shard_map/all_to_all | solution.py:491
  120.2 10.5 %all-to-all-start.5 = ((f32[8,4,256]{2,1,0:T(4,128)}), f32[8,4,256]{2,1,0:T(4,128)S(1)}, u32[]{:S(2)}, u32[]{:S(2)}) async-start(f32[8,4,256]{2,1,0:T(4,128)} %gather.3), calls=%async_computation.5 | async-start | bytes 65536 | tf_op jit(solution)/shard_map/all_to_all | solution.py:525

commit v5 on v4

--- a/solution.py
+++ b/solution.py
@@ -9,7 +9,7 @@
 from jax.sharding import PartitionSpec as P
 
 BLOCK = 128
-XROWS = 8
+PAST = 3
 CHUNKS = 2
 VMEM = 56 * 1024 * 1024
 SPREAD_GROUP = 5
@@ -142,8 +142,10 @@
 
 def spread_kernel(first, count, slots_padded, wx, zq, bwh, bwl, rh, rl, ih, il, out, *sums):
     step = pl.program_id(0)
-    wide = wx[...]
-    extent = wide.shape[0]
+    padded = -(-count // 8) * 8
+    width = sums[0].shape[0] - PAST * padded
+    width = width // count
+    wide = wx[0:width, :]
     right = (bwh[...], bwl[...])
 
     @pl.when(step == 0)
@@ -154,21 +156,23 @@
     for low, high in groups(count, SPREAD_GROUP):
         pieces = []
         for c in range(2):
-            for g in range(low, high):
-                at = c * slots_padded + first + g
-                pieces.append(wide * zq[at : at + 1, :])
+            base = c * slots_padded + first
+            pieces += [wide * zq[base + g : base + g + 1, :] for g in range(low, high)]
+            if high == count:
+                strip = zq[base : base + padded, :]
+                pieces += [wx[width + i : width + i + 1, :] * strip for i in range(PAST)]
         part = dot3(split(jnp.concatenate(pieces, axis=0)), right, 1)
-        rows = (high - low) * extent
+        rows = part.shape[0] // 2
         for c in range(2):
-            sums[c][low * extent : high * extent, :] += part[c * rows : (c + 1) * rows]
+            sums[c][low * width : low * width + rows, :] += part[c * rows : (c + 1) * rows]
 
     @pl.when(step == pl.num_programs(0) - 1)
     def _():
         real, imag = (split(acc[...]) for acc in sums)
         lines = dot3(real, (rh[...], rl[...])) + dot3(imag, (ih[...], il[...]))
-        lanes = out.shape[3]
+        lanes = out.shape[2]
         for s in range(out.shape[0]):
-            out[s] = lines[:, s * lanes : (s + 1) * lanes].reshape(out.shape[1:])
+            out[s] = lines[:, s * lanes : (s + 1) * lanes]
 
 
 def influence_kernel(first, half, scale, where_ref, own, across, edge, flip, same, back, out):
@@ -197,18 +201,22 @@
 
 
 def filter_kernel(lines, factor, th, tl, out):
-    sects, count, extent, lanes = lines.shape
-    width = extent - XROWS
-    mesh_size = sects * width
+    sects, extent, lanes = lines.shape
+    count, mesh_size, _ = factor.shape
+    width = mesh_size // sects
+    past = count * width
+    padded = (extent - past) // PAST
+    empty = jnp.zeros((8 - PAST, lanes), jnp.float32)
     table = (th[...], tl[...])
     columns = []
     for g in range(count):
         pieces = []
         for s in range(sects):
-            body = lines[s, g]
-            before = lines[(s - 1) % sects, g, width:extent, :]
-            pieces.append(body[0:XROWS] + before)
-            pieces.append(body[XROWS:width])
+            before = [past + i * padded + g for i in range(PAST)]
+            before = [lines[(s - 1) % sects, at : at + 1, :] for at in before]
+            at = g * width
+            pieces.append(lines[s, at : at + 8, :] + jnp.concatenate(before + [empty], axis=0))
+            pieces.append(lines[s, at + 8 : at + width, :])
         columns.append(jnp.concatenate(pieces, axis=0))
     both = dot3(table, split(jnp.concatenate(columns, axis=1)))
     half = lanes // 2
@@ -221,55 +229,76 @@
         sin = both[mesh_size:, g * lanes : (g + 1) * lanes]
         columns.append((cos + sign * pltpu.roll(sin, half, 1)) * factor[g])
     both = dot3(table, split(jnp.concatenate(columns, axis=1)))
+    out[:, past:, :] = jnp.zeros((sects, extent - past, lanes), jnp.float32)
     for g in range(count):
         cos = both[0:mesh_size, g * lanes : (g + 1) * lanes]
         sin = both[mesh_size:, g * lanes : (g + 1) * lanes]
         field = cos - sign * pltpu.roll(sin, half, 1)
         for s in range(sects):
             after = ((s + 1) % sects) * width
-            out[s, g, 0:width, :] = field[s * width : (s + 1) * width]
-            out[s, g, width:extent, :] = field[after : after + XROWS]
+            out[s, g * width : (g + 1) * width, :] = field[s * width : (s + 1) * width]
+            for i in range(PAST):
+                at = past + i * padded + g
+                out[s, at : at + 1, :] = field[after + i : after + i + 1]
 
 
 def gather_kernel(first, count, slots_padded, lines, bh, bl, wx, vx, zq, zv, bwh, bwl, bvh, bvl, *rest):
     *earlier, out, eh, el = rest
-    sects, _, extent, lanes = lines.shape
-    rows = count * extent
+    sects, extent, lanes = lines.shape
     mesh_size = bwh.shape[0]
+    width = mesh_size // sects
+    past = count * width
+    padded = (extent - past) // PAST
 
     @pl.when(pl.program_id(0) == 0)
     def _():
-        joined = jnp.concatenate([lines[s].reshape(rows, lanes) for s in range(sects)], axis=1)
+        joined = jnp.concatenate([lines[s] for s in range(sects)], axis=1)
         field = dot3(split(joined), (bh[...], bl[...]))
         pieces = []
         for g in range(count):
             for c in range(2):
-                line = field[g * extent : (g + 1) * extent, c * mesh_size : (c + 1) * mesh_size]
+                line = field[g * width : (g + 1) * width, c * mesh_size : (c + 1) * mesh_size]
                 pieces.append(line)
+        pieces += [field[past:, c * mesh_size : (c + 1) * mesh_size] for c in range(2)]
         high, low = split(jnp.concatenate(pieces, axis=0))
         eh[...] = high
         el[...] = low
 
     weights = (bwh[...], bwl[...])
     slopes = (bvh[...], bvl[...])
-    sums = [jnp.zeros(wx.shape, jnp.float32) for _ in range(3)]
+    steps = wx.shape[1]
+    sums = [jnp.zeros((width, steps), jnp.float32) for _ in range(3)]
+    strips = [[jnp.zeros((padded, steps), jnp.float32)] * PAST for _ in range(3)]
     for low, high in groups(count, GATHER_GROUP):
-        part = slice(2 * low * extent, 2 * high * extent)
+        part = slice(2 * low * width, 2 * (high * width if high < count else extent))
         left = (eh[part, :], el[part, :])
         along = dot3(left, weights)
         slope = dot3(left, slopes)
         for g in range(low, high):
             for c in range(2):
                 at = c * slots_padded + first + g
-                base = (2 * (g - low) + c) * extent
-                line = along[base : base + extent]
+                base = (2 * (g - low) + c) * width
+                line = along[base : base + width]
                 sums[0] = sums[0] + line * zq[at : at + 1, :]
-                sums[1] = sums[1] + slope[base : base + extent] * zq[at : at + 1, :]
+                sums[1] = sums[1] + slope[base : base + width] * zq[at : at + 1, :]
                 sums[2] = sums[2] + line * zv[at : at + 1, :]
-    forces = [
-        -jnp.sum(total * shape[...], axis=0, keepdims=True)
-        for total, shape in zip(sums, (vx, wx, wx))
-    ]
+        if high == count:
+            for c in range(2):
+                at = c * slots_padded + first
+                for i in range(PAST):
+                    base = 2 * (high - low) * width + (c * PAST + i) * padded
+                    line = along[base : base + padded]
+                    other = slope[base : base + padded]
+                    strips[0][i] = strips[0][i] + line * zq[at : at + padded, :]
+                    strips[1][i] = strips[1][i] + other * zq[at : at + padded, :]
+                    strips[2][i] = strips[2][i] + line * zv[at : at + padded, :]
+    forces = []
+    for body, strip, shape in zip(sums, strips, (vx, wx, wx)):
+        force = jnp.sum(body * shape[0:width, :], axis=0, keepdims=True)
+        for i in range(PAST):
+            at = width + i
+            force = force + shape[at : at + 1, :] * jnp.sum(strip[i], axis=0, keepdims=True)
+        forces.append(-force)
     result = jnp.concatenate(forces + [jnp.zeros_like(forces[0])], axis=0)
     width = out.shape[2]
     for d in range(out.shape[0]):
@@ -340,8 +369,10 @@
     listed_count = pair_blocks.shape[3]
     half = z_width // 2
     slots = half + 1
-    slots_padded = -(-slots // 8) * 8
-    extent = x_width + XROWS
+    firsts = [-(-slots * n // CHUNKS) for n in range(CHUNKS + 1)]
+    counts = [b - a for a, b in zip(firsts, firsts[1:])]
+    padded = [-(-count // 8) * 8 for count in counts]
+    slots_padded = -(-max(a + b for a, b in zip(firsts, padded)) // 8) * 8
     lanes = 2 * x_width
     total = doms * atom_count
     where_am_i = jnp.stack([sect, dom, (dom >= doms // 2).astype(jnp.int32)])
@@ -366,8 +397,6 @@
     same = np.eye(mesh_size, dtype=np.float32)
     back = np.roll(same[::-1], 1, axis=0)
     flip, same, back = (jnp.asarray(m).astype(jnp.bfloat16) for m in (flip, same, back))
-    firsts = [-(-slots * n // CHUNKS) for n in range(CHUNKS + 1)]
-    counts = [b - a for a, b in zip(firsts, firsts[1:])]
     planes = []
     for first, count in zip(firsts, counts):
         lowest = half - max(first + count - 1, 1)
@@ -394,7 +423,7 @@
     atom_step = 512
     grid = (total // atom_step,)
     shapes = [
-        ((extent, total), f32),
+        ((x_width + 8, total), f32),
         ((2 * slots_padded, total), f32),
         ((mesh_size, total), bf16),
         ((mesh_size, total), bf16),
@@ -421,20 +450,21 @@
 
     sent = []
     for first, count in zip(firsts, counts):
-        shape = (sects, count, extent, lanes)
+        extent = count * x_width + PAST * (-(-count // 8) * 8)
+        shape = (sects, extent, lanes)
         lines = pl.pallas_call(
             lambda *refs, first=first, count=count: spread_kernel(first, count, slots_padded, *refs),
             grid=grid,
             in_specs=[
-                along_atoms(extent, atom_step),
+                along_atoms(x_width + 8, atom_step),
                 along_atoms(2 * slots_padded, atom_step),
                 along_atoms(mesh_size, atom_step),
                 along_atoms(mesh_size, atom_step),
             ]
             + [whole(t) for t in (rh, rl, ih, il)],
-            out_specs=pl.BlockSpec(shape, lambda n: (0, 0, 0, 0)),
+            out_specs=pl.BlockSpec(shape, lambda n: (0, 0, 0)),
             out_shape=jax.ShapeDtypeStruct(shape, f32),
-            scratch_shapes=[pltpu.VMEM((count * extent, mesh_size), f32)] * 2,
+            scratch_shapes=[pltpu.VMEM((extent, mesh_size), f32)] * 2,
             compiler_params=params(),
             cost_estimate=cost(9),
             name="spread",
@@ -517,7 +547,7 @@
             + [by_dom] * len(earlier),
             out_specs=by_dom,
             out_shape=jax.ShapeDtypeStruct((doms, 4, atom_count), f32),
-            scratch_shapes=[pltpu.VMEM((2 * count * extent, mesh_size), bf16)] * 2,
+            scratch_shapes=[pltpu.VMEM((2 * lines.shape[1], mesh_size), bf16)] * 2,
             compiler_params=params(),
             cost_estimate=cost(13),
             name="gather",

time: 133 us -> 131 us (0.985)
  Pallas kernels: 69.3 us -> 67.8 us
    ppermute x1, starting transfers between devices: 2.79 us -> 0.69 us  [shards(): planes[0] = lax.ppermute(planes[0], 'dom', dom_flip)]
    ppermute x1, starting transfers between devices: 0.82 us -> 2.91 us  [shards(): edge = lax.ppermute(corner, ('sect', 'dom'), edges)]
  transfers between devices with their start and end apart: 13 -> 13, of which waited for: 6 -> 5; matrix products, arithmetic and copies ran while one was open for 7% -> 8% of each run, Pallas kernels for 43% -> 42%
where the time goes in v5:
time: 131 us; the launch traced here: 130 us
  Pallas kernels  67.8 us (52%)
  starting transfers between devices  38.9 us (30%)
  waiting for transfers between devices  12.2 us (9%)
  other arithmetic  6.68 us (5%)
  local copies, waits for them, and re-layouts  4.14 us (3%)
    pallas_call x2, Pallas kernels, shards(): pl.pallas_call(lambda *refs, first=first, count=count: gather_kernel(firs...  24.4 us
    pallas_call x2, Pallas kernels, shards(): pl.pallas_call(lambda *refs, first=first, count=count: spread_kernel(firs...  17.2 us
    pallas_call x2, Pallas kernels, shards(): pl.pallas_call(filter_kernel, grid=(1,), in_specs=[IN_VMEM, IN_VMEM, whol...  9.05 us
    pallas_call x2, Pallas kernels, basis(): pl.pallas_call(lambda *refs: basis_kernel(which, mesh_size, x_width, z_wi...  8.11 us
    all_to_all x2, starting transfers between devices, shards(): lax.all_to_all(lines, 'sect', split_axis=0, concat_axis=0, tiled=True)  7.71 us
    pallas_call x2, Pallas kernels, folded(): pl.pallas_call(lambda *refs: influence_kernel(first, half, float(mesh_siz...  7.68 us
    all_to_all x2, starting transfers between devices, shards(): lax.all_to_all(field, 'sect', split_axis=0, concat_axis=0, tiled=True)  7.46 us
    all_to_all x1, starting transfers between devices, shards(): row = lax.all_to_all(copies, 'dom', 0, 0, tiled=True)  6.33 us
  transfers between devices with their start and end apart: 13, of which 5 were waited for; matrix products, arithmetic and copies ran while one was open for 8% of the time, Pallas kernels for 42%

profile of v5, /device:TPU:0, one launch (start us, length us, event | category | flops | bytes accessed | tf_op | source)
XLA Modules:
  0.0 130.0 jit_solution(706967841164236638)
XLA Ops:
  0.0 1.3 %pack.1 = f32[8,2,8,128]{3,2,1,0:T(8,128)} custom-call(s32[3,1,1,256]{3,2,1,0:T(1,128)} %cells.1, f32[3,1,1,256]{3,2,1,0:T(1,128)} %fracs.1, f32[1,1,256]{2,1,0:T(1,128)} %charges.1), custom_call_target="tpu_custom_call" | custom-call | tf_op jit(solution)/shard_map/pack/pallas_call | solution.py:381
  1.3 6.3 %all-to-all-start = ((f32[8,2,8,128]{3,2,1,0:T(8,128)}), f32[8,2,8,128]{3,2,1,0:T(8,128)S(1)}, u32[]{:S(2)}, u32[]{:S(2)}) async-start(f32[8,2,8,128]{3,2,1,0:T(8,128)} %pack.1), calls=%async_computation | async-start | bytes 131072 | tf_op jit(solution)/shard_map/all_to_all | solution.py:386
  7.7 1.3 fusion.66
  9.0 2.5 %collective-permute-start.1 = (f32[8,64,256]{2,1,0:T(8,128)S(1)}, f32[8,64,256]{2,1,0:T(8,128)}, u32[]{:S(2)}, u32[]{:S(2)}) collective-permute-start(f32[8,64,256]{2,1,0:T(8,128)S(1)} %get-tuple-element.61), channel_id=1, source_target_pairs={{0,24},{8,16},{16,8},{24,0},{1,25},{9,17},{17,9},{25,1},{2,26},{10... | collective-permute-start | bytes 1572872 | tf_op jit(solution)/shard_map/ppermute | solution.py:407
  11.5 0.5 collective-permute-start
  12.0 0.7 slice_bitcast_fusion
  12.7 0.9 slice.160
  13.6 0.7 pad_add_fusion.refs_0_
  14.2 0.0 all-to-all-done.refs_1_
  14.2 0.0 copy-start
  14.2 0.6 copy-done
  14.9 4.0 %basis.2 = (f32[72,2048]{1,0:T(8,128)}, f32[48,2048]{1,0:T(8,128)}, bf16[256,2048]{1,0:T(8,128)(2,1)}, bf16[256,2048]{1,0:T(8,128)(2,1)}) custom-call(s32[3]{0:T(128)} %pad_add_fusion.refs_0_, f32[8,2,8,128]{3,2,1,0:T(8,128)} %copy-done), custom_call_target="tpu_custom_call" | custom-call | flops 4000000000 | bytes 400000 | tf_op jit(solution)/shard_map/basis/pallas_call | solution.py:433
  18.9 9.0 %spread.2 = f32[4,624,128]{2,1,0:T(8,128)} custom-call(f32[72,2048]{1,0:T(8,128)} %get-tuple-element.30.refs_0_.refs_3_, f32[48,2048]{1,0:T(8,128)} %get-tuple-element.31.refs_1_.refs_5_, bf16[256,2048]{1,0:T(8,128)(2,1)} %get-tuple-element.32.refs_2_.refs_7_, bf16[256,2048]{1,0:T(8,128)(2,1)} %get-tuple-element.33.refs_3_.refs_8_, ...), custom_call_target="tpu_custom_call" | custom-call | flops 8999999488 | bytes 900000 | tf_op jit(solution)/shard_map/spread/pallas_call | solution.py:455
  27.9 0.0 copy-start.2
  27.9 0.0 collective-permute-done.1
  28.0 3.7 %all-to-all-start.1 = ((f32[4,624,128]{2,1,0:T(8,128)}), f32[4,624,128]{2,1,0:T(8,128)S(1)}, u32[]{:S(2)}, u32[]{:S(2)}) async-start(f32[4,624,128]{2,1,0:T(8,128)} %spread.2), calls=%async_computation.1 | async-start | bytes 2555904 | tf_op jit(solution)/shard_map/all_to_all | solution.py:480
  31.7 0.0 copy-done.2
  31.7 2.9 %collective-permute-start.6 = (f32[16,1,256]{2,1,0:T(1,128)S(1)}, f32[16,1,256]{2,1,0:T(1,128)S(1)}, u32[]{:S(2)}, u32[]{:S(2)}) collective-permute-start(f32[16,1,256]{2,1,0:T(1,128)S(1)} %slice.160), channel_id=1, source_target_pairs={{0,7},{1,6},{2,5},{3,4},{4,3},{5,2},{6,1},{7,0},{8,31},{9,30},{10,... | collective-permute-start | bytes 49160 | tf_op jit(solution)/shard_map/ppermute | solution.py:479
  34.6 0.7 collective-permute-start.5
  35.3 8.2 %spread.3 = f32[4,536,128]{2,1,0:T(8,128)} custom-call(f32[72,2048]{1,0:T(8,128)} %get-tuple-element.30.refs_0_.refs_3_, f32[48,2048]{1,0:T(8,128)} %get-tuple-element.31.refs_1_.refs_5_, bf16[256,2048]{1,0:T(8,128)(2,1)} %get-tuple-element.32.refs_2_.refs_7_, bf16[256,2048]{1,0:T(8,128)(2,1)} %get-tuple-element.33.refs_3_.refs_8_, ...), custom_call_target="tpu_custom_call" | custom-call | flops 8999999488 | bytes 900000 | tf_op jit(solution)/shard_map/spread/pallas_call | solution.py:455
  43.5 0.0 copy-start.1
  43.5 4.1 %basis.3 = (f32[72,2048]{1,0:T(8,128)}, f32[48,2048]{1,0:T(8,128)}, bf16[256,2048]{1,0:T(8,128)(2,1)}, bf16[256,2048]{1,0:T(8,128)(2,1)}) custom-call(s32[3]{0:T(128)} %pad_add_fusion.refs_0_, f32[8,2,8,128]{3,2,1,0:T(8,128)} %copy-done), custom_call_target="tpu_custom_call" | custom-call | flops 100000000 | bytes 10000 | tf_op jit(solution)/shard_map/basis/pallas_call | solution.py:433
  47.6 1.7 %all-to-all-done.1.lines = f32[4,624,128]{2,1,0:T(8,128)S(1)} async-done(((f32[4,624,128]{2,1,0:T(8,128)}), f32[4,624,128]{2,1,0:T(8,128)S(1)}, u32[]{:S(2)}, u32[]{:S(2)}) %all-to-all-start.1) | async-done | bytes 1277984 | tf_op jit(solution)/shard_map/all_to_all | solution.py:480
  49.3 4.0 %all-to-all-start.2 = ((f32[4,536,128]{2,1,0:T(8,128)}), f32[4,536,128]{2,1,0:T(8,128)S(1)}, u32[]{:S(2)}, u32[]{:S(2)}) async-start(f32[4,536,128]{2,1,0:T(8,128)} %spread.3), calls=%async_computation.2 | async-start | bytes 2195456 | tf_op jit(solution)/shard_map/all_to_all | solution.py:480
  53.3 0.0 collective-permute-done
  53.3 0.0 copy-done.1
  53.3 2.9 %collective-permute-start.3 = (f32[8,2,8,128]{3,2,1,0:T(8,128)S(1)}, f32[8,2,8,128]{3,2,1,0:T(8,128)S(1)}, u32[]{:S(2)}, u32[]{:S(2)}) collective-permute-start(f32[8,2,8,128]{3,2,1,0:T(8,128)S(1)} %copy-done.1), channel_id=1, source_target_pairs={{8,0},{16,8},{24,16},{0,24},{9,1},{17,9},{25,17},{1,25},{10,2},{18... | collective-permute-start | bytes 196616 | tf_op jit(solution)/shard_map/ppermute | solution.py:486
  56.2 0.0 collective-permute-start.2
  56.2 2.2 %collective-permute-start.4 = (f32[8,64,256]{2,1,0:T(8,128)S(1)}, f32[8,64,256]{2,1,0:T(8,128)}, u32[]{:S(2)}, u32[]{:S(2)}) collective-permute-start(f32[8,64,256]{2,1,0:T(8,128)S(1)} %collective-permute-done), channel_id=1, source_target_pairs={{0,7},{1,6},{2,5},{3,4},{4,3},{5,2},{6,1},{7,0},{8,15},{9,14},{10,... | collective-permute-start | bytes 1572872 | tf_op jit(solution)/shard_map/ppermute | solution.py:482
  58.4 0.0 collective-permute-done.6.refs_3_
  58.4 0.0 collective-permute-done.5.refs_2_
  58.4 3.9 %influence.3.factor = f32[9,256,128]{2,1,0:T(8,128)} custom-call(s32[3]{0:T(128)} %pad_add_fusion.refs_0_, f32[32,64,256]{2,1,0:T(8,128)} %refs_1_.3, f32[8,64,256]{2,1,0:T(8,128)} %collective-permute-done.5.refs_2_, f32[16,1,256]{2,1,0:T(1,128)S(1)} %collective-permute-done.6.refs_3_, bf16[128,64]{1,0:T(8,128)(2,1)} %constant.187.refs_4_, ...), custom_call_target="tpu_custom_call" | custom-call | flops 3500000000 | bytes 350000 | tf_op jit(solution)/shard_map/influence/pallas_call | solution.py:489
  62.4 4.8 %filter.3 = f32[4,624,128]{2,1,0:T(8,128)} custom-call(f32[4,624,128]{2,1,0:T(8,128)S(1)} %all-to-all-done.1.lines, f32[9,256,128]{2,1,0:T(8,128)} %influence.3.factor, bf16[512,256]{1,0:T(8,128)(2,1)} %constant.190.th, bf16[512,256]{1,0:T(8,128)(2,1)} %constant.193.tl), custom_call_target="tpu_custom_call" | custom-call | flops 5500000256 | bytes 550000 | tf_op jit(solution)/shard_map/filter/pallas_call | solution.py:505
  67.1 1.7 %all-to-all-done.2.lines = f32[4,536,128]{2,1,0:T(8,128)S(1)} async-done(((f32[4,536,128]{2,1,0:T(8,128)}), f32[4,536,128]{2,1,0:T(8,128)S(1)}, u32[]{:S(2)}, u32[]{:S(2)}) %all-to-all-start.2) | async-done | bytes 1097760 | tf_op jit(solution)/shard_map/all_to_all | solution.py:480
  68.8 3.7 %all-to-all-start.4 = ((f32[4,624,128]{2,1,0:T(8,128)}), f32[4,624,128]{2,1,0:T(8,128)S(1)}, u32[]{:S(2)}, u32[]{:S(2)}) async-start(f32[4,624,128]{2,1,0:T(8,128)} %filter.3), calls=%async_computation.4 | async-start | bytes 2555904 | tf_op jit(solution)/shard_map/all_to_all | solution.py:521
  72.5 0.0 collective-permute-done.3
  72.5 0.0 collective-permute-done.2
  72.6 0.2 convolution_bitcast_fusion
  72.8 3.0 %multiply_reduce_fusion.2 = (f32[128]{0:T(128)S(1)}, f32[128]{0:T(128)S(1)}, f32[128]{0:T(128)S(1)}) fusion(f32[8,128]{1,0:T(8,128)S(1)} %get-tuple-element.68, f32[128]{0:T(128)S(1)} %get-tuple-element.82, f32[8,128]{1,0:T(8,128)S(1)} %get-tuple-element.69, f32[128]{0:T(128)S(1)} %get-tuple-element.83, f32[8,128]{1,0:T(8,128)S(1)} %get-tuple-element.64, ...), kind=kLoop, calls=%fused_computation.35 | loop fusion | flops 14941824 | bytes 33792 | tf_op jit(solution)/shard_map/reduce_sum | solution.py:358
  75.8 3.0 %multiply_reduce_fusion.5 = (f32[128]{0:T(128)S(1)}, f32[128]{0:T(128)S(1)}, f32[128]{0:T(128)S(1)}) fusion(f32[8,128]{1,0:T(8,128)S(1)} %get-tuple-element.75, f32[128]{0:T(128)S(1)} %get-tuple-element.89, f32[8,128]{1,0:T(8,128)S(1)} %get-tuple-element.76, f32[128]{0:T(128)S(1)} %get-tuple-element.90, f32[8,128]{1,0:T(8,128)S(1)} %get-tuple-element.71, ...), kind=kLoop, calls=%fused_computation.63 | loop fusion | flops 14941824 | bytes 33792 | tf_op jit(solution)/shard_map/reduce_sum | solution.py:358
  78.8 0.0 collective-permute-done.4.refs_2_
  78.8 3.8 %influence.2.factor = f32[8,256,128]{2,1,0:T(8,128)} custom-call(s32[3]{0:T(128)} %pad_add_fusion.refs_0_, f32[32,64,256]{2,1,0:T(8,128)} %refs_1_.3, f32[8,64,256]{2,1,0:T(8,128)} %collective-permute-done.4.refs_2_, f32[16,1,256]{2,1,0:T(1,128)S(1)} %collective-permute-done.6.refs_3_, bf16[128,64]{1,0:T(8,128)(2,1)} %constant.187.refs_4_, ...), custom_call_target="tpu_custom_call" | custom-call | flops 3500000000 | bytes 350000 | tf_op jit(solution)/shard_map/influence/pallas_call | solution.py:489
  82.5 4.3 %filter.2 = f32[4,536,128]{2,1,0:T(8,128)} custom-call(f32[4,536,128]{2,1,0:T(8,128)S(1)} %all-to-all-done.2.lines, f32[8,256,128]{2,1,0:T(8,128)} %influence.2.factor, bf16[512,256]{1,0:T(8,128)(2,1)} %constant.190.th, bf16[512,256]{1,0:T(8,128)(2,1)} %constant.193.tl), custom_call_target="tpu_custom_call" | custom-call | flops 5500000256 | bytes 550000 | tf_op jit(solution)/shard_map/filter/pallas_call | solution.py:505
  86.8 2.2 %all-to-all-done.4.refs_0_ = f32[4,624,128]{2,1,0:T(8,128)S(1)} async-done(((f32[4,624,128]{2,1,0:T(8,128)}), f32[4,624,128]{2,1,0:T(8,128)S(1)}, u32[]{:S(2)}, u32[]{:S(2)}) %all-to-all-start.4) | async-done | bytes 1277984 | tf_op jit(solution)/shard_map/all_to_all | solution.py:521
  89.0 3.7 %all-to-all-start.3 = ((f32[4,536,128]{2,1,0:T(8,128)}), f32[4,536,128]{2,1,0:T(8,128)S(1)}, u32[]{:S(2)}, u32[]{:S(2)}) async-start(f32[4,536,128]{2,1,0:T(8,128)} %filter.2), calls=%async_computation.3 | async-start | bytes 2195456 | tf_op jit(solution)/shard_map/all_to_all | solution.py:521
  92.7 12.8 %gather.2.refs_11_ = f32[8,4,256]{2,1,0:T(4,128)} custom-call(f32[4,624,128]{2,1,0:T(8,128)S(1)} %all-to-all-done.4.refs_0_, bf16[512,512]{1,0:T(8,128)(2,1)} %constant.194.refs_1_, bf16[512,512]{1,0:T(8,128)(2,1)} %constant.197.refs_2_, f32[72,2048]{1,0:T(8,128)} %get-tuple-element.30.refs_0_.refs_3_, f32[72,2048]{1,0:T(8,128)} %get-tuple-element.49.refs_4_, ...), custom_call_target="tpu_custom_call" | custom-call | flops 12999999488 | bytes 1300000 | tf_op jit(solution)/shard_map/gather/pallas_call | solution.py:542
  105.5 0.9 all-to-all-done.3.refs_0_
  106.4 11.6 %gather.3 = f32[8,4,256]{2,1,0:T(4,128)} custom-call(f32[4,536,128]{2,1,0:T(8,128)S(1)} %all-to-all-done.3.refs_0_, bf16[512,512]{1,0:T(8,128)(2,1)} %constant.194.refs_1_, bf16[512,512]{1,0:T(8,128)(2,1)} %constant.197.refs_2_, f32[72,2048]{1,0:T(8,128)} %get-tuple-element.30.refs_0_.refs_3_, f32[72,2048]{1,0:T(8,128)} %get-tuple-element.49.refs_4_, ...), custom_call_target="tpu_custom_call" | custom-call | flops 12999999488 | bytes 1300000 | tf_op jit(solution)/shard_map/gather/pallas_call | solution.py:542
  118.0 5.7 %all-to-all-start.5 = ((f32[8,4,256]{2,1,0:T(4,128)}), f32[8,4,256]{2,1,0:T(4,128)S(1)}, u32[]{:S(2)}, u32[]{:S(2)}) async-start(f32[8,4,256]{2,1,0:T(4,128)} %gather.3), calls=%async_computation.5 | async-start | bytes 65536 | tf_op jit(solution)/shard_map/all_to_all | solution.py:555
  123.7 5.7 %all-to-all-done.5 = f32[8,4,256]{2,1,0:T(4,128)S(1)} async-done(((f32[8,4,256]{2,1,0:T(4,128)}), f32[8,4,256]{2,1,0:T(4,128)S(1)}, u32[]{:S(2)}, u32[]{:S(2)}) %all-to-all-start.5) | async-done | bytes 32800 | tf_op jit(solution)/shard_map/all_to_all | solution.py:555
  129.4 0.6 reshape.198
  (7 shorter events, 0.1 us)
Async XLA Ops:
  1.3 12.9 %all-to-all-start = ((f32[8,2,8,128]{3,2,1,0:T(8,128)}), f32[8,2,8,128]{3,2,1,0:T(8,128)S(1)}, u32[]{:S(2)}, u32[]{:S(2)}) async-start(f32[8,2,8,128]{3,2,1,0:T(8,128)} %pack.1), calls=%async_computation | async-start | bytes 131072 | tf_op jit(solution)/shard_map/all_to_all | solution.py:386
  9.0 19.0 %collective-permute-start.1 = (f32[8,64,256]{2,1,0:T(8,128)S(1)}, f32[8,64,256]{2,1,0:T(8,128)}, u32[]{:S(2)}, u32[]{:S(2)}) collective-permute-start(f32[8,64,256]{2,1,0:T(8,128)S(1)} %get-tuple-element.61), channel_id=1, source_target_pairs={{0,24},{8,16},{16,8},{24,0},{1,25},{9,17},{17,9},{25,1},{2,26},{10... | collective-permute-start | bytes 1572872 | tf_op jit(solution)/shard_map/ppermute | solution.py:407
  11.5 41.8 %collective-permute-start = (f32[8,64,256]{2,1,0:T(8,128)S(1)}, f32[8,64,256]{2,1,0:T(8,128)S(1)}, u32[]{:S(2)}, u32[]{:S(2)}) collective-permute-start(f32[8,64,256]{2,1,0:T(8,128)S(1)} %get-tuple-element.62), channel_id=1, source_target_pairs={{0,24},{8,16},{16,8},{24,0},{1,25},{9,17},{17,9},{25,1},{2,26},{10... | collective-permute-start | bytes 1572872 | tf_op jit(solution)/shard_map/ppermute | solution.py:407
  14.2 0.6 copy-start
  27.9 3.8 %copy-start.2 = (s32[1,1,2,8]{3,2,1,0:T(2,128)S(1)}, s32[1,1,2,8]{3,2,1,0:T(2,128)}, u32[]{:S(2)}) copy-start(s32[1,1,2,8]{3,2,1,0:T(2,128)} %param.15) | copy-start | bytes 196
  28.0 21.3 %all-to-all-start.1 = ((f32[4,624,128]{2,1,0:T(8,128)}), f32[4,624,128]{2,1,0:T(8,128)S(1)}, u32[]{:S(2)}, u32[]{:S(2)}) async-start(f32[4,624,128]{2,1,0:T(8,128)} %spread.2), calls=%async_computation.1 | async-start | bytes 2555904 | tf_op jit(solution)/shard_map/all_to_all | solution.py:480
  31.7 26.7 %collective-permute-start.6 = (f32[16,1,256]{2,1,0:T(1,128)S(1)}, f32[16,1,256]{2,1,0:T(1,128)S(1)}, u32[]{:S(2)}, u32[]{:S(2)}) collective-permute-start(f32[16,1,256]{2,1,0:T(1,128)S(1)} %slice.160), channel_id=1, source_target_pairs={{0,7},{1,6},{2,5},{3,4},{4,3},{5,2},{6,1},{7,0},{8,31},{9,30},{10,... | collective-permute-start | bytes 49160 | tf_op jit(solution)/shard_map/ppermute | solution.py:479
  34.6 23.8 %collective-permute-start.5 = (f32[8,64,256]{2,1,0:T(8,128)}, f32[8,64,256]{2,1,0:T(8,128)}, u32[]{:S(2)}, u32[]{:S(2)}) collective-permute-start(f32[8,64,256]{2,1,0:T(8,128)} %collective-permute-done.1), channel_id=1, source_target_pairs={{0,7},{1,6},{2,5},{3,4},{4,3},{5,2},{6,1},{7,0},{8,15},{9,14},{10,... | collective-permute-start | bytes 1572872 | tf_op jit(solution)/shard_map/ppermute | solution.py:478
  43.5 9.7 %copy-start.1 = (f32[8,2,8,128]{3,2,1,0:T(8,128)S(1)}, f32[8,2,8,128]{3,2,1,0:T(8,128)}, u32[]{:S(2)}) copy-start(f32[8,2,8,128]{3,2,1,0:T(8,128)} %copy-done) | copy-start | bytes 196612
  49.3 19.5 %all-to-all-start.2 = ((f32[4,536,128]{2,1,0:T(8,128)}), f32[4,536,128]{2,1,0:T(8,128)S(1)}, u32[]{:S(2)}, u32[]{:S(2)}) async-start(f32[4,536,128]{2,1,0:T(8,128)} %spread.3), calls=%async_computation.2 | async-start | bytes 2195456 | tf_op jit(solution)/shard_map/all_to_all | solution.py:480
  53.3 19.3 %collective-permute-start.3 = (f32[8,2,8,128]{3,2,1,0:T(8,128)S(1)}, f32[8,2,8,128]{3,2,1,0:T(8,128)S(1)}, u32[]{:S(2)}, u32[]{:S(2)}) collective-permute-start(f32[8,2,8,128]{3,2,1,0:T(8,128)S(1)} %copy-done.1), channel_id=1, source_target_pairs={{8,0},{16,8},{24,16},{0,24},{9,1},{17,9},{25,17},{1,25},{10,2},{18... | collective-permute-start | bytes 196616 | tf_op jit(solution)/shard_map/ppermute | solution.py:486
  56.2 16.4 %collective-permute-start.2 = (f32[8,2,8,128]{3,2,1,0:T(8,128)S(1)}, f32[8,2,8,128]{3,2,1,0:T(8,128)S(1)}, u32[]{:S(2)}, u32[]{:S(2)}) collective-permute-start(f32[8,2,8,128]{3,2,1,0:T(8,128)S(1)} %copy-done.1), channel_id=1, source_target_pairs={{0,8},{8,16},{16,24},{24,0},{1,9},{9,17},{17,25},{25,1},{2,10},{10... | collective-permute-start | bytes 196616 | tf_op jit(solution)/shard_map/ppermute | solution.py:486
  56.2 22.6 %collective-permute-start.4 = (f32[8,64,256]{2,1,0:T(8,128)S(1)}, f32[8,64,256]{2,1,0:T(8,128)}, u32[]{:S(2)}, u32[]{:S(2)}) collective-permute-start(f32[8,64,256]{2,1,0:T(8,128)S(1)} %collective-permute-done), channel_id=1, source_target_pairs={{0,7},{1,6},{2,5},{3,4},{4,3},{5,2},{6,1},{7,0},{8,15},{9,14},{10,... | collective-permute-start | bytes 1572872 | tf_op jit(solution)/shard_map/ppermute | solution.py:482
  68.8 20.2 %all-to-all-start.4 = ((f32[4,624,128]{2,1,0:T(8,128)}), f32[4,624,128]{2,1,0:T(8,128)S(1)}, u32[]{:S(2)}, u32[]{:S(2)}) async-start(f32[4,624,128]{2,1,0:T(8,128)} %filter.3), calls=%async_computation.4 | async-start | bytes 2555904 | tf_op jit(solution)/shard_map/all_to_all | solution.py:521
  89.0 17.4 %all-to-all-start.3 = ((f32[4,536,128]{2,1,0:T(8,128)}), f32[4,536,128]{2,1,0:T(8,128)S(1)}, u32[]{:S(2)}, u32[]{:S(2)}) async-start(f32[4,536,128]{2,1,0:T(8,128)} %filter.2), calls=%async_computation.3 | async-start | bytes 2195456 | tf_op jit(solution)/shard_map/all_to_all | solution.py:521
  118.0 11.4 %all-to-all-start.5 = ((f32[8,4,256]{2,1,0:T(4,128)}), f32[8,4,256]{2,1,0:T(4,128)S(1)}, u32[]{:S(2)}, u32[]{:S(2)}) async-start(f32[8,4,256]{2,1,0:T(4,128)} %gather.3), calls=%async_computation.5 | async-start | bytes 65536 | tf_op jit(solution)/shard_map/all_to_all | solution.py:555

commit v6 on v5

--- a/solution.py
+++ b/solution.py
@@ -384,7 +384,6 @@
         name="pack",
     )(cells, fracs, charges)
     row = lax.all_to_all(copies, "dom", 0, 0, tiled=True)
-    packed = copies[0]
 
     edges = []
     for s in range(sects):
@@ -420,7 +419,7 @@
     bh, bl = split_table(np.concatenate([by_sect(cos, -sin).T, by_sect(sin, cos).T], axis=1))
     th, tl = split_table(np.concatenate([cos, sin], axis=0))
 
-    atom_step = 512
+    atom_step = 1024
     grid = (total // atom_step,)
     shapes = [
         ((x_width + 8, total), f32),
@@ -470,9 +469,10 @@
             name="spread",
         )(wx, zq, bwh, bwl, rh, rl, ih, il)
         sent.append(lines)
-    corner, beside, planes[0], sent[0] = lax.optimization_barrier(
-        (influence[half:, 0:1], row, planes[0], sent[0])
-    )
+    later, beside, planes[0], sent[0] = lax.optimization_barrier(
+        (influence, row, planes[0], sent[0])
+    )
+    corner = later[half:, 0:1]
     vx, zv, bvh, bvl = basis(1, beside)
     vx, sent[-1] = lax.optimization_barrier((vx, sent[-1]))
     planes[0] = lax.ppermute(planes[0], "dom", dom_flip)
@@ -500,7 +500,8 @@
     for n in range(1, CHUNKS):
         factors.append(folded(firsts[n], counts[n], planes[n]))
     fields = []
-    near, row, packed, sent[-1] = lax.optimization_barrier((near, row, packed, sent[-1]))
+    near, row, copies, sent[-1] = lax.optimization_barrier((near, row, copies, sent[-1]))
+    packed = copies[0]
     for lines, factor in zip(sent, factors):
         field = pl.pallas_call(
             filter_kernel,

time: 131 us -> 131 us (level)
  transfers between devices with their start and end apart: 13 -> 13, of which waited for: 5 -> 6; matrix products, arithmetic and copies ran while one was open for 8% -> 8% of each run, Pallas kernels for 42% -> 41%
where the time goes in v6:
time: 131 us; the launch traced here: 130 us
  Pallas kernels  66.7 us (51%)
  starting transfers between devices  38.3 us (29%)
  waiting for transfers between devices  13.3 us (10%)
  other arithmetic  6.6 us (5%)
  local copies, waits for them, and re-layouts  4.4 us (3%)
    pallas_call x2, Pallas kernels, shards(): pl.pallas_call(lambda *refs, first=first, count=count: gather_kernel(firs...  24.7 us
    pallas_call x2, Pallas kernels, shards(): pl.pallas_call(lambda *refs, first=first, count=count: spread_kernel(firs...  16.7 us
    pallas_call x2, Pallas kernels, shards(): pl.pallas_call(filter_kernel, grid=(1,), in_specs=[IN_VMEM, IN_VMEM, whol...  9.05 us
    all_to_all x2, starting transfers between devices, shards(): lax.all_to_all(lines, 'sect', split_axis=0, concat_axis=0, tiled=True)  7.7 us
    pallas_call x2, Pallas kernels, folded(): pl.pallas_call(lambda *refs: influence_kernel(first, half, float(mesh_siz...  7.67 us
    all_to_all x2, starting transfers between devices, shards(): lax.all_to_all(field, 'sect', split_axis=0, concat_axis=0, tiled=True)  7.46 us
    pallas_call x2, Pallas kernels, basis(): pl.pallas_call(lambda *refs: basis_kernel(which, mesh_size, x_width, z_wi...  7.3 us
    all_to_all x1, starting transfers between devices, shards(): row = lax.all_to_all(copies, 'dom', 0, 0, tiled=True)  6.33 us
  transfers between devices with their start and end apart: 13, of which 6 were waited for; matrix products, arithmetic and copies ran while one was open for 8% of the time, Pallas kernels for 41%

profile of v6, /device:TPU:0, one launch (start us, length us, event | category | flops | bytes accessed | tf_op | source)
XLA Modules:
  0.0 129.6 jit_solution(12743934300714014973)
XLA Ops:
  0.0 1.3 %pack.1 = f32[8,2,8,128]{3,2,1,0:T(8,128)} custom-call(s32[3,1,1,256]{3,2,1,0:T(1,128)} %cells.1, f32[3,1,1,256]{3,2,1,0:T(1,128)} %fracs.1, f32[1,1,256]{2,1,0:T(1,128)} %charges.1), custom_call_target="tpu_custom_call" | custom-call | tf_op jit(solution)/shard_map/pack/pallas_call | solution.py:381
  1.3 6.3 %all-to-all-start = ((f32[8,2,8,128]{3,2,1,0:T(8,128)}), f32[8,2,8,128]{3,2,1,0:T(8,128)S(1)}, u32[]{:S(2)}, u32[]{:S(2)}) async-start(f32[8,2,8,128]{3,2,1,0:T(8,128)} %pack.1), calls=%async_computation | async-start | bytes 131072 | tf_op jit(solution)/shard_map/all_to_all | solution.py:386
  7.7 1.3 fusion.66
  9.0 2.5 %collective-permute-start.1 = (f32[8,64,256]{2,1,0:T(8,128)S(1)}, f32[8,64,256]{2,1,0:T(8,128)}, u32[]{:S(2)}, u32[]{:S(2)}) collective-permute-start(f32[8,64,256]{2,1,0:T(8,128)S(1)} %get-tuple-element.61), channel_id=1, source_target_pairs={{0,24},{8,16},{16,8},{24,0},{1,25},{9,17},{17,9},{25,1},{2,26},{10... | collective-permute-start | bytes 1572872 | tf_op jit(solution)/shard_map/ppermute | solution.py:406
  11.5 0.5 collective-permute-start
  12.0 0.6 pad_add_fusion.refs_0_
  12.5 1.0 all-to-all-done.refs_1_
  13.6 0.0 copy-start
  13.6 0.6 copy-done
  14.2 3.6 %basis.2 = (f32[72,2048]{1,0:T(8,128)}, f32[48,2048]{1,0:T(8,128)}, bf16[256,2048]{1,0:T(8,128)(2,1)}, bf16[256,2048]{1,0:T(8,128)(2,1)}) custom-call(s32[3]{0:T(128)} %pad_add_fusion.refs_0_, f32[8,2,8,128]{3,2,1,0:T(8,128)} %copy-done), custom_call_target="tpu_custom_call" | custom-call | flops 4000000000 | bytes 400000 | tf_op jit(solution)/shard_map/basis/pallas_call | solution.py:432
  17.9 8.8 %spread.2 = f32[4,624,128]{2,1,0:T(8,128)} custom-call(f32[72,2048]{1,0:T(8,128)} %get-tuple-element.30.refs_0_.refs_3_, f32[48,2048]{1,0:T(8,128)} %get-tuple-element.31.refs_1_.refs_5_, bf16[256,2048]{1,0:T(8,128)(2,1)} %get-tuple-element.32.refs_2_.refs_7_, bf16[256,2048]{1,0:T(8,128)(2,1)} %get-tuple-element.33.refs_3_.refs_8_, ...), custom_call_target="tpu_custom_call" | custom-call | flops 8999999488 | bytes 900000 | tf_op jit(solution)/shard_map/spread/pallas_call | solution.py:454
  26.6 0.0 copy-start.2
  26.6 0.0 collective-permute-done.1
  26.6 3.7 %all-to-all-start.1 = ((f32[4,624,128]{2,1,0:T(8,128)}), f32[4,624,128]{2,1,0:T(8,128)S(1)}, u32[]{:S(2)}, u32[]{:S(2)}) async-start(f32[4,624,128]{2,1,0:T(8,128)} %spread.2), calls=%async_computation.1 | async-start | bytes 2555904 | tf_op jit(solution)/shard_map/all_to_all | solution.py:480
  30.4 0.0 copy-done.2
  30.4 0.9 slice.191
  31.3 1.9 %collective-permute-start.6 = (f32[16,1,256]{2,1,0:T(1,128)S(1)}, f32[16,1,256]{2,1,0:T(1,128)S(1)}, u32[]{:S(2)}, u32[]{:S(2)}) collective-permute-start(f32[16,1,256]{2,1,0:T(1,128)S(1)} %slice.191), channel_id=1, source_target_pairs={{0,7},{1,6},{2,5},{3,4},{4,3},{5,2},{6,1},{7,0},{8,31},{9,30},{10,... | collective-permute-start | bytes 49160 | tf_op jit(solution)/shard_map/ppermute | solution.py:479
  33.2 1.7 %collective-permute-start.5 = (f32[8,64,256]{2,1,0:T(8,128)}, f32[8,64,256]{2,1,0:T(8,128)}, u32[]{:S(2)}, u32[]{:S(2)}) collective-permute-start(f32[8,64,256]{2,1,0:T(8,128)} %collective-permute-done.1), channel_id=1, source_target_pairs={{0,7},{1,6},{2,5},{3,4},{4,3},{5,2},{6,1},{7,0},{8,15},{9,14},{10,... | collective-permute-start | bytes 1572872 | tf_op jit(solution)/shard_map/ppermute | solution.py:478
  34.9 7.9 %spread.3 = f32[4,536,128]{2,1,0:T(8,128)} custom-call(f32[72,2048]{1,0:T(8,128)} %get-tuple-element.30.refs_0_.refs_3_, f32[48,2048]{1,0:T(8,128)} %get-tuple-element.31.refs_1_.refs_5_, bf16[256,2048]{1,0:T(8,128)(2,1)} %get-tuple-element.32.refs_2_.refs_7_, bf16[256,2048]{1,0:T(8,128)(2,1)} %get-tuple-element.33.refs_3_.refs_8_, ...), custom_call_target="tpu_custom_call" | custom-call | flops 8999999488 | bytes 900000 | tf_op jit(solution)/shard_map/spread/pallas_call | solution.py:454
  42.8 0.0 copy-start.1
  42.8 3.7 %basis.3 = (f32[72,2048]{1,0:T(8,128)}, f32[48,2048]{1,0:T(8,128)}, bf16[256,2048]{1,0:T(8,128)(2,1)}, bf16[256,2048]{1,0:T(8,128)(2,1)}) custom-call(s32[3]{0:T(128)} %pad_add_fusion.refs_0_, f32[8,2,8,128]{3,2,1,0:T(8,128)} %copy-done), custom_call_target="tpu_custom_call" | custom-call | flops 100000000 | bytes 10000 | tf_op jit(solution)/shard_map/basis/pallas_call | solution.py:432
  46.5 2.8 %all-to-all-done.1.lines = f32[4,624,128]{2,1,0:T(8,128)S(1)} async-done(((f32[4,624,128]{2,1,0:T(8,128)}), f32[4,624,128]{2,1,0:T(8,128)S(1)}, u32[]{:S(2)}, u32[]{:S(2)}) %all-to-all-start.1) | async-done | bytes 1277984 | tf_op jit(solution)/shard_map/all_to_all | solution.py:480
  49.3 4.0 %all-to-all-start.2 = ((f32[4,536,128]{2,1,0:T(8,128)}), f32[4,536,128]{2,1,0:T(8,128)S(1)}, u32[]{:S(2)}, u32[]{:S(2)}) async-start(f32[4,536,128]{2,1,0:T(8,128)} %spread.3), calls=%async_computation.2 | async-start | bytes 2195456 | tf_op jit(solution)/shard_map/all_to_all | solution.py:480
  53.3 0.0 collective-permute-done
  53.3 0.0 copy-done.1
  53.3 2.9 %collective-permute-start.3 = (f32[8,2,8,128]{3,2,1,0:T(8,128)S(1)}, f32[8,2,8,128]{3,2,1,0:T(8,128)S(1)}, u32[]{:S(2)}, u32[]{:S(2)}) collective-permute-start(f32[8,2,8,128]{3,2,1,0:T(8,128)S(1)} %copy-done.1), channel_id=1, source_target_pairs={{8,0},{16,8},{24,16},{0,24},{9,1},{17,9},{25,17},{1,25},{10,2},{18... | collective-permute-start | bytes 196616 | tf_op jit(solution)/shard_map/ppermute | solution.py:486
  56.2 0.0 collective-permute-start.2
  56.2 2.2 %collective-permute-start.4 = (f32[8,64,256]{2,1,0:T(8,128)S(1)}, f32[8,64,256]{2,1,0:T(8,128)}, u32[]{:S(2)}, u32[]{:S(2)}) collective-permute-start(f32[8,64,256]{2,1,0:T(8,128)S(1)} %collective-permute-done), channel_id=1, source_target_pairs={{0,7},{1,6},{2,5},{3,4},{4,3},{5,2},{6,1},{7,0},{8,15},{9,14},{10,... | collective-permute-start | bytes 1572872 | tf_op jit(solution)/shard_map/ppermute | solution.py:482
  58.5 0.0 collective-permute-done.6.refs_3_
  58.5 0.0 collective-permute-done.5.refs_2_
  58.5 3.9 %influence.3.factor = f32[9,256,128]{2,1,0:T(8,128)} custom-call(s32[3]{0:T(128)} %pad_add_fusion.refs_0_, f32[32,64,256]{2,1,0:T(8,128)} %refs_1_.3, f32[8,64,256]{2,1,0:T(8,128)} %collective-permute-done.5.refs_2_, f32[16,1,256]{2,1,0:T(1,128)S(1)} %collective-permute-done.6.refs_3_, bf16[128,64]{1,0:T(8,128)(2,1)} %constant.187.refs_4_, ...), custom_call_target="tpu_custom_call" | custom-call | flops 3500000000 | bytes 350000 | tf_op jit(solution)/shard_map/influence/pallas_call | solution.py:489
  62.4 4.8 %filter.3 = f32[4,624,128]{2,1,0:T(8,128)} custom-call(f32[4,624,128]{2,1,0:T(8,128)S(1)} %all-to-all-done.1.lines, f32[9,256,128]{2,1,0:T(8,128)} %influence.3.factor, bf16[512,256]{1,0:T(8,128)(2,1)} %constant.190.th, bf16[512,256]{1,0:T(8,128)(2,1)} %constant.193.tl), custom_call_target="tpu_custom_call" | custom-call | flops 5500000256 | bytes 550000 | tf_op jit(solution)/shard_map/filter/pallas_call | solution.py:506
  67.1 1.7 %all-to-all-done.2.lines = f32[4,536,128]{2,1,0:T(8,128)S(1)} async-done(((f32[4,536,128]{2,1,0:T(8,128)}), f32[4,536,128]{2,1,0:T(8,128)S(1)}, u32[]{:S(2)}, u32[]{:S(2)}) %all-to-all-start.2) | async-done | bytes 1097760 | tf_op jit(solution)/shard_map/all_to_all | solution.py:480
  68.8 3.7 %all-to-all-start.4 = ((f32[4,624,128]{2,1,0:T(8,128)}), f32[4,624,128]{2,1,0:T(8,128)S(1)}, u32[]{:S(2)}, u32[]{:S(2)}) async-start(f32[4,624,128]{2,1,0:T(8,128)} %filter.3), calls=%async_computation.4 | async-start | bytes 2555904 | tf_op jit(solution)/shard_map/all_to_all | solution.py:522
  72.6 0.0 collective-permute-done.3
  72.6 0.0 collective-permute-done.2
  72.6 1.0 slice_bitcast_fusion.27
  73.6 0.2 convolution_bitcast_fusion
  73.8 3.0 %multiply_reduce_fusion.2 = (f32[128]{0:T(128)S(1)}, f32[128]{0:T(128)S(1)}, f32[128]{0:T(128)S(1)}) fusion(f32[8,128]{1,0:T(8,128)S(1)} %get-tuple-element.82, f32[128]{0:T(128)S(1)} %get-tuple-element.68, f32[8,128]{1,0:T(8,128)S(1)} %get-tuple-element.83, f32[128]{0:T(128)S(1)} %get-tuple-element.69, f32[8,128]{1,0:T(8,128)S(1)} %get-tuple-element.78, ...), kind=kLoop, calls=%fused_computation.35 | loop fusion | flops 14941824 | bytes 33792 | tf_op jit(solution)/shard_map/reduce_sum | solution.py:358
  76.8 3.0 %multiply_reduce_fusion.5 = (f32[128]{0:T(128)S(1)}, f32[128]{0:T(128)S(1)}, f32[128]{0:T(128)S(1)}) fusion(f32[8,128]{1,0:T(8,128)S(1)} %get-tuple-element.89, f32[128]{0:T(128)S(1)} %get-tuple-element.75, f32[8,128]{1,0:T(8,128)S(1)} %get-tuple-element.90, f32[128]{0:T(128)S(1)} %get-tuple-element.76, f32[8,128]{1,0:T(8,128)S(1)} %get-tuple-element.85, ...), kind=kLoop, calls=%fused_computation.63 | loop fusion | flops 14941824 | bytes 33792 | tf_op jit(solution)/shard_map/reduce_sum | solution.py:358
  79.7 0.0 collective-permute-done.4.refs_2_
  79.8 3.8 %influence.2.factor = f32[8,256,128]{2,1,0:T(8,128)} custom-call(s32[3]{0:T(128)} %pad_add_fusion.refs_0_, f32[32,64,256]{2,1,0:T(8,128)} %refs_1_.3, f32[8,64,256]{2,1,0:T(8,128)} %collective-permute-done.4.refs_2_, f32[16,1,256]{2,1,0:T(1,128)S(1)} %collective-permute-done.6.refs_3_, bf16[128,64]{1,0:T(8,128)(2,1)} %constant.187.refs_4_, ...), custom_call_target="tpu_custom_call" | custom-call | flops 3500000000 | bytes 350000 | tf_op jit(solution)/shard_map/influence/pallas_call | solution.py:489
  83.5 4.3 %filter.2 = f32[4,536,128]{2,1,0:T(8,128)} custom-call(f32[4,536,128]{2,1,0:T(8,128)S(1)} %all-to-all-done.2.lines, f32[8,256,128]{2,1,0:T(8,128)} %influence.2.factor, bf16[512,256]{1,0:T(8,128)(2,1)} %constant.190.th, bf16[512,256]{1,0:T(8,128)(2,1)} %constant.193.tl), custom_call_target="tpu_custom_call" | custom-call | flops 5500000256 | bytes 550000 | tf_op jit(solution)/shard_map/filter/pallas_call | solution.py:506
  87.8 1.2 all-to-all-done.4.refs_0_
  89.0 3.7 %all-to-all-start.3 = ((f32[4,536,128]{2,1,0:T(8,128)}), f32[4,536,128]{2,1,0:T(8,128)S(1)}, u32[]{:S(2)}, u32[]{:S(2)}) async-start(f32[4,536,128]{2,1,0:T(8,128)} %filter.2), calls=%async_computation.3 | async-start | bytes 2195456 | tf_op jit(solution)/shard_map/all_to_all | solution.py:522
  92.7 12.9 %gather.2.refs_11_ = f32[8,4,256]{2,1,0:T(4,128)} custom-call(f32[4,624,128]{2,1,0:T(8,128)S(1)} %all-to-all-done.4.refs_0_, bf16[512,512]{1,0:T(8,128)(2,1)} %constant.194.refs_1_, bf16[512,512]{1,0:T(8,128)(2,1)} %constant.197.refs_2_, f32[72,2048]{1,0:T(8,128)} %get-tuple-element.30.refs_0_.refs_3_, f32[72,2048]{1,0:T(8,128)} %get-tuple-element.49.refs_4_, ...), custom_call_target="tpu_custom_call" | custom-call | flops 12999999488 | bytes 1300000 | tf_op jit(solution)/shard_map/gather/pallas_call | solution.py:543
  105.6 0.8 all-to-all-done.3.refs_0_
  106.4 11.8 %gather.3 = f32[8,4,256]{2,1,0:T(4,128)} custom-call(f32[4,536,128]{2,1,0:T(8,128)S(1)} %all-to-all-done.3.refs_0_, bf16[512,512]{1,0:T(8,128)(2,1)} %constant.194.refs_1_, bf16[512,512]{1,0:T(8,128)(2,1)} %constant.197.refs_2_, f32[72,2048]{1,0:T(8,128)} %get-tuple-element.30.refs_0_.refs_3_, f32[72,2048]{1,0:T(8,128)} %get-tuple-element.49.refs_4_, ...), custom_call_target="tpu_custom_call" | custom-call | flops 12999999488 | bytes 1300000 | tf_op jit(solution)/shard_map/gather/pallas_call | solution.py:543
  118.2 5.1 %all-to-all-start.5 = ((f32[8,4,256]{2,1,0:T(4,128)}), f32[8,4,256]{2,1,0:T(4,128)S(1)}, u32[]{:S(2)}, u32[]{:S(2)}) async-start(f32[8,4,256]{2,1,0:T(4,128)} %gather.3), calls=%async_computation.5 | async-start | bytes 65536 | tf_op jit(solution)/shard_map/all_to_all | solution.py:556
  123.3 5.7 %all-to-all-done.5 = f32[8,4,256]{2,1,0:T(4,128)S(1)} async-done(((f32[8,4,256]{2,1,0:T(4,128)}), f32[8,4,256]{2,1,0:T(4,128)S(1)}, u32[]{:S(2)}, u32[]{:S(2)}) %all-to-all-start.5) | async-done | bytes 32800 | tf_op jit(solution)/shard_map/all_to_all | solution.py:556
  129.0 0.6 reshape.202
  (6 shorter events, 0.1 us)
Async XLA Ops:
  1.3 12.2 %all-to-all-start = ((f32[8,2,8,128]{3,2,1,0:T(8,128)}), f32[8,2,8,128]{3,2,1,0:T(8,128)S(1)}, u32[]{:S(2)}, u32[]{:S(2)}) async-start(f32[8,2,8,128]{3,2,1,0:T(8,128)} %pack.1), calls=%async_computation | async-start | bytes 131072 | tf_op jit(solution)/shard_map/all_to_all | solution.py:386
  9.0 17.7 %collective-permute-start.1 = (f32[8,64,256]{2,1,0:T(8,128)S(1)}, f32[8,64,256]{2,1,0:T(8,128)}, u32[]{:S(2)}, u32[]{:S(2)}) collective-permute-start(f32[8,64,256]{2,1,0:T(8,128)S(1)} %get-tuple-element.61), channel_id=1, source_target_pairs={{0,24},{8,16},{16,8},{24,0},{1,25},{9,17},{17,9},{25,1},{2,26},{10... | collective-permute-start | bytes 1572872 | tf_op jit(solution)/shard_map/ppermute | solution.py:406
  11.5 41.8 %collective-permute-start = (f32[8,64,256]{2,1,0:T(8,128)S(1)}, f32[8,64,256]{2,1,0:T(8,128)S(1)}, u32[]{:S(2)}, u32[]{:S(2)}) collective-permute-start(f32[8,64,256]{2,1,0:T(8,128)S(1)} %get-tuple-element.62), channel_id=1, source_target_pairs={{0,24},{8,16},{16,8},{24,0},{1,25},{9,17},{17,9},{25,1},{2,26},{10... | collective-permute-start | bytes 1572872 | tf_op jit(solution)/shard_map/ppermute | solution.py:406
  13.6 0.6 copy-start
  26.6 3.7 %copy-start.2 = (s32[1,1,2,8]{3,2,1,0:T(2,128)S(1)}, s32[1,1,2,8]{3,2,1,0:T(2,128)}, u32[]{:S(2)}) copy-start(s32[1,1,2,8]{3,2,1,0:T(2,128)} %param.15) | copy-start | bytes 196
  26.6 22.7 %all-to-all-start.1 = ((f32[4,624,128]{2,1,0:T(8,128)}), f32[4,624,128]{2,1,0:T(8,128)S(1)}, u32[]{:S(2)}, u32[]{:S(2)}) async-start(f32[4,624,128]{2,1,0:T(8,128)} %spread.2), calls=%async_computation.1 | async-start | bytes 2555904 | tf_op jit(solution)/shard_map/all_to_all | solution.py:480
  31.3 27.1 %collective-permute-start.6 = (f32[16,1,256]{2,1,0:T(1,128)S(1)}, f32[16,1,256]{2,1,0:T(1,128)S(1)}, u32[]{:S(2)}, u32[]{:S(2)}) collective-permute-start(f32[16,1,256]{2,1,0:T(1,128)S(1)} %slice.191), channel_id=1, source_target_pairs={{0,7},{1,6},{2,5},{3,4},{4,3},{5,2},{6,1},{7,0},{8,31},{9,30},{10,... | collective-permute-start | bytes 49160 | tf_op jit(solution)/shard_map/ppermute | solution.py:479
  33.2 25.3 %collective-permute-start.5 = (f32[8,64,256]{2,1,0:T(8,128)}, f32[8,64,256]{2,1,0:T(8,128)}, u32[]{:S(2)}, u32[]{:S(2)}) collective-permute-start(f32[8,64,256]{2,1,0:T(8,128)} %collective-permute-done.1), channel_id=1, source_target_pairs={{0,7},{1,6},{2,5},{3,4},{4,3},{5,2},{6,1},{7,0},{8,15},{9,14},{10,... | collective-permute-start | bytes 1572872 | tf_op jit(solution)/shard_map/ppermute | solution.py:478
  42.8 10.4 %copy-start.1 = (f32[8,2,8,128]{3,2,1,0:T(8,128)S(1)}, f32[8,2,8,128]{3,2,1,0:T(8,128)}, u32[]{:S(2)}) copy-start(f32[8,2,8,128]{3,2,1,0:T(8,128)} %copy-done) | copy-start | bytes 196612
  49.3 19.5 %all-to-all-start.2 = ((f32[4,536,128]{2,1,0:T(8,128)}), f32[4,536,128]{2,1,0:T(8,128)S(1)}, u32[]{:S(2)}, u32[]{:S(2)}) async-start(f32[4,536,128]{2,1,0:T(8,128)} %spread.3), calls=%async_computation.2 | async-start | bytes 2195456 | tf_op jit(solution)/shard_map/all_to_all | solution.py:480
  53.3 19.3 %collective-permute-start.3 = (f32[8,2,8,128]{3,2,1,0:T(8,128)S(1)}, f32[8,2,8,128]{3,2,1,0:T(8,128)S(1)}, u32[]{:S(2)}, u32[]{:S(2)}) collective-permute-start(f32[8,2,8,128]{3,2,1,0:T(8,128)S(1)} %copy-done.1), channel_id=1, source_target_pairs={{8,0},{16,8},{24,16},{0,24},{9,1},{17,9},{25,17},{1,25},{10,2},{18... | collective-permute-start | bytes 196616 | tf_op jit(solution)/shard_map/ppermute | solution.py:486
  56.2 16.4 %collective-permute-start.2 = (f32[8,2,8,128]{3,2,1,0:T(8,128)S(1)}, f32[8,2,8,128]{3,2,1,0:T(8,128)S(1)}, u32[]{:S(2)}, u32[]{:S(2)}) collective-permute-start(f32[8,2,8,128]{3,2,1,0:T(8,128)S(1)} %copy-done.1), channel_id=1, source_target_pairs={{0,8},{8,16},{16,24},{24,0},{1,9},{9,17},{17,25},{25,1},{2,10},{10... | collective-permute-start | bytes 196616 | tf_op jit(solution)/shard_map/ppermute | solution.py:486
  56.2 23.5 %collective-permute-start.4 = (f32[8,64,256]{2,1,0:T(8,128)S(1)}, f32[8,64,256]{2,1,0:T(8,128)}, u32[]{:S(2)}, u32[]{:S(2)}) collective-permute-start(f32[8,64,256]{2,1,0:T(8,128)S(1)} %collective-permute-done), channel_id=1, source_target_pairs={{0,7},{1,6},{2,5},{3,4},{4,3},{5,2},{6,1},{7,0},{8,15},{9,14},{10,... | collective-permute-start | bytes 1572872 | tf_op jit(solution)/shard_map/ppermute | solution.py:482
  68.8 20.2 %all-to-all-start.4 = ((f32[4,624,128]{2,1,0:T(8,128)}), f32[4,624,128]{2,1,0:T(8,128)S(1)}, u32[]{:S(2)}, u32[]{:S(2)}) async-start(f32[4,624,128]{2,1,0:T(8,128)} %filter.3), calls=%async_computation.4 | async-start | bytes 2555904 | tf_op jit(solution)/shard_map/all_to_all | solution.py:522
  89.0 17.4 %all-to-all-start.3 = ((f32[4,536,128]{2,1,0:T(8,128)}), f32[4,536,128]{2,1,0:T(8,128)S(1)}, u32[]{:S(2)}, u32[]{:S(2)}) async-start(f32[4,536,128]{2,1,0:T(8,128)} %filter.2), calls=%async_computation.3 | async-start | bytes 2195456 | tf_op jit(solution)/shard_map/all_to_all | solution.py:522
  118.2 10.8 %all-to-all-start.5 = ((f32[8,4,256]{2,1,0:T(4,128)}), f32[8,4,256]{2,1,0:T(4,128)S(1)}, u32[]{:S(2)}, u32[]{:S(2)}) async-start(f32[8,4,256]{2,1,0:T(4,128)} %gather.3), calls=%async_computation.5 | async-start | bytes 65536 | tf_op jit(solution)/shard_map/all_to_all | solution.py:556
